TPU v7x, 128 devices: a whole 4x4x4 slice. The times are simulated.
128 devices in a mesh: seq: 16 (over x_hi, y, core), fsdp: 2 (over x_lo), dp: 4 (over z).
Axes of the slice: x: 4 (x_hi: 2, x_lo: 2; x = x_hi * 2 + x_lo), y: 4, z: 4, core: 2. Of those that a mesh axis runs over, the one named last changes fastest.
Arguments:
- queries: bfloat16 [8, 4096, 4096], P(('fsdp', 'dp'), 'seq'), may hold values from -160 to 160
- hidden: bfloat16 [8, 4096, 8192], P(('fsdp', 'dp'), 'seq'), may hold values from -8 to 8
- key_weight: bfloat16 [8192, 512], P('fsdp'), may hold values from -1 to 1
- doc_lengths: int32 [8, 32], P(('fsdp', 'dp')), may hold values from 1 to 256, 4096 in all within a row
- entropy_cot: bfloat16 [8, 4096, 32], P(('fsdp', 'dp'), 'seq'), may hold values from -600 to 600
Outputs:
- entropy: float32 [8, 4096, 32], P(('fsdp', 'dp'), 'seq')
- grad_queries: bfloat16 [8, 4096, 4096], P(('fsdp', 'dp'), 'seq')
- grad_key_weight: bfloat16 [8192, 512], P('fsdp')
Inputs may be any that keep to these rules, and one draw needn't show every extreme that they name: `doc_lengths`: each sequence's 32 documents are packed in order, their lengths sum to 4096, and the longest is exactly 256.
All inputs are finite; a program needn't handle non-finite values.
Results may differ from a plain program's by a relative error of at most 0.0088.
Values may be sent and summed in bfloat16 or wider, within the bound.
No kernel may reach another device: no remote copies, remote signals or barrier semaphores. Data moves between devices by JAX's collectives and lax.ppermute only.
A program may use at most 128 MiB of HBM per device.

v0:
```python
import jax
import jax.numpy as jnp
from jax import lax
from jax.sharding import PartitionSpec as P

QH = 32
KVH = 4
HD = 128


def document_index(lengths, seq_len):
    ends = jnp.cumsum(lengths)
    position = jnp.arange(seq_len, dtype=jnp.int32)
    return jnp.sum((ends[None, :] <= position[:, None]).astype(jnp.int32), axis=1)


def attend(queries, key_rows, cotangent, doc_index, doc_len):
    row_count, key_heads, group_size, head_size = queries.shape
    full_len = key_rows.shape[0]
    block_rows = min(512, row_count)
    window = block_rows + doc_len
    factor = head_size ** (-0.5)
    keys_padded = jnp.concatenate(
        [jnp.zeros((doc_len, key_heads, head_size), key_rows.dtype), key_rows], axis=0
    )
    index_padded = jnp.concatenate([jnp.full((doc_len,), -1, jnp.int32), doc_index], axis=0)

    def one_block(step_index, state_now):
        entropy, grad_query, grad_key = state_now
        row_start = (step_index * block_rows).astype(jnp.int32)
        query_block = lax.dynamic_slice_in_dim(queries, row_start, block_rows, 0)
        weight_block = lax.dynamic_slice_in_dim(cotangent, row_start, block_rows, 0).astype(
            jnp.float32
        )
        key_block = lax.dynamic_slice_in_dim(keys_padded, row_start, window, 0)
        key_docs = lax.dynamic_slice_in_dim(index_padded, row_start, window, 0)
        query_docs = lax.dynamic_slice_in_dim(doc_index, row_start, block_rows, 0)
        query_pos = row_start + jnp.arange(block_rows, dtype=jnp.int32)
        key_pos = row_start - doc_len + jnp.arange(window, dtype=jnp.int32)
        visible = (query_docs[:, None] == key_docs[None, :]) & (
            key_pos[None, :] <= query_pos[:, None]
        )
        scores = (
            jnp.einsum("rkgd,wkd->kgrw", query_block, key_block, preferred_element_type=jnp.float32)
            * factor
        )
        scores = jnp.where(visible, scores, -1e30)
        row_max = jnp.max(scores, axis=-1, keepdims=True)
        powers = jnp.exp(scores - row_max)
        denominator = jnp.sum(powers, axis=-1, keepdims=True)
        probability = powers / denominator
        mean_score = jnp.sum(jnp.where(visible, probability * scores, 0.0), axis=-1, keepdims=True)
        block_entropy = (row_max + jnp.log(denominator) - mean_score)[..., 0]
        row_weight = jnp.transpose(weight_block, (1, 2, 0))[..., None]
        slope = jnp.where(visible, row_weight * probability * (mean_score - scores), 0.0).astype(
            jnp.bfloat16
        )
        query_part = (
            jnp.einsum("kgrw,wkd->rkgd", slope, key_block, preferred_element_type=jnp.float32)
            * factor
        )
        key_part = (
            jnp.einsum("kgrw,rkgd->wkd", slope, query_block, preferred_element_type=jnp.float32)
            * factor
        )
        entropy = lax.dynamic_update_slice_in_dim(
            entropy, jnp.transpose(block_entropy, (2, 0, 1)), row_start, 0
        )
        grad_query = lax.dynamic_update_slice_in_dim(grad_query, query_part, row_start, 0)
        previous = lax.dynamic_slice_in_dim(grad_key, row_start, window, 0)
        grad_key = lax.dynamic_update_slice_in_dim(grad_key, previous + key_part, row_start, 0)
        return (entropy, grad_query, grad_key)

    initial = (
        jnp.zeros((row_count, key_heads, group_size), jnp.float32),
        jnp.zeros((row_count, key_heads, group_size, head_size), jnp.float32),
        jnp.zeros((full_len + doc_len, key_heads, head_size), jnp.float32),
    )
    entropy, grad_query, grad_key = lax.fori_loop(0, row_count // block_rows, one_block, initial)
    return (entropy, grad_query, grad_key[doc_len:])


def shards(queries, hidden, key_weight, doc_lengths, entropy_cot):
    tokens = hidden[0]
    local_rows = tokens.shape[0]
    seq_parts = lax.axis_size("seq")
    seq_len = local_rows * seq_parts
    group_size = QH // KVH
    doc_index = document_index(doc_lengths[0], seq_len)
    columns = tokens
    key_local = jnp.dot(
        columns,
        lax.all_gather(key_weight, "fsdp", axis=0, tiled=True),
        preferred_element_type=jnp.float32,
    ).astype(jnp.bfloat16)
    query_local = queries[0]
    cot_local = entropy_cot[0]
    share = QH // seq_parts
    outgoing = jnp.broadcast_to(
        key_local.reshape(local_rows, KVH, 1, HD), (local_rows, KVH, group_size, HD)
    )
    outgoing = outgoing.reshape(local_rows, KVH * group_size * HD)
    query_heads, key_heads_seq, cot_heads = (
        lax.all_to_all(query_local, "seq", split_axis=1, concat_axis=0, tiled=True),
        lax.all_to_all(outgoing, "seq", split_axis=1, concat_axis=0, tiled=True),
        lax.all_to_all(cot_local, "seq", split_axis=1, concat_axis=0, tiled=True),
    )
    key_count = key_heads_seq.shape[1] // HD
    entropy, grad_query, grad_key = attend(
        query_heads.reshape(seq_len, key_count, share // key_count, HD),
        key_heads_seq.reshape(seq_len, key_count, HD),
        cot_heads.reshape(seq_len, key_count, share // key_count),
        doc_index,
        local_rows,
    )
    grad_local, key_grad_local, entropy_local = (
        lax.all_to_all(
            grad_query.reshape(seq_len, share * HD), "seq", split_axis=0, concat_axis=1, tiled=True
        ),
        lax.all_to_all(
            grad_key.reshape(seq_len, key_count * HD),
            "seq",
            split_axis=0,
            concat_axis=1,
            tiled=True,
        ),
        lax.all_to_all(
            entropy.reshape(seq_len, share), "seq", split_axis=0, concat_axis=1, tiled=True
        ),
    )
    key_grad = jnp.sum(key_grad_local.reshape(local_rows, KVH, -1, HD), axis=2).reshape(
        local_rows, KVH * HD
    )
    key_grad_low = key_grad.astype(jnp.bfloat16)
    columns = tokens
    term_rows = lax.psum_scatter(
        lax.dot_general(
            columns, key_grad_low, (((0,), (0,)), ((), ())), preferred_element_type=jnp.float32
        ),
        "fsdp",
        scatter_dimension=0,
        tiled=True,
    )
    summed = lax.psum(term_rows, ("seq", "dp"))
    norm_factor = (seq_len * lax.axis_size("fsdp") * lax.axis_size("dp")) ** (-0.5)
    weight_grad = (summed * norm_factor).astype(jnp.bfloat16)
    return (
        entropy_local.reshape(1, local_rows, QH),
        grad_local.astype(jnp.bfloat16).reshape(1, local_rows, QH * HD),
        weight_grad,
    )


def solution(mesh):
    return jax.shard_map(
        shards,
        mesh=mesh,
        in_specs=(
            P(("fsdp", "dp"), "seq", None),
            P(("fsdp", "dp"), "seq", None),
            P("fsdp", None),
            P(("fsdp", "dp"), None),
            P(("fsdp", "dp"), "seq", None),
        ),
        out_specs=(P(("fsdp", "dp"), "seq", None), P(("fsdp", "dp"), "seq", None), P("fsdp", None)),
        check_vma=False,
    )
```

profile of v0, /device:TPU:1, one launch (start us, length us, event | category | flops | bytes accessed | tf_op | source)
XLA Modules:
  0.0 1254.1 jit_solution(18081824443787886025)
XLA Ops:
  8.8 2.4 copy.83
  11.2 8.4 all-to-all-start.1
  19.6 114.3 %all-gather.2.cloned.1.call-done = bf16[8192,512]{1,0:T(8,128)(2,1)} async-done(((bf16[4096,512]{1,0:T(8,128)(2,1)}), bf16[8192,512]{1,0:T(8,128)(2,1)}) %all-gather.2.cloned.1.call-update) | async-done | bytes 8388624 | tf_op jit(solution)/shard_map/all_gather | solution.py:93
  133.9 7.0 fusion.41
  141.1 1.6 broadcast_in_dim.83
  142.7 8.6 all-to-all-start
  152.1 27.7 %all-to-all-done = bf16[256,16,256]{0,2,1:T(8,128)(2,1)} async-done(((bf16[256,16,256]{0,2,1:T(8,128)(2,1)}), bf16[256,16,256]{0,2,1:T(8,128)(2,1)}, u32[]{:S(2)}, u32[]{:S(2)}) %all-to-all-start) | async-done | bytes 2097184 | tf_op jit(solution)/shard_map/all_to_all | solution.py:105
  179.8 7.1 all-to-all-start.2
  187.3 2.5 copy.84
  189.8 4.2 reshape.222
  194.0 4.1 copy.82
  198.1 2.9 reshape.221
  201.0 1.5 concatenate.7
  203.4 2.3 broadcast_in_dim.81
  205.7 88.0 %while.19 = (s32[]{:T(128)}, f32[4096,2,1]{0,1,2:T(2,128)}, bf16[4096,2,1,128]{0,3,1,2:T(8,128)(2,1)S(1)}, f32[4352,2,128]{0,2,1:T(8,128)}, s32[4096]{0:T(1024)S...) while((s32[]{:T(128)}, f32[4096,2,1]{0,1,2:T(2,128)}, ...), condition=%wide.region_6.7_spmd, body=%wide.region_2.6_spmd.sunk | while | flops 630850816 | bytes 21601552 | solution.py:79
  206.3 1.9 fusion.58
  208.9 1.0 select_reduce_fusion.2
  210.6 2.5 fusion.60
  213.1 3.7 fusion.61
  217.3 1.9 fusion.58
  219.9 1.0 select_reduce_fusion.2
  221.6 2.5 fusion.60
  224.1 3.6 fusion.61
  228.3 1.9 fusion.58
  230.9 1.0 select_reduce_fusion.2
  232.6 2.5 fusion.60
  235.0 3.7 fusion.61
  239.3 1.9 fusion.58
  241.9 1.0 select_reduce_fusion.2
  243.6 2.5 fusion.60
  246.0 3.7 fusion.61
  250.3 1.9 fusion.58
  252.9 1.0 select_reduce_fusion.2
  254.6 2.5 fusion.60
  257.0 3.7 fusion.61
  261.3 1.9 fusion.58
  263.9 1.0 select_reduce_fusion.2
  265.6 2.5 fusion.60
  268.1 3.7 fusion.61
  272.3 1.9 fusion.58
  274.9 1.0 select_reduce_fusion.2
  276.6 2.5 fusion.60
  279.0 3.7 fusion.61
  283.3 1.9 fusion.58
  287.6 2.5 fusion.60
  290.1 3.7 fusion.61
  293.7 2.5 slice.3
  296.2 1.7 copy.102
  298.0 2.4 copy.90
  300.4 57.7 %all_to_all.93 = f32[16,256,256]{1,2,0:T(8,128)} all-to-all(f32[16,256,256]{1,2,0:T(8,128)S(1)} %copy.90), channel_id=1, replica_groups=mesh['seq'=16,'fsdp'=2,'dp'=4] {'seq'}, dimensions={0} | all-to-all | bytes 8388608 | tf_op jit(solution)/shard_map/all_to_all | solution.py:120
  358.1 2.5 reduce_sum.41
  360.7 10.3 convolution_bitcast_fusion
  371.0 190.3 %reduce-scatter.2.cloned.1.call-done = f32[4096,512]{0,1:T(8,128)} async-done(((f32[8192,512]{0,1:T(8,128)}), f32[4096,512]{0,1:T(8,128)}) %reduce-scatter.2.cloned.1.call-update) | async-done | bytes 8388624 | tf_op jit(solution)/shard_map/reduce_scatter | solution.py:136
  561.3 7.1 all-to-all-start.3
  568.4 2.0 copy.101
  570.4 4.3 copy.98
  574.6 1.1 all-to-all-done.3
  575.7 6.2 all-to-all-start.4
  582.5 28.8 %all-to-all-done.4 = bf16[16,256,256]{2,1,0:T(8,128)(2,1)S(1)} async-done(((bf16[16,256,256]{2,1,0:T(8,128)(2,1)}), bf16[16,256,256]{2,1,0:T(8,128)(2,1)S(1)}, u32[]{:S(2)}, u32[]{:S(2)}) %all-to-all-start.4) | async-done | bytes 2097184 | tf_op jit(solution)/shard_map/all_to_all | solution.py:117
  611.3 2.4 copy.89
  613.7 4.1 copy.91
  617.7 617.0 %all-reduce.4.cloned.1.call-done = f32[4096,512]{0,1:T(8,128)} async-done(((f32[4096,512]{0,1:T(8,128)}), f32[4096,512]{0,1:T(8,128)}) %all-reduce.4.cloned.1.call-update) | async-done | bytes 8388624 | tf_op jit(solution)/shard_map/psum | solution.py:144
  1234.8 6.4 multiply_convert_fusion
  1241.2 6.4 copy.92
  (89 shorter events, 20.7 us)
Async XLA Ops:
  7.2 1.6 copy-start
  7.2 126.8 %all-gather.2.cloned.1.call-start = ((), (), s32[]{:S(2)}) async-start(), calls=%async_computation.7 | async-start | bytes 12582912 | tf_op jit(solution)/shard_map/all_gather | solution.py:93
  11.2 129.9 %all-to-all-start.1 = ((bf16[256,16,256]{0,2,1:T(8,128)(2,1)}), bf16[256,16,256]{0,2,1:T(8,128)(2,1)S(1)}, u32[]{:S(2)}, u32[]{:S(2)}) async-start(bf16[256,16,256]{0,2,1:T(8,128)(2,1)} %bitcast.144), calls=%async_computation.1 | async-start | bytes 4194304 | tf_op jit(solution)/shard_map/all_to_all | solution.py:104
  141.1 10.2 copy-start.2
  141.1 10.4 copy-start.1
  142.7 37.1 %all-to-all-start = ((bf16[256,16,256]{0,2,1:T(8,128)(2,1)}), bf16[256,16,256]{0,2,1:T(8,128)(2,1)}, u32[]{:S(2)}, u32[]{:S(2)}) async-start(bf16[256,16,256]{0,2,1:T(8,128)(2,1)} %bitcast.145), calls=%async_computation | async-start | bytes 4194304 | tf_op jit(solution)/shard_map/all_to_all | solution.py:105
  179.8 22.7 %all-to-all-start.2 = ((bf16[256,16,2]{0,2,1:T(2,128)(2,1)}), bf16[256,16,2]{0,2,1:T(2,128)(2,1)S(1)}, u32[]{:S(2)}, u32[]{:S(2)}) async-start(bf16[256,16,2]{0,2,1:T(2,128)(2,1)} %all_to_all.76), calls=%async_computation.2 | async-start | bytes 32768 | tf_op jit(solution)/shard_map/all_to_all | solution.py:106
  187.0 374.3 %reduce-scatter.2.cloned.1.call-start = ((), (), s32[]{:S(2)}) async-start(), calls=%async_computation.8 | async-start | bytes 25165824 | tf_op jit(solution)/shard_map/reduce_scatter | solution.py:136
  370.9 863.9 %all-reduce.4.cloned.1.call-start = ((), (), s32[]{:S(2)}) async-start(), calls=%async_computation.9 | async-start | bytes 16777216 | tf_op jit(solution)/shard_map/psum | solution.py:144
  561.3 14.4 %all-to-all-start.3 = ((f32[16,256,2]{1,2,0:T(2,128)}), f32[16,256,2]{1,2,0:T(2,128)S(1)}, u32[]{:S(2)}, u32[]{:S(2)}) async-start(f32[16,256,2]{1,2,0:T(2,128)} %bitcast.20), calls=%async_computation.3 | async-start | bytes 65536 | tf_op jit(solution)/shard_map/all_to_all | solution.py:127
  575.7 35.6 %all-to-all-start.4 = ((bf16[16,256,256]{2,1,0:T(8,128)(2,1)}), bf16[16,256,256]{2,1,0:T(8,128)(2,1)S(1)}, u32[]{:S(2)}, u32[]{:S(2)}) async-start(bf16[16,256,256]{2,1,0:T(8,128)(2,1)} %copy.98), calls=%async_computation.4 | async-start | bytes 4194304 | tf_op jit(solution)/shard_map/all_to_all | solution.py:117
Sparse Core Ops, SparseCore 0:
  9.7 124.2 all-gather.1
  371.1 190.1 reduce-scatter.1
  563.9 670.8 all-reduce.3
where the time goes:
time: 1260 us; the launch traced here: 1250 us
  waiting for transfers between devices  980 us (78%)
  matrix products  81.7 us (6%)
  blocking collectives  57.7 us (5%)
  local copies, waits for them, and re-layouts  51.6 us (4%)
  starting transfers between devices  37.7 us (3%)
  other arithmetic  31.4 us (2%)
  between operations  13.9 us (1%)
    psum x1, waiting for transfers between devices, shards(): summed = lax.psum(term_rows, ('seq', 'dp'))  617 us
    reduce_scatter x1, waiting for transfers between devices, shards(): lax.psum_scatter(lax.dot_general(columns, key_grad_low, (((0,), (0,)), ((...  190 us
    all_gather x1, waiting for transfers between devices, shards(): lax.all_gather(key_weight, 'fsdp', axis=0, tiled=True)  114 us
    all_to_all x1, blocking collectives, shards(): lax.all_to_all(grad_key.reshape(seq_len, key_count * HD), 'seq', split_ax...  57.7 us
    dot_general x8, matrix products, one_block(): jnp.einsum('kgrw,rkgd->wkd', slope, query_block, preferred_element_type=j...  29.3 us
    all_to_all x1, waiting for transfers between devices, shards(): lax.all_to_all(grad_query.reshape(seq_len, share * HD), 'seq', split_axis...  28.8 us
    all_to_all x1, waiting for transfers between devices, shards(): lax.all_to_all(outgoing, 'seq', split_axis=1, concat_axis=0, tiled=True)  27.7 us
  transfers between devices with their start and end apart: 8, of which 6 were waited for; matrix products, arithmetic and copies ran while one was open for 3% of the time, Pallas kernels for 0%

commit v1 on v0

v1 whole, which is shorter than its diff:
```python
import functools
import math

import jax
import jax.numpy as jnp
from jax import lax
from jax.experimental import pallas as pl
from jax.experimental.pallas import tpu as pltpu
from jax.sharding import PartitionSpec as P

QH = 32
KVH = 4
HD = 128
GROUP = QH // KVH
BF = jnp.bfloat16
F32 = jnp.float32
AXES = ("seq", "fsdp", "dp")
FACTOR = HD ** (-0.5)
EXP_SCALE = FACTOR * math.log2(math.e)
NEG = -1e30


def coords(index):
    seq, rest = divmod(index, 8)
    fsdp, z = divmod(rest, 4)
    return seq // 8, (seq // 2) % 4, seq % 2, fsdp, z


def linear(xh, y, core, xl, z):
    return ((xh * 8 + y * 2 + core) * 2 + xl) * 4 + z


def move(value, where):
    pairs = []
    for index in range(128):
        target = where(*coords(index))
        if target is not None:
            pairs.append((index, linear(*target)))
    return lax.ppermute(value, AXES, pairs)


def along_x(xh, y, core, xl, z, step, other=0):
    x = (xh * 2 + xl + step) % 4
    return x // 2, y, core ^ other, x % 2, z


def params(**kw):
    return pltpu.CompilerParams(vmem_limit_bytes=56 << 20, **kw)


def cost(flops, moved):
    return pl.CostEstimate(flops=int(flops), bytes_accessed=int(moved), transcendentals=0)


def own_half_kernel(place, hidden, weight, out):
    @pl.when(pl.program_id(0) == 0)
    def _():
        out[...] = jnp.zeros_like(out)

    out[...] += jnp.dot(hidden[...], weight[...], preferred_element_type=F32)


def project_own(place, tokens, weight):
    rows, model = tokens.shape
    half, width = weight.shape
    step = half // 4
    return pl.pallas_call(
        own_half_kernel,
        grid_spec=pltpu.PrefetchScalarGridSpec(
            num_scalar_prefetch=1,
            grid=(4,),
            in_specs=[
                pl.BlockSpec((rows, step), lambda i, p: (0, p[0] * 4 + i)),
                pl.BlockSpec((step, width), lambda i, p: (i, 0)),
            ],
            out_specs=pl.BlockSpec((rows, width), lambda i, p: (0, 0)),
        ),
        out_shape=jax.ShapeDtypeStruct((rows, width), F32),
        compiler_params=params(),
        cost_estimate=cost(2 * rows * half * width, 6 << 20),
        name="project_own",
    )(place, tokens, weight)


def pair_kernel(place, hidden_a, hidden_b, weight_a, weight_b, total, out):
    acc = total[...] + jnp.dot(hidden_a[...], weight_a[...], preferred_element_type=F32)
    acc = acc + jnp.dot(hidden_b[...], weight_b[...], preferred_element_type=F32)
    out[...] = acc.astype(out.dtype)


def project_pair(place, tokens, weight_a, weight_b, total, chunk, dtype):
    rows, model = tokens.shape
    step, width = weight_a.shape

    def block_a(i, p):
        return (0, (1 - p[0]) * 4 + p[1] * 2 + chunk)

    def block_b(i, p):
        return (0, (1 - p[0]) * 4 + (1 - p[1]) * 2 + chunk)

    whole = lambda i, p: (0, 0)
    return pl.pallas_call(
        pair_kernel,
        grid_spec=pltpu.PrefetchScalarGridSpec(
            num_scalar_prefetch=1,
            grid=(1,),
            in_specs=[
                pl.BlockSpec((rows, step), block_a),
                pl.BlockSpec((rows, step), block_b),
                pl.BlockSpec((step, width), whole),
                pl.BlockSpec((step, width), whole),
                pl.BlockSpec((rows, width), whole),
            ],
            out_specs=pl.BlockSpec((rows, width), whole),
        ),
        out_shape=jax.ShapeDtypeStruct((rows, width), dtype),
        compiler_params=params(),
        cost_estimate=cost(4 * rows * step * width, 4 << 20),
        name="project_pair",
    )(place, tokens, tokens, weight_a, weight_b, total)


def attend_kernel(place, lengths, query, key_own, key_halo, weight, entropy, grad_query, grad_own,
                  grad_halo, bias, keys, keys_t):
    @pl.when(pl.program_id(0) == 0)
    def _():
        base = place[2] * 256
        position = base + lax.broadcasted_iota(jnp.int32, (8, 256), 1)

        def add(i, state):
            end, first = state
            end = end + lengths[0, i]
            return end, jnp.where(position >= end, end, first)

        _, first = lax.fori_loop(
            0, lengths.shape[1], add, (jnp.int32(0), jnp.zeros((8, 256), jnp.int32))
        )
        for half in range(2):
            begin = first[0:1, half * 128:(half + 1) * 128]
            here = position[0:1, half * 128:(half + 1) * 128]
            there = base - 256 + half * 128 + lax.broadcasted_iota(jnp.int32, (384, 128), 0)
            seen = (there >= begin) & (there <= here)
            value = jnp.where(seen, 0.0, NEG)
            bias[half, :, 0:128] = value
            bias[half, :, 128:256] = value

    keys[0:256, :] = key_halo[...]
    keys[256:512, :] = key_own[...]
    keys_t[...] = keys[...].T
    weights = weight[...].astype(F32)
    sums = [None, None]
    for pair in range(GROUP // 2):
        cols = [slice((2 * pair + k) * HD, (2 * pair + k + 1) * HD) for k in range(2)]
        for half in range(2):
            rows = slice(half * 128, (half + 1) * 128)
            window = slice(half * 128, half * 128 + 384)
            stack = jnp.concatenate([query[rows, cols[0]], query[rows, cols[1]]], axis=0)
            raw = lax.dot_general(
                keys[window, :], stack, (((1,), (1,)), ((), ())), preferred_element_type=F32
            ) + bias[half]
            top = jnp.max(raw, axis=0, keepdims=True)
            gap = raw - top
            power = jnp.exp2(gap * EXP_SCALE)
            den = jnp.sum(power, axis=0, keepdims=True)
            mean = jnp.sum(power * gap, axis=0, keepdims=True) / den
            row_weight = jnp.concatenate(
                [weights[2 * pair:2 * pair + 1, rows], weights[2 * pair + 1:2 * pair + 2, rows]], axis=1
            )
            slope_b = row_weight * FACTOR / den
            slope_a = slope_b * mean
            slope = (power * (slope_a - slope_b * gap)).astype(BF)
            level = jnp.log(den) - FACTOR * mean
            entropy[2 * pair:2 * pair + 1, rows] = level[:, 0:128]
            entropy[2 * pair + 1:2 * pair + 2, rows] = level[:, 128:256]
            turned = jnp.dot(keys_t[:, window], slope, preferred_element_type=F32) * FACTOR
            straight = turned.T.astype(BF)
            grad_query[rows, cols[0]] = straight[0:128]
            grad_query[rows, cols[1]] = straight[128:256]
            part = jnp.dot(slope, stack, preferred_element_type=F32)
            sums[half] = part if sums[half] is None else sums[half] + part
    low, high = sums
    grad_halo[0:128, :] = (low[0:128] * FACTOR).astype(grad_halo.dtype)
    grad_halo[128:256, :] = ((low[128:256] + high[0:128]) * FACTOR).astype(grad_halo.dtype)
    grad_own[0:128, :] = (low[256:384] + high[128:256]) * FACTOR
    grad_own[128:256, :] = high[256:384] * FACTOR


def attend(place, lengths, queries, key_own, key_halo, weight):
    rows, width = queries.shape
    wide = GROUP * HD
    by_head = lambda j, p, l: (0, j)
    return pl.pallas_call(
        attend_kernel,
        grid_spec=pltpu.PrefetchScalarGridSpec(
            num_scalar_prefetch=2,
            grid=(KVH,),
            in_specs=[
                pl.BlockSpec((rows, wide), by_head),
                pl.BlockSpec((rows, HD), by_head),
                pl.BlockSpec((rows, HD), by_head),
                pl.BlockSpec((GROUP, rows), lambda j, p, l: (j, 0)),
            ],
            out_specs=[
                pl.BlockSpec((GROUP, rows), lambda j, p, l: (j, 0)),
                pl.BlockSpec((rows, wide), by_head),
                pl.BlockSpec((rows, HD), by_head),
                pl.BlockSpec((rows, HD), by_head),
            ],
            scratch_shapes=[
                pltpu.VMEM((2, 384, 256), F32),
                pltpu.VMEM((512, HD), BF),
                pltpu.VMEM((HD, 512), BF),
            ],
        ),
        out_shape=[
            jax.ShapeDtypeStruct((QH, rows), F32),
            jax.ShapeDtypeStruct((rows, width), BF),
            jax.ShapeDtypeStruct((rows, KVH * HD), F32),
            jax.ShapeDtypeStruct((rows, KVH * HD), BF),
        ],
        compiler_params=params(),
        cost_estimate=cost(4 << 30, 6 << 20),
        name="attend",
    )(place, lengths, queries, key_own, key_halo, weight)


def weight_grad_kernel(place, *refs):
    hidden, grads, outs = refs[0:6], refs[6:12], refs[12:]
    total = None
    for piece, grad in zip(hidden, grads):
        part = lax.dot_general(
            piece[...], grad[...], (((0,), (0,)), ((), ())), preferred_element_type=F32
        )
        total = part if total is None else total + part
    low = total.astype(BF)
    for k in range(8):

        @pl.when(pl.program_id(0) == k)
        def _():
            outs[k][...] = low


def weight_grad(place, tokens, pieces, grads):
    def chunk(i, p):
        own = jnp.where(i < 4, p[3], p[4])
        return jnp.where(i < 4, 0, 4) + (own + i) % 4

    def own_block(i, p):
        return (0, (p[0] * 2 + p[1]) * 8 + chunk(i, p))

    whole = lambda i, p: (0, 0)
    return pl.pallas_call(
        weight_grad_kernel,
        grid_spec=pltpu.PrefetchScalarGridSpec(
            num_scalar_prefetch=1,
            grid=(8,),
            in_specs=[pl.BlockSpec((256, 256), own_block)]
            + [pl.BlockSpec((v.shape[0], 256), lambda i, p: (0, chunk(i, p))) for v in pieces]
            + [pl.BlockSpec(v.shape, whole) for v in grads],
            out_specs=[pl.BlockSpec((256, 512), whole)] * 8,
        ),
        out_shape=[jax.ShapeDtypeStruct((256, 512), BF)] * 8,
        compiler_params=params(),
        cost_estimate=cost(2 * 1024 * 2048 * 512, 8 << 20),
        name="weight_grad",
    )(place, tokens, *pieces, *grads)


def sum_split_kernel(place, *refs):
    first, second, outs = refs[0:4], refs[4:8], refs[8:16]
    work = refs[16]
    for half, group in enumerate((first, second)):
        total = group[0][...].astype(F32)
        for ref in group[1:]:
            total = total + ref[...].astype(F32)
        work[half] = total
    for half in range(2):
        own = place[4] if half == 0 else place[3]
        for d in range(4):
            start = pl.multiple_of(((own + d) % 4) * 64, 64)
            outs[4 * half + d][...] = work[half, pl.ds(start, 64), :].astype(BF)


def sum_split(place, first, second):
    return pl.pallas_call(
        sum_split_kernel,
        in_specs=[pl.BlockSpec(memory_space=pltpu.SMEM)] + [pl.BlockSpec(memory_space=pltpu.VMEM)] * 8,
        out_specs=[pl.BlockSpec(memory_space=pltpu.VMEM)] * 8,
        out_shape=[jax.ShapeDtypeStruct((64, 512), BF)] * 8,
        scratch_shapes=[pltpu.VMEM((2, 256, 512), F32)],
        compiler_params=params(),
        cost_estimate=cost(2 << 20, 3 << 20),
        name="sum_split",
    )(place, *first, *second)


def sum_join_kernel(*refs):
    first, second, out = refs[0:4], refs[4:8], refs[8]
    for half, group in enumerate((first, second)):
        total = group[0][...].astype(F32)
        for ref in group[1:]:
            total = total + ref[...].astype(F32)
        out[half * 64:(half + 1) * 64, :] = total.astype(BF)


def sum_join(first, second):
    return pl.pallas_call(
        sum_join_kernel,
        in_specs=[pl.BlockSpec(memory_space=pltpu.VMEM)] * 8,
        out_specs=pl.BlockSpec(memory_space=pltpu.VMEM),
        out_shape=jax.ShapeDtypeStruct((128, 512), BF),
        compiler_params=params(),
        cost_estimate=cost(1 << 20, 1 << 20),
        name="sum_join",
    )(*first, *second)


def finish_kernel(scale, mine, other, first, second):
    total = (mine[...].astype(F32) + other[...].astype(F32)) * scale
    low = total.astype(BF)
    first[...] = low[0:64]
    second[...] = low[64:128]


def finish(mine, other, scale):
    return pl.pallas_call(
        functools.partial(finish_kernel, scale),
        in_specs=[pl.BlockSpec(memory_space=pltpu.VMEM)] * 2,
        out_specs=[pl.BlockSpec(memory_space=pltpu.VMEM)] * 2,
        out_shape=[jax.ShapeDtypeStruct((64, 512), BF)] * 2,
        compiler_params=params(),
        cost_estimate=cost(1 << 20, 1 << 20),
        name="finish",
    )(mine, other)


def gather_small_kernel(place, *refs):
    first, second, outs = refs[0:4], refs[4:8], refs[8:10]
    for half, group in enumerate((first, second)):
        own = place[4] if half == 0 else place[3]
        for d in range(4):
            start = pl.multiple_of(((own + 4 - d) % 4) * 64, 64)
            outs[half][pl.ds(start, 64), :] = group[d][...]


def gather_small(place, first, second):
    return pl.pallas_call(
        gather_small_kernel,
        in_specs=[pl.BlockSpec(memory_space=pltpu.SMEM)] + [pl.BlockSpec(memory_space=pltpu.VMEM)] * 8,
        out_specs=[pl.BlockSpec(memory_space=pltpu.VMEM)] * 2,
        out_shape=[jax.ShapeDtypeStruct((256, 512), BF)] * 2,
        compiler_params=params(),
        cost_estimate=cost(1 << 20, 1 << 20),
        name="gather_small",
    )(place, *first, *second)


def gather_large_kernel(place, *refs):
    out = refs[16]
    for side in range(2):
        core = place[1] if side == 0 else 1 - place[1]
        for half in range(2):
            own = place[3] if half == 0 else place[4]
            for d in range(4):
                start = core * 2048 + half * 1024 + ((own + 4 - d) % 4) * 256
                start = pl.multiple_of(start, 256)
                out[pl.ds(start, 256), :] = refs[8 * side + 4 * half + d][...]


def gather_large(place, mine, others):
    return pl.pallas_call(
        gather_large_kernel,
        in_specs=[pl.BlockSpec(memory_space=pltpu.SMEM)] + [pl.BlockSpec(memory_space=pltpu.VMEM)] * 16,
        out_specs=pl.BlockSpec(memory_space=pltpu.VMEM),
        out_shape=jax.ShapeDtypeStruct((4096, 512), BF),
        compiler_params=params(),
        cost_estimate=cost(1 << 20, 8 << 20),
        name="gather_large",
    )(place, *mine, *others)


def shift_y(d):
    return lambda xh, y, core, xl, z: (xh, (y + d) % 4, core, xl, z)


def shift_z(d):
    return lambda xh, y, core, xl, z: (xh, y, core, xl, (z + d) % 4)


def swap_core(xh, y, core, xl, z):
    return xh, y, 1 - core, xl, z


def next_rows(step):
    def where(xh, y, core, xl, z):
        seq = xh * 8 + y * 2 + core + step
        if seq < 0 or seq > 15:
            return None
        return seq // 8, (seq // 2) % 4, seq % 2, xl, z

    return where


def shards(queries, hidden, key_weight, doc_lengths, entropy_cot):
    tokens = hidden[0]
    rows, model = tokens.shape
    half, width = key_weight.shape
    seq, fsdp, z = lax.axis_index("seq"), lax.axis_index("fsdp"), lax.axis_index("dp")
    core, y = seq % 2, (seq // 2) % 4
    place = jnp.stack([fsdp, core, seq, y, z]).astype(jnp.int32)

    mine = lax.dynamic_slice_in_dim(key_weight, core * (half // 2), half // 2, 0)
    fetch = lambda xh, y, core, xl, z: along_x(xh, y, core, xl, z, 1 - 2 * core)
    got = [move(mine[k * half // 4:(k + 1) * half // 4], fetch) for k in range(2)]
    swapped = [move(v, swap_core) for v in got]
    total = project_own(place, tokens, key_weight)
    total = project_pair(place, tokens, got[0], swapped[0], total, 0, F32)
    key_own = project_pair(place, tokens, got[1], swapped[1], total, 1, BF)
    key_halo = move(key_own, next_rows(1))

    quarter = model // 4
    tied, _ = lax.optimization_barrier((tokens, got[1]))

    def column(first, last, is_fsdp, is_core):
        start = (is_fsdp * 2 + is_core) * quarter
        return lax.dynamic_slice(tied, (first, start), (last - first, quarter))

    split = rows // 2
    routes = [swap_core]
    for step in (1, -1):
        for other in (0, 1):
            routes.append(functools.partial(along_x, step=step, other=other))
    pieces = [move(column(0, rows, fsdp, 1 - core), routes[0])]
    for k, route in enumerate(routes[1:]):
        first = 0 if k < 2 else split
        pieces.append(
            move(column(first, first + split, 1 - fsdp, core if k % 2 == 0 else 1 - core), route)
        )

    entropy, grad_query, grad_own, grad_halo = attend(
        place, doc_lengths, queries[0], key_own, key_halo, entropy_cot[0].T
    )

    from_next = move(grad_halo, next_rows(-1))
    key_grad = (grad_own + from_next.astype(F32)).astype(BF)
    grads = [key_grad, move(key_grad, routes[0])]
    for k, route in enumerate(routes[1:]):
        first = 0 if k < 2 else split
        grads.append(move(key_grad[first:first + split], route))

    parts = weight_grad(place, tokens, pieces, grads)
    first = [parts[0]] + [move(parts[d], shift_y(d)) for d in (1, 2, 3)]
    second = [parts[4]] + [move(parts[4 + d], shift_z(d)) for d in (1, 2, 3)]
    parts = sum_split(place, first, second)
    first = [parts[0]] + [move(parts[d], shift_z(d)) for d in (1, 2, 3)]
    second = [parts[4]] + [move(parts[4 + d], shift_y(d)) for d in (1, 2, 3)]
    joined = sum_join(first, second)
    across = move(joined, lambda xh, y, core, xl, z: (1 - xh, y, core, xl, z))
    scale = (rows * 16 * 8) ** (-0.5)
    low, high = finish(joined, across, scale)
    first = [low] + [move(low, shift_z(d)) for d in (1, 2, 3)]
    second = [high] + [move(high, shift_y(d)) for d in (1, 2, 3)]
    low, high = gather_small(place, first, second)
    final = [low] + [move(low, shift_y(d)) for d in (1, 2, 3)]
    final += [high] + [move(high, shift_z(d)) for d in (1, 2, 3)]
    others = [move(v, swap_core) for v in final]
    grad_weight = gather_large(place, final, others)
    return entropy.T[None], grad_query[None], grad_weight


def solution(mesh):
    return jax.shard_map(
        shards,
        mesh=mesh,
        in_specs=(
            P(("fsdp", "dp"), "seq", None),
            P(("fsdp", "dp"), "seq", None),
            P("fsdp", None),
            P(("fsdp", "dp"), None),
            P(("fsdp", "dp"), "seq", None),
        ),
        out_specs=(P(("fsdp", "dp"), "seq", None), P(("fsdp", "dp"), "seq", None), P("fsdp", None)),
        check_vma=False,
    )
```

time: 1260 us -> 227 us (0.18)
  waiting for transfers between devices: 980 us -> 75.3 us
  matrix products: 81.7 us -> 0 us
  blocking collectives: 57.7 us -> 0 us
  Pallas kernels: 0 us -> 53.7 us
  starting transfers between devices: 37.7 us -> 85.2 us
  local copies, waits for them, and re-layouts: 51.6 us -> 10.5 us
  other arithmetic: 31.4 us -> 0.07 us
  between operations: 13.9 us -> 1.16 us
    psum x1 -> x0, waiting for transfers between devices: 617 us -> none  [shards(): summed = lax.psum(term_rows, ('seq', 'dp'))]
    reduce_scatter x1 -> x0, waiting for transfers between devices: 190 us -> none  [shards(): lax.psum_scatter(lax.dot_general(columns, key_grad_low, (((0,), (0,)), ((...]
    all_gather x1 -> x0, waiting for transfers between devices: 114 us -> none  [shards(): lax.all_gather(key_weight, 'fsdp', axis=0, tiled=True)]
    ppermute x0 -> x49, starting transfers between devices: none -> 85.2 us  [move(): return lax.ppermute(value, AXES, pairs)]
    dot_general x26 -> x0, matrix products: 81.7 us -> none  [the longest x8 29.3 us: one_block(): jnp.einsum('kgrw,rkgd->wkd', slope, query_block, preferred_element_type=j...]
    ppermute x0 -> x49, waiting for transfers between devices: none -> 75.3 us  [move(): return lax.ppermute(value, AXES, pairs)]
    all_to_all x1 -> x0, blocking collectives: 57.7 us -> none  [shards(): lax.all_to_all(grad_key.reshape(seq_len, key_count * HD), 'seq', split_ax...]
    all_to_all x5 -> x0, waiting for transfers between devices: 57.6 us -> none  [the longest x1 28.8 us: shards(): lax.all_to_all(grad_query.reshape(seq_len, share * HD), 'seq', split_axis...]
  transfers between devices with their start and end apart: 8 -> 49, of which waited for: 6 -> 23; matrix products, arithmetic and copies ran while one was open for 3% -> 1% of each run, Pallas kernels for 0% -> 12%
where the time goes in v1:
time: 227 us; the launch traced here: 226 us
  starting transfers between devices  85.2 us (38%)
  waiting for transfers between devices  75.3 us (33%)
  Pallas kernels  53.7 us (24%)
  local copies, waits for them, and re-layouts  10.5 us (5%)
    ppermute x49, starting transfers between devices, move(): return lax.ppermute(value, AXES, pairs)  85.2 us
    ppermute x49, waiting for transfers between devices, move(): return lax.ppermute(value, AXES, pairs)  75.3 us
    pallas_call x1, Pallas kernels, attend(): pl.pallas_call(attend_kernel, grid_spec=pltpu.PrefetchScalarGridSpec(num_...  16.9 us
    pallas_call x1, Pallas kernels, weight_grad(): pl.pallas_call(weight_grad_kernel, grid_spec=pltpu.PrefetchScalarGridSpec...  10.4 us
    pallas_call x2, Pallas kernels, project_pair(): pl.pallas_call(pair_kernel, grid_spec=pltpu.PrefetchScalarGridSpec(num_sc...  8.22 us
    unnamed x100, local copies, waits for them, and re-layouts  6.71 us
    pallas_call x1, Pallas kernels, project_own(): pl.pallas_call(own_half_kernel, grid_spec=pltpu.PrefetchScalarGridSpec(nu...  5.76 us
  transfers between devices with their start and end apart: 49, of which 23 were waited for; matrix products, arithmetic and copies ran while one was open for 1% of the time, Pallas kernels for 12%

profile of v1, /device:TPU:1, one launch (start us, length us, event | category | flops | bytes accessed | tf_op | source)
XLA Modules:
  0.0 226.0 jit_solution(4560506144363558574)
XLA Ops:
  0.6 1.7 constant_dynamic-slice_fusion.4
  2.3 3.4 %collective-permute-start.2 = (bf16[1024,512]{1,0:T(8,128)(2,1)S(1)}, bf16[1024,512]{1,0:T(8,128)(2,1)S(1)}, u32[]{:S(2)}, u32[]{:S(2)}) collective-permute-start(bf16[1024,512]{1,0:T(8,128)(2,1)S(1)} %get-tuple-element.57), channel_id=1, source_target_pairs={{0,4},{1,5},{2,6},{3,7},{4,64},{5,65},{6,66},{7,67},{8,76},{9,77},... | collective-permute-start | bytes 3145736 | tf_op jit(solution)/shard_map/ppermute | solution.py:39
  6.3 11.2 %collective-permute-done.2.weight_a = bf16[1024,512]{1,0:T(8,128)(2,1)S(1)} collective-permute-done((bf16[1024,512]{1,0:T(8,128)(2,1)S(1)}, bf16[1024,512]{1,0:T(8,128)(2,1)S(1)}, u32[]{:S(2)}, u32[]{:S(2)}) %collective-permute-start.2) | collective-permute-done | bytes 1048608 | tf_op jit(solution)/shard_map/ppermute | solution.py:39
  17.5 2.4 %collective-permute-start.3 = (bf16[1024,512]{1,0:T(8,128)(2,1)S(1)}, bf16[1024,512]{1,0:T(8,128)(2,1)S(1)}, u32[]{:S(2)}, u32[]{:S(2)}) collective-permute-start(bf16[1024,512]{1,0:T(8,128)(2,1)S(1)} %collective-permute-done.2.weight_a), channel_id=1, source_target_pairs={{0,8},{1,9},{2,10},{3,11},{4,12},{5,13},{6,14},{7,15},{8,0},{9,1},... | collective-permute-start | bytes 3145736 | tf_op jit(solution)/shard_map/ppermute | solution.py:39
  19.8 8.9 %collective-permute-done.weight_a = bf16[1024,512]{1,0:T(8,128)(2,1)S(1)} collective-permute-done((bf16[1024,512]{1,0:T(8,128)(2,1)S(1)}, bf16[1024,512]{1,0:T(8,128)(2,1)S(1)}, u32[]{:S(2)}, u32[]{:S(2)}) %collective-permute-start) | collective-permute-done | bytes 1048608 | tf_op jit(solution)/shard_map/ppermute | solution.py:39
  28.7 2.4 %collective-permute-start.1 = (bf16[1024,512]{1,0:T(8,128)(2,1)S(1)}, bf16[1024,512]{1,0:T(8,128)(2,1)}, u32[]{:S(2)}, u32[]{:S(2)}) collective-permute-start(bf16[1024,512]{1,0:T(8,128)(2,1)S(1)} %collective-permute-done.weight_a), channel_id=1, source_target_pairs={{0,8},{1,9},{2,10},{3,11},{4,12},{5,13},{6,14},{7,15},{8,0},{9,1},... | collective-permute-start | bytes 3145736 | tf_op jit(solution)/shard_map/ppermute | solution.py:39
  31.7 5.8 %project_own.1.total = f32[256,512]{1,0:T(8,128)} custom-call(s32[5]{0:T(128)} %stack.23.place, bf16[256,8192]{1,0:T(8,128)(2,1)} %bitcast.14, bf16[4096,512]{1,0:T(8,128)(2,1)} %weight.1), custom_call_target="tpu_custom_call" | custom-call | flops 1073741824 | bytes 6291456 | tf_op jit(solution)/shard_map/project_own/pallas_call | solution.py:67
  37.5 1.0 copy-done.4
  38.5 4.2 %project_pair.2.total = f32[256,512]{1,0:T(8,128)} custom-call(s32[5]{0:T(128)} %stack.23.place, bf16[256,8192]{1,0:T(8,128)(2,1)} %bitcast.15, bf16[256,8192]{1,0:T(8,128)(2,1)} %bitcast.16, bf16[1024,512]{1,0:T(8,128)(2,1)} %copy-done.3, bf16[1024,512]{1,0:T(8,128)(2,1)} %copy-done.4, f32[256,512]{1,0:T(8,128)} %project_own.1.total), custom_call_target="tpu_custom_call" | custom-call | flops 536870912 | bytes 4194304 | tf_op jit(solution)/shard_map/project_pair/pallas_call | solution.py:102
  42.7 4.1 %project_pair.3.key_own = bf16[256,512]{1,0:T(8,128)(2,1)} custom-call(s32[5]{0:T(128)} %stack.23.place, bf16[256,8192]{1,0:T(8,128)(2,1)} %bitcast.17, bf16[256,8192]{1,0:T(8,128)(2,1)} %bitcast.18, bf16[1024,512]{1,0:T(8,128)(2,1)} %copy-done.5, bf16[1024,512]{1,0:T(8,128)(2,1)} %collective-permute-done.1.weight_b, f32[256,512]{1,0:T(8,128)} %project_pair.2.total), custom_call_target="tpu_custom_call" | custom-call | flops 536870912 | bytes 4194304 | tf_op jit(solution)/shard_map/project_pair/pallas_call | solution.py:102
  46.7 3.3 %collective-permute-start.4 = (bf16[256,512]{1,0:T(8,128)(2,1)}, bf16[256,512]{1,0:T(8,128)(2,1)S(1)}, u32[]{:S(2)}, u32[]{:S(2)}) collective-permute-start(bf16[256,512]{1,0:T(8,128)(2,1)} %project_pair.3.key_own), channel_id=1, source_target_pairs={{0,8},{1,9},{2,10},{3,11},{4,12},{5,13},{6,14},{7,15},{8,16},{9,17... | collective-permute-start | bytes 786440 | tf_op jit(solution)/shard_map/ppermute | solution.py:39
  50.0 1.3 constant_dynamic-slice_fusion.3
  51.4 2.2 collective-permute-done.4.key_halo
  53.6 0.7 copy-done.49
  54.3 16.9 %attend.1 = (f32[32,256]{1,0:T(8,128)}, bf16[256,4096]{1,0:T(8,128)(2,1)}, f32[256,512]{1,0:T(8,128)}, bf16[256,512]{1,0:T(8,128)(2,1)}) custom-call(s32[5]{0:T(128)} %stack.23.place, s32[1,32]{1,0:T(1,128)} %lengths.1, bf16[256,4096]{1,0:T(8,128)(2,1)} %bitcast.22, bf16[256,512]{1,0:T(8,128)(2,1)} %project_pair.3.key_own, bf16[256,512]{1,0:T(8,128)(2,1)} %copy-done.49, ...), custom_call_target="tpu_custom_call" | custom-call | flops 4294967296 | bytes 6291456 | tf_op jit(solution)/shard_map/attend/pallas_call | solution.py:192
  71.2 2.1 collective-permute-start.10
  73.4 6.0 %collective-permute-start.9 = (bf16[128,2048]{1,0:T(8,128)(2,1)S(1)}, bf16[128,2048]{1,0:T(8,128)(2,1)S(1)}, u32[]{:S(2)}, u32[]{:S(2)}) collective-permute-start(bf16[128,2048]{1,0:T(8,128)(2,1)S(1)} %get-tuple-element.53), channel_id=1, source_target_pairs={{0,76},{1,77},{2,78},{3,79},{4,8},{5,9},{6,10},{7,11},{8,68},{9,69... | collective-permute-start | bytes 1572872 | tf_op jit(solution)/shard_map/ppermute | solution.py:39
  80.0 1.6 collective-permute-start.7
  81.7 8.9 %collective-permute-done.9.refs_5_ = bf16[128,2048]{1,0:T(8,128)(2,1)S(1)} collective-permute-done((bf16[128,2048]{1,0:T(8,128)(2,1)S(1)}, bf16[128,2048]{1,0:T(8,128)(2,1)S(1)}, u32[]{:S(2)}, u32[]{:S(2)}) %collective-permute-start.9) | collective-permute-done | bytes 524320 | tf_op jit(solution)/shard_map/ppermute | solution.py:39
  90.6 1.6 collective-permute-start.11
  92.2 9.6 %collective-permute-done.8.refs_4_ = bf16[128,2048]{1,0:T(8,128)(2,1)S(1)} collective-permute-done((bf16[128,2048]{1,0:T(8,128)(2,1)S(1)}, bf16[128,2048]{1,0:T(8,128)(2,1)S(1)}, u32[]{:S(2)}, u32[]{:S(2)}) %collective-permute-start.8) | collective-permute-done | bytes 524320 | tf_op jit(solution)/shard_map/ppermute | solution.py:39
  101.8 4.3 %collective-permute-start.15 = (bf16[128,512]{1,0:T(8,128)(2,1)S(1)}, bf16[128,512]{1,0:T(8,128)(2,1)S(1)}, u32[]{:S(2)}, u32[]{:S(2)}) collective-permute-start(bf16[128,512]{1,0:T(8,128)(2,1)S(1)} %get-tuple-element.59), channel_id=1, source_target_pairs={{0,76},{1,77},{2,78},{3,79},{4,8},{5,9},{6,10},{7,11},{8,68},{9,69... | collective-permute-start | bytes 393224 | tf_op jit(solution)/shard_map/ppermute | solution.py:39
  106.1 1.8 collective-permute-start.14
  108.2 2.2 collective-permute-done.15.refs_11_
  110.3 1.6 collective-permute-done.14.refs_10_
  112.0 3.0 %collective-permute-done.13.refs_9_ = bf16[128,512]{1,0:T(8,128)(2,1)S(1)} collective-permute-done((bf16[128,512]{1,0:T(8,128)(2,1)S(1)}, bf16[128,512]{1,0:T(8,128)(2,1)S(1)}, u32[]{:S(2)}, u32[]{:S(2)}) %collective-permute-start.13) | collective-permute-done | bytes 131104 | tf_op jit(solution)/shard_map/ppermute | solution.py:39
  115.0 1.0 collective-permute-done.12.refs_8_
  116.7 0.7 copy-done.18
  117.4 10.4 %weight_grad.1 = (bf16[256,512]{1,0:T(8,128)(2,1)}, bf16[256,512]{1,0:T(8,128)(2,1)}, bf16[256,512]{1,0:T(8,128)(2,1)}, bf16[256,512]{1,0:T(8,128)(2,1)}, bf16[2...) custom-call(s32[5]{0:T(128)} %stack.23.place, ...), custom_call_target="tpu_custom_call" | custom-call | flops 2147483648 | bytes 8388608 | tf_op jit(solution)/shard_map/weight_grad/pallas_call | solution.py:252
  128.5 2.0 collective-permute-start.18
  130.5 1.6 collective-permute-start.19
  132.1 3.3 %collective-permute-start.20 = (bf16[256,512]{1,0:T(8,128)(2,1)}, bf16[256,512]{1,0:T(8,128)(2,1)S(1)}, u32[]{:S(2)}, u32[]{:S(2)}) collective-permute-start(bf16[256,512]{1,0:T(8,128)(2,1)} %get-tuple-element.39), channel_id=1, source_target_pairs={{0,2},{1,3},{2,0},{3,1},{4,6},{5,7},{6,4},{7,5},{8,10},{9,11},{10,... | collective-permute-start | bytes 786440 | tf_op jit(solution)/shard_map/ppermute | solution.py:39
  135.5 1.3 collective-permute-done.16.refs_1_
  136.8 3.8 %collective-permute-start.21 = (bf16[256,512]{1,0:T(8,128)(2,1)}, bf16[256,512]{1,0:T(8,128)(2,1)S(1)}, u32[]{:S(2)}, u32[]{:S(2)}) collective-permute-start(bf16[256,512]{1,0:T(8,128)(2,1)} %get-tuple-element.40), channel_id=1, source_target_pairs={{0,3},{1,0},{2,1},{3,2},{4,7},{5,4},{6,5},{7,6},{8,11},{9,8},{10,9... | collective-permute-start | bytes 786440 | tf_op jit(solution)/shard_map/ppermute | solution.py:39
  140.6 1.6 collective-permute-done.18.refs_3_
  142.1 3.5 %collective-permute-done.20.refs_6_ = bf16[256,512]{1,0:T(8,128)(2,1)S(1)} collective-permute-done((bf16[256,512]{1,0:T(8,128)(2,1)}, bf16[256,512]{1,0:T(8,128)(2,1)S(1)}, u32[]{:S(2)}, u32[]{:S(2)}) %collective-permute-start.20) | collective-permute-done | bytes 262176 | tf_op jit(solution)/shard_map/ppermute | solution.py:39
  146.4 2.7 %sum_split.1 = (bf16[64,512]{1,0:T(8,128)(2,1)}, bf16[64,512]{1,0:T(8,128)(2,1)}, bf16[64,512]{1,0:T(8,128)(2,1)}, bf16[64,512]{1,0:T(8,128)(2,1)}, bf16[64,512]...) custom-call(s32[5]{0:T(128)} %stack.23.place, ...), custom_call_target="tpu_custom_call" | custom-call | flops 2097152 | bytes 3145728 | tf_op jit(solution)/shard_map/sum_split/pallas_call | solution.py:285
  149.8 2.9 %collective-permute-start.23 = (bf16[64,512]{1,0:T(8,128)(2,1)}, bf16[64,512]{1,0:T(8,128)(2,1)S(1)}, u32[]{:S(2)}, u32[]{:S(2)}) collective-permute-start(bf16[64,512]{1,0:T(8,128)(2,1)} %get-tuple-element.43), channel_id=1, source_target_pairs={{0,2},{1,3},{2,0},{3,1},{4,6},{5,7},{6,4},{7,5},{8,10},{9,11},{10,... | collective-permute-start | bytes 196616 | tf_op jit(solution)/shard_map/ppermute | solution.py:39
  152.8 2.2 collective-permute-start.25
  155.0 1.7 collective-permute-start.26
  156.7 2.1 collective-permute-start.27
  158.8 1.0 collective-permute-done.26.refs_6_
  161.1 1.8 sum_join.1.mine
  162.8 4.0 %collective-permute-start.28 = (bf16[128,512]{1,0:T(8,128)(2,1)}, bf16[128,512]{1,0:T(8,128)(2,1)S(1)}, u32[]{:S(2)}, u32[]{:S(2)}) collective-permute-start(bf16[128,512]{1,0:T(8,128)(2,1)} %sum_join.1.mine), channel_id=1, source_target_pairs={{0,64},{1,65},{2,66},{3,67},{4,68},{5,69},{6,70},{7,71},{8,72},{9,... | collective-permute-start | bytes 393224 | tf_op jit(solution)/shard_map/ppermute | solution.py:39
  166.8 2.6 %collective-permute-done.28.other = bf16[128,512]{1,0:T(8,128)(2,1)S(1)} collective-permute-done((bf16[128,512]{1,0:T(8,128)(2,1)}, bf16[128,512]{1,0:T(8,128)(2,1)S(1)}, u32[]{:S(2)}, u32[]{:S(2)}) %collective-permute-start.28) | collective-permute-done | bytes 131104 | tf_op jit(solution)/shard_map/ppermute | solution.py:39
  170.0 1.6 finish.1
  172.2 2.7 %collective-permute-start.30 = (bf16[64,512]{1,0:T(8,128)(2,1)}, bf16[64,512]{1,0:T(8,128)(2,1)S(1)}, u32[]{:S(2)}, u32[]{:S(2)}) collective-permute-start(bf16[64,512]{1,0:T(8,128)(2,1)} %get-tuple-element.49.refs_0_), channel_id=1, source_target_pairs={{0,2},{1,3},{2,0},{3,1},{4,6},{5,7},{6,4},{7,5},{8,10},{9,11},{10,... | collective-permute-start | bytes 196616 | tf_op jit(solution)/shard_map/ppermute | solution.py:39
  174.9 2.2 collective-permute-start.34
  177.8 1.6 collective-permute-done.29.refs_1_
  179.5 2.5 %collective-permute-done.33.refs_6_ = bf16[64,512]{1,0:T(8,128)(2,1)S(1)} collective-permute-done((bf16[64,512]{1,0:T(8,128)(2,1)}, bf16[64,512]{1,0:T(8,128)(2,1)S(1)}, u32[]{:S(2)}, u32[]{:S(2)}) %collective-permute-start.33) | collective-permute-done | bytes 65568 | tf_op jit(solution)/shard_map/ppermute | solution.py:39
  183.3 1.9 gather_small.1
  185.2 9.6 %collective-permute-start.41 = (bf16[256,512]{1,0:T(8,128)(2,1)}, bf16[256,512]{1,0:T(8,128)(2,1)S(1)}, u32[]{:S(2)}, u32[]{:S(2)}) collective-permute-start(bf16[256,512]{1,0:T(8,128)(2,1)} %get-tuple-element.51.refs_0_), channel_id=1, source_target_pairs={{0,8},{1,9},{2,10},{3,11},{4,12},{5,13},{6,14},{7,15},{8,0},{9,1},... | collective-permute-start | bytes 786440 | tf_op jit(solution)/shard_map/ppermute | solution.py:39
  195.1 0.8 collective-permute-start.36
  195.8 0.9 collective-permute-start.35
  196.7 0.9 collective-permute-start.45
  197.6 3.0 %collective-permute-start.40 = (bf16[256,512]{1,0:T(8,128)(2,1)}, bf16[256,512]{1,0:T(8,128)(2,1)S(1)}, u32[]{:S(2)}, u32[]{:S(2)}) collective-permute-start(bf16[256,512]{1,0:T(8,128)(2,1)} %get-tuple-element.52.refs_4_), channel_id=1, source_target_pairs={{0,3},{1,0},{2,1},{3,2},{4,7},{5,4},{6,5},{7,6},{8,11},{9,8},{10,9... | collective-permute-start | bytes 786440 | tf_op jit(solution)/shard_map/ppermute | solution.py:39
  200.5 2.4 %collective-permute-done.37.refs_3_ = bf16[256,512]{1,0:T(8,128)(2,1)S(1)} collective-permute-done((bf16[256,512]{1,0:T(8,128)(2,1)}, bf16[256,512]{1,0:T(8,128)(2,1)S(1)}, u32[]{:S(2)}, u32[]{:S(2)}) %collective-permute-start.37) | collective-permute-done | bytes 262176 | tf_op jit(solution)/shard_map/ppermute | solution.py:39
  202.9 1.8 collective-permute-start.39
  204.7 1.7 collective-permute-start.38
  206.5 4.2 %collective-permute-done.35.refs_1_ = bf16[256,512]{1,0:T(8,128)(2,1)S(1)} collective-permute-done((bf16[256,512]{1,0:T(8,128)(2,1)}, bf16[256,512]{1,0:T(8,128)(2,1)S(1)}, u32[]{:S(2)}, u32[]{:S(2)}) %collective-permute-start.35) | collective-permute-done | bytes 262176 | tf_op jit(solution)/shard_map/ppermute | solution.py:39
  211.7 3.5 %collective-permute-start.48 = (bf16[256,512]{1,0:T(8,128)(2,1)S(1)}, bf16[256,512]{1,0:T(8,128)(2,1)S(1)}, u32[]{:S(2)}, u32[]{:S(2)}) collective-permute-start(bf16[256,512]{1,0:T(8,128)(2,1)S(1)} %collective-permute-done.40.refs_7_), channel_id=1, source_target_pairs={{0,8},{1,9},{2,10},{3,11},{4,12},{5,13},{6,14},{7,15},{8,0},{9,1},... | collective-permute-start | bytes 786440 | tf_op jit(solution)/shard_map/ppermute | solution.py:39
  215.1 3.4 %collective-permute-done.38.refs_5_ = bf16[256,512]{1,0:T(8,128)(2,1)S(1)} collective-permute-done((bf16[256,512]{1,0:T(8,128)(2,1)}, bf16[256,512]{1,0:T(8,128)(2,1)S(1)}, u32[]{:S(2)}, u32[]{:S(2)}) %collective-permute-start.38) | collective-permute-done | bytes 262176 | tf_op jit(solution)/shard_map/ppermute | solution.py:39
  219.1 1.0 collective-permute-done.47.refs_14_
  221.6 4.4 %gather_large.1 = bf16[4096,512]{1,0:T(8,128)(2,1)} custom-call(s32[5]{0:T(128)} %stack.23.place, bf16[256,512]{1,0:T(8,128)(2,1)} %get-tuple-element.51.refs_0_, bf16[256,512]{1,0:T(8,128)(2,1)} %copy-done.14, bf16[256,512]{1,0:T(8,128)(2,1)} %copy-done.13, bf16[256,512]{1,0:T(8,128)(2,1)} %copy-done.12, bf16[256,512]{1,0:T(8,128)(2,1)} %get-tuple-element.52.refs_4_, ...), custom_call_target="tpu_custom_call" | custom-call | flops 1048576 | bytes 8388608 | tf_op jit(solution)/shard_map/gather_large/pallas_call | solution.py:371
  (150 shorter events, 12.9 us)
Async XLA Ops:
  2.3 15.1 %collective-permute-start.2 = (bf16[1024,512]{1,0:T(8,128)(2,1)S(1)}, bf16[1024,512]{1,0:T(8,128)(2,1)S(1)}, u32[]{:S(2)}, u32[]{:S(2)}) collective-permute-start(bf16[1024,512]{1,0:T(8,128)(2,1)S(1)} %get-tuple-element.57), channel_id=1, source_target_pairs={{0,4},{1,5},{2,6},{3,7},{4,64},{5,65},{6,66},{7,67},{8,76},{9,77},... | collective-permute-start | bytes 3145736 | tf_op jit(solution)/shard_map/ppermute | solution.py:39
  5.7 23.0 %collective-permute-start = (bf16[1024,512]{1,0:T(8,128)(2,1)S(1)}, bf16[1024,512]{1,0:T(8,128)(2,1)S(1)}, u32[]{:S(2)}, u32[]{:S(2)}) collective-permute-start(bf16[1024,512]{1,0:T(8,128)(2,1)S(1)} %get-tuple-element.58), channel_id=1, source_target_pairs={{0,4},{1,5},{2,6},{3,7},{4,64},{5,65},{6,66},{7,67},{8,76},{9,77},... | collective-permute-start | bytes 3145736 | tf_op jit(solution)/shard_map/ppermute | solution.py:39
  17.5 20.0 %copy-start.3 = (bf16[1024,512]{1,0:T(8,128)(2,1)}, bf16[1024,512]{1,0:T(8,128)(2,1)S(1)}, u32[]{:S(2)}) copy-start(bf16[1024,512]{1,0:T(8,128)(2,1)S(1)} %collective-permute-done.2.weight_a) | copy-start | bytes 3145732
  17.5 20.0 %collective-permute-start.3 = (bf16[1024,512]{1,0:T(8,128)(2,1)S(1)}, bf16[1024,512]{1,0:T(8,128)(2,1)S(1)}, u32[]{:S(2)}, u32[]{:S(2)}) collective-permute-start(bf16[1024,512]{1,0:T(8,128)(2,1)S(1)} %collective-permute-done.2.weight_a), channel_id=1, source_target_pairs={{0,8},{1,9},{2,10},{3,11},{4,12},{5,13},{6,14},{7,15},{8,0},{9,1},... | collective-permute-start | bytes 3145736 | tf_op jit(solution)/shard_map/ppermute | solution.py:39
  28.7 14.0 %collective-permute-start.1 = (bf16[1024,512]{1,0:T(8,128)(2,1)S(1)}, bf16[1024,512]{1,0:T(8,128)(2,1)}, u32[]{:S(2)}, u32[]{:S(2)}) collective-permute-start(bf16[1024,512]{1,0:T(8,128)(2,1)S(1)} %collective-permute-done.weight_a), channel_id=1, source_target_pairs={{0,8},{1,9},{2,10},{3,11},{4,12},{5,13},{6,14},{7,15},{8,0},{9,1},... | collective-permute-start | bytes 3145736 | tf_op jit(solution)/shard_map/ppermute | solution.py:39
  46.7 6.9 %collective-permute-start.4 = (bf16[256,512]{1,0:T(8,128)(2,1)}, bf16[256,512]{1,0:T(8,128)(2,1)S(1)}, u32[]{:S(2)}, u32[]{:S(2)}) collective-permute-start(bf16[256,512]{1,0:T(8,128)(2,1)} %project_pair.3.key_own), channel_id=1, source_target_pairs={{0,8},{1,9},{2,10},{3,11},{4,12},{5,13},{6,14},{7,15},{8,16},{9,17... | collective-permute-start | bytes 786440 | tf_op jit(solution)/shard_map/ppermute | solution.py:39
  51.4 56.6 %collective-permute-start.5 = (bf16[256,2048]{1,0:T(8,128)(2,1)S(1)}, bf16[256,2048]{1,0:T(8,128)(2,1)S(1)}, u32[]{:S(2)}, u32[]{:S(2)}) collective-permute-start(bf16[256,2048]{1,0:T(8,128)(2,1)S(1)} %constant_dynamic-slice_fusion.3), channel_id=1, source_target_pairs={{0,8},{1,9},{2,10},{3,11},{4,12},{5,13},{6,14},{7,15},{8,0},{9,1},... | collective-permute-start | bytes 3145736 | tf_op jit(solution)/shard_map/ppermute | solution.py:39
  54.3 19.0 %copy-start = (bf16[1,256,8192]{2,1,0:T(8,128)(2,1)S(1)}, bf16[1,256,8192]{2,1,0:T(8,128)(2,1)}, u32[]{:S(2)}) copy-start(bf16[1,256,8192]{2,1,0:T(8,128)(2,1)} %param.6) | copy-start | bytes 12582916
  71.2 10.4 %copy-start.10 = (f32[256,512]{1,0:T(8,128)S(1)}, f32[256,512]{1,0:T(8,128)}, u32[]{:S(2)}) copy-start(f32[256,512]{1,0:T(8,128)} %get-tuple-element.31) | copy-start | bytes 1572868
  71.2 10.4 %collective-permute-start.10 = (bf16[256,512]{1,0:T(8,128)(2,1)}, bf16[256,512]{1,0:T(8,128)(2,1)S(1)}, u32[]{:S(2)}, u32[]{:S(2)}) collective-permute-start(bf16[256,512]{1,0:T(8,128)(2,1)} %get-tuple-element.32), channel_id=1, source_target_pairs={{8,0},{9,1},{10,2},{11,3},{12,4},{13,5},{14,6},{15,7},{16,8},{17,9... | collective-permute-start | bytes 786440 | tf_op jit(solution)/shard_map/ppermute | solution.py:39
  73.4 17.1 %collective-permute-start.9 = (bf16[128,2048]{1,0:T(8,128)(2,1)S(1)}, bf16[128,2048]{1,0:T(8,128)(2,1)S(1)}, u32[]{:S(2)}, u32[]{:S(2)}) collective-permute-start(bf16[128,2048]{1,0:T(8,128)(2,1)S(1)} %get-tuple-element.53), channel_id=1, source_target_pairs={{0,76},{1,77},{2,78},{3,79},{4,8},{5,9},{6,10},{7,11},{8,68},{9,69... | collective-permute-start | bytes 1572872 | tf_op jit(solution)/shard_map/ppermute | solution.py:39
  79.5 22.3 %collective-permute-start.8 = (bf16[128,2048]{1,0:T(8,128)(2,1)S(1)}, bf16[128,2048]{1,0:T(8,128)(2,1)S(1)}, u32[]{:S(2)}, u32[]{:S(2)}) collective-permute-start(bf16[128,2048]{1,0:T(8,128)(2,1)S(1)} %get-tuple-element.54), channel_id=1, source_target_pairs={{0,68},{1,69},{2,70},{3,71},{4,0},{5,1},{6,2},{7,3},{8,76},{9,77},... | collective-permute-start | bytes 1572872 | tf_op jit(solution)/shard_map/ppermute | solution.py:39
  80.0 26.1 %collective-permute-start.7 = (bf16[128,2048]{1,0:T(8,128)(2,1)S(1)}, bf16[128,2048]{1,0:T(8,128)(2,1)S(1)}, u32[]{:S(2)}, u32[]{:S(2)}) collective-permute-start(bf16[128,2048]{1,0:T(8,128)(2,1)S(1)} %get-tuple-element.55), channel_id=1, source_target_pairs={{0,12},{1,13},{2,14},{3,15},{4,72},{5,73},{6,74},{7,75},{8,4},{9,5... | collective-permute-start | bytes 1572872 | tf_op jit(solution)/shard_map/ppermute | solution.py:39
  81.6 26.4 %collective-permute-start.6 = (bf16[128,2048]{1,0:T(8,128)(2,1)S(1)}, bf16[128,2048]{1,0:T(8,128)(2,1)S(1)}, u32[]{:S(2)}, u32[]{:S(2)}) collective-permute-start(bf16[128,2048]{1,0:T(8,128)(2,1)S(1)} %get-tuple-element.56), channel_id=1, source_target_pairs={{0,4},{1,5},{2,6},{3,7},{4,64},{5,65},{6,66},{7,67},{8,12},{9,13},... | collective-permute-start | bytes 1572872 | tf_op jit(solution)/shard_map/ppermute | solution.py:39
  81.7 34.3 %copy-start.1 = (bf16[256,512]{1,0:T(8,128)(2,1)}, bf16[256,512]{1,0:T(8,128)(2,1)S(1)}, u32[]{:S(2)}) copy-start(bf16[256,512]{1,0:T(8,128)(2,1)S(1)} %add_convert_fusion.refs_6_) | copy-start | bytes 786436
  90.6 25.5 %copy-start.6 = (bf16[128,2048]{1,0:T(8,128)(2,1)}, bf16[128,2048]{1,0:T(8,128)(2,1)S(1)}, u32[]{:S(2)}) copy-start(bf16[128,2048]{1,0:T(8,128)(2,1)S(1)} %collective-permute-done.9.refs_5_) | copy-start | bytes 1572868
  90.6 25.4 %collective-permute-start.11 = (bf16[256,512]{1,0:T(8,128)(2,1)S(1)}, bf16[256,512]{1,0:T(8,128)(2,1)S(1)}, u32[]{:S(2)}, u32[]{:S(2)}) collective-permute-start(bf16[256,512]{1,0:T(8,128)(2,1)S(1)} %add_convert_fusion.refs_6_), channel_id=1, source_target_pairs={{0,8},{1,9},{2,10},{3,11},{4,12},{5,13},{6,14},{7,15},{8,0},{9,1},... | collective-permute-start | bytes 786440 | tf_op jit(solution)/shard_map/ppermute | solution.py:39
  101.8 14.2 %copy-start.7 = (bf16[128,2048]{1,0:T(8,128)(2,1)}, bf16[128,2048]{1,0:T(8,128)(2,1)S(1)}, u32[]{:S(2)}) copy-start(bf16[128,2048]{1,0:T(8,128)(2,1)S(1)} %collective-permute-done.8.refs_4_) | copy-start | bytes 1572868
  101.8 8.5 %collective-permute-start.15 = (bf16[128,512]{1,0:T(8,128)(2,1)S(1)}, bf16[128,512]{1,0:T(8,128)(2,1)S(1)}, u32[]{:S(2)}, u32[]{:S(2)}) collective-permute-start(bf16[128,512]{1,0:T(8,128)(2,1)S(1)} %get-tuple-element.59), channel_id=1, source_target_pairs={{0,76},{1,77},{2,78},{3,79},{4,8},{5,9},{6,10},{7,11},{8,68},{9,69... | collective-permute-start | bytes 393224 | tf_op jit(solution)/shard_map/ppermute | solution.py:39
  106.1 9.9 %copy-start.8 = (bf16[128,2048]{1,0:T(8,128)(2,1)}, bf16[128,2048]{1,0:T(8,128)(2,1)S(1)}, u32[]{:S(2)}) copy-start(bf16[128,2048]{1,0:T(8,128)(2,1)S(1)} %collective-permute-done.7.refs_3_) | copy-start | bytes 1572868
  106.1 5.8 %collective-permute-start.14 = (bf16[128,512]{1,0:T(8,128)(2,1)S(1)}, bf16[128,512]{1,0:T(8,128)(2,1)S(1)}, u32[]{:S(2)}, u32[]{:S(2)}) collective-permute-start(bf16[128,512]{1,0:T(8,128)(2,1)S(1)} %get-tuple-element.59), channel_id=1, source_target_pairs={{0,68},{1,69},{2,70},{3,71},{4,0},{5,1},{6,2},{7,3},{8,76},{9,77},... | collective-permute-start | bytes 393224 | tf_op jit(solution)/shard_map/ppermute | solution.py:39
  108.0 7.0 %collective-permute-start.13 = (bf16[128,512]{1,0:T(8,128)(2,1)S(1)}, bf16[128,512]{1,0:T(8,128)(2,1)S(1)}, u32[]{:S(2)}, u32[]{:S(2)}) collective-permute-start(bf16[128,512]{1,0:T(8,128)(2,1)S(1)} %get-tuple-element.60), channel_id=1, source_target_pairs={{0,12},{1,13},{2,14},{3,15},{4,72},{5,73},{6,74},{7,75},{8,4},{9,5... | collective-permute-start | bytes 393224 | tf_op jit(solution)/shard_map/ppermute | solution.py:39
  108.0 8.0 %collective-permute-start.12 = (bf16[128,512]{1,0:T(8,128)(2,1)S(1)}, bf16[128,512]{1,0:T(8,128)(2,1)S(1)}, u32[]{:S(2)}, u32[]{:S(2)}) collective-permute-start(bf16[128,512]{1,0:T(8,128)(2,1)S(1)} %get-tuple-element.60), channel_id=1, source_target_pairs={{0,4},{1,5},{2,6},{3,7},{4,64},{5,65},{6,66},{7,67},{8,12},{9,13},... | collective-permute-start | bytes 393224 | tf_op jit(solution)/shard_map/ppermute | solution.py:39
  127.8 9.0 %collective-permute-start.16 = (bf16[256,512]{1,0:T(8,128)(2,1)}, bf16[256,512]{1,0:T(8,128)(2,1)S(1)}, u32[]{:S(2)}, u32[]{:S(2)}) collective-permute-start(bf16[256,512]{1,0:T(8,128)(2,1)} %get-tuple-element.34), channel_id=1, source_target_pairs={{0,16},{1,17},{2,18},{3,19},{4,20},{5,21},{6,22},{7,23},{8,24},{9,... | collective-permute-start | bytes 786440 | tf_op jit(solution)/shard_map/ppermute | solution.py:39
  127.9 12.7 %collective-permute-start.17 = (bf16[256,512]{1,0:T(8,128)(2,1)}, bf16[256,512]{1,0:T(8,128)(2,1)S(1)}, u32[]{:S(2)}, u32[]{:S(2)}) collective-permute-start(bf16[256,512]{1,0:T(8,128)(2,1)} %get-tuple-element.35), channel_id=1, source_target_pairs={{0,32},{1,33},{2,34},{3,35},{4,36},{5,37},{6,38},{7,39},{8,40},{9,... | collective-permute-start | bytes 786440 | tf_op jit(solution)/shard_map/ppermute | solution.py:39
  128.5 13.6 %collective-permute-start.18 = (bf16[256,512]{1,0:T(8,128)(2,1)}, bf16[256,512]{1,0:T(8,128)(2,1)S(1)}, u32[]{:S(2)}, u32[]{:S(2)}) collective-permute-start(bf16[256,512]{1,0:T(8,128)(2,1)} %get-tuple-element.36), channel_id=1, source_target_pairs={{0,48},{1,49},{2,50},{3,51},{4,52},{5,53},{6,54},{7,55},{8,56},{9,... | collective-permute-start | bytes 786440 | tf_op jit(solution)/shard_map/ppermute | solution.py:39
  130.5 11.6 %collective-permute-start.19 = (bf16[256,512]{1,0:T(8,128)(2,1)}, bf16[256,512]{1,0:T(8,128)(2,1)S(1)}, u32[]{:S(2)}, u32[]{:S(2)}) collective-permute-start(bf16[256,512]{1,0:T(8,128)(2,1)} %get-tuple-element.38), channel_id=1, source_target_pairs={{0,1},{1,2},{2,3},{3,0},{4,5},{5,6},{6,7},{7,4},{8,9},{9,10},{10,1... | collective-permute-start | bytes 786440 | tf_op jit(solution)/shard_map/ppermute | solution.py:39
  132.1 13.5 %collective-permute-start.20 = (bf16[256,512]{1,0:T(8,128)(2,1)}, bf16[256,512]{1,0:T(8,128)(2,1)S(1)}, u32[]{:S(2)}, u32[]{:S(2)}) collective-permute-start(bf16[256,512]{1,0:T(8,128)(2,1)} %get-tuple-element.39), channel_id=1, source_target_pairs={{0,2},{1,3},{2,0},{3,1},{4,6},{5,7},{6,4},{7,5},{8,10},{9,11},{10,... | collective-permute-start | bytes 786440 | tf_op jit(solution)/shard_map/ppermute | solution.py:39
  136.8 8.8 %copy-start.21 = (bf16[256,512]{1,0:T(8,128)(2,1)}, bf16[256,512]{1,0:T(8,128)(2,1)S(1)}, u32[]{:S(2)}) copy-start(bf16[256,512]{1,0:T(8,128)(2,1)S(1)} %collective-permute-done.16.refs_1_) | copy-start | bytes 786436
  136.8 8.8 %collective-permute-start.21 = (bf16[256,512]{1,0:T(8,128)(2,1)}, bf16[256,512]{1,0:T(8,128)(2,1)S(1)}, u32[]{:S(2)}, u32[]{:S(2)}) collective-permute-start(bf16[256,512]{1,0:T(8,128)(2,1)} %get-tuple-element.40), channel_id=1, source_target_pairs={{0,3},{1,0},{2,1},{3,2},{4,7},{5,4},{6,5},{7,6},{8,11},{9,8},{10,9... | collective-permute-start | bytes 786440 | tf_op jit(solution)/shard_map/ppermute | solution.py:39
  149.2 7.6 %collective-permute-start.22 = (bf16[64,512]{1,0:T(8,128)(2,1)}, bf16[64,512]{1,0:T(8,128)(2,1)S(1)}, u32[]{:S(2)}, u32[]{:S(2)}) collective-permute-start(bf16[64,512]{1,0:T(8,128)(2,1)} %get-tuple-element.42), channel_id=1, source_target_pairs={{0,1},{1,2},{2,3},{3,0},{4,5},{5,6},{6,7},{7,4},{8,9},{9,10},{10,1... | collective-permute-start | bytes 196616 | tf_op jit(solution)/shard_map/ppermute | solution.py:39
  149.8 9.0 %collective-permute-start.23 = (bf16[64,512]{1,0:T(8,128)(2,1)}, bf16[64,512]{1,0:T(8,128)(2,1)S(1)}, u32[]{:S(2)}, u32[]{:S(2)}) collective-permute-start(bf16[64,512]{1,0:T(8,128)(2,1)} %get-tuple-element.43), channel_id=1, source_target_pairs={{0,2},{1,3},{2,0},{3,1},{4,6},{5,7},{6,4},{7,5},{8,10},{9,11},{10,... | collective-permute-start | bytes 196616 | tf_op jit(solution)/shard_map/ppermute | solution.py:39
  152.7 6.1 %collective-permute-start.24 = (bf16[64,512]{1,0:T(8,128)(2,1)}, bf16[64,512]{1,0:T(8,128)(2,1)S(1)}, u32[]{:S(2)}, u32[]{:S(2)}) collective-permute-start(bf16[64,512]{1,0:T(8,128)(2,1)} %get-tuple-element.44), channel_id=1, source_target_pairs={{0,3},{1,0},{2,1},{3,2},{4,7},{5,4},{6,5},{7,6},{8,11},{9,8},{10,9... | collective-permute-start | bytes 196616 | tf_op jit(solution)/shard_map/ppermute | solution.py:39
  152.8 6.0 %collective-permute-start.25 = (bf16[64,512]{1,0:T(8,128)(2,1)}, bf16[64,512]{1,0:T(8,128)(2,1)S(1)}, u32[]{:S(2)}, u32[]{:S(2)}) collective-permute-start(bf16[64,512]{1,0:T(8,128)(2,1)} %get-tuple-element.46), channel_id=1, source_target_pairs={{0,16},{1,17},{2,18},{3,19},{4,20},{5,21},{6,22},{7,23},{8,24},{9,... | collective-permute-start | bytes 196616 | tf_op jit(solution)/shard_map/ppermute | solution.py:39
  155.0 4.8 %collective-permute-start.26 = (bf16[64,512]{1,0:T(8,128)(2,1)}, bf16[64,512]{1,0:T(8,128)(2,1)S(1)}, u32[]{:S(2)}, u32[]{:S(2)}) collective-permute-start(bf16[64,512]{1,0:T(8,128)(2,1)} %get-tuple-element.47), channel_id=1, source_target_pairs={{0,32},{1,33},{2,34},{3,35},{4,36},{5,37},{6,38},{7,39},{8,40},{9,... | collective-permute-start | bytes 196616 | tf_op jit(solution)/shard_map/ppermute | solution.py:39
  156.7 3.7 %collective-permute-start.27 = (bf16[64,512]{1,0:T(8,128)(2,1)}, bf16[64,512]{1,0:T(8,128)(2,1)S(1)}, u32[]{:S(2)}, u32[]{:S(2)}) collective-permute-start(bf16[64,512]{1,0:T(8,128)(2,1)} %get-tuple-element.48), channel_id=1, source_target_pairs={{0,48},{1,49},{2,50},{3,51},{4,52},{5,53},{6,54},{7,55},{8,56},{9,... | collective-permute-start | bytes 196616 | tf_op jit(solution)/shard_map/ppermute | solution.py:39
  162.8 6.5 %collective-permute-start.28 = (bf16[128,512]{1,0:T(8,128)(2,1)}, bf16[128,512]{1,0:T(8,128)(2,1)S(1)}, u32[]{:S(2)}, u32[]{:S(2)}) collective-permute-start(bf16[128,512]{1,0:T(8,128)(2,1)} %sum_join.1.mine), channel_id=1, source_target_pairs={{0,64},{1,65},{2,66},{3,67},{4,68},{5,69},{6,70},{7,71},{8,72},{9,... | collective-permute-start | bytes 393224 | tf_op jit(solution)/shard_map/ppermute | solution.py:39
  171.7 6.1 %collective-permute-start.31 = (bf16[64,512]{1,0:T(8,128)(2,1)}, bf16[64,512]{1,0:T(8,128)(2,1)S(1)}, u32[]{:S(2)}, u32[]{:S(2)}) collective-permute-start(bf16[64,512]{1,0:T(8,128)(2,1)} %get-tuple-element.49.refs_0_), channel_id=1, source_target_pairs={{0,3},{1,0},{2,1},{3,2},{4,7},{5,4},{6,5},{7,6},{8,11},{9,8},{10,9... | collective-permute-start | bytes 196616 | tf_op jit(solution)/shard_map/ppermute | solution.py:39
  172.2 5.5 %collective-permute-start.30 = (bf16[64,512]{1,0:T(8,128)(2,1)}, bf16[64,512]{1,0:T(8,128)(2,1)S(1)}, u32[]{:S(2)}, u32[]{:S(2)}) collective-permute-start(bf16[64,512]{1,0:T(8,128)(2,1)} %get-tuple-element.49.refs_0_), channel_id=1, source_target_pairs={{0,2},{1,3},{2,0},{3,1},{4,6},{5,7},{6,4},{7,5},{8,10},{9,11},{10,... | collective-permute-start | bytes 196616 | tf_op jit(solution)/shard_map/ppermute | solution.py:39
  174.9 4.5 %collective-permute-start.29 = (bf16[64,512]{1,0:T(8,128)(2,1)}, bf16[64,512]{1,0:T(8,128)(2,1)S(1)}, u32[]{:S(2)}, u32[]{:S(2)}) collective-permute-start(bf16[64,512]{1,0:T(8,128)(2,1)} %get-tuple-element.49.refs_0_), channel_id=1, source_target_pairs={{0,1},{1,2},{2,3},{3,0},{4,5},{5,6},{6,7},{7,4},{8,9},{9,10},{10,1... | collective-permute-start | bytes 196616 | tf_op jit(solution)/shard_map/ppermute | solution.py:39
  174.9 4.5 %collective-permute-start.34 = (bf16[64,512]{1,0:T(8,128)(2,1)}, bf16[64,512]{1,0:T(8,128)(2,1)S(1)}, u32[]{:S(2)}, u32[]{:S(2)}) collective-permute-start(bf16[64,512]{1,0:T(8,128)(2,1)} %get-tuple-element.50.refs_4_), channel_id=1, source_target_pairs={{0,48},{1,49},{2,50},{3,51},{4,52},{5,53},{6,54},{7,55},{8,56},{9,... | collective-permute-start | bytes 196616 | tf_op jit(solution)/shard_map/ppermute | solution.py:39
  177.1 4.9 %collective-permute-start.33 = (bf16[64,512]{1,0:T(8,128)(2,1)}, bf16[64,512]{1,0:T(8,128)(2,1)S(1)}, u32[]{:S(2)}, u32[]{:S(2)}) collective-permute-start(bf16[64,512]{1,0:T(8,128)(2,1)} %get-tuple-element.50.refs_4_), channel_id=1, source_target_pairs={{0,32},{1,33},{2,34},{3,35},{4,36},{5,37},{6,38},{7,39},{8,40},{9,... | collective-permute-start | bytes 196616 | tf_op jit(solution)/shard_map/ppermute | solution.py:39
  177.8 4.9 %collective-permute-start.32 = (bf16[64,512]{1,0:T(8,128)(2,1)}, bf16[64,512]{1,0:T(8,128)(2,1)S(1)}, u32[]{:S(2)}, u32[]{:S(2)}) collective-permute-start(bf16[64,512]{1,0:T(8,128)(2,1)} %get-tuple-element.50.refs_4_), channel_id=1, source_target_pairs={{0,16},{1,17},{2,18},{3,19},{4,20},{5,21},{6,22},{7,23},{8,24},{9,... | collective-permute-start | bytes 196616 | tf_op jit(solution)/shard_map/ppermute | solution.py:39
  185.2 12.3 %collective-permute-start.41 = (bf16[256,512]{1,0:T(8,128)(2,1)}, bf16[256,512]{1,0:T(8,128)(2,1)S(1)}, u32[]{:S(2)}, u32[]{:S(2)}) collective-permute-start(bf16[256,512]{1,0:T(8,128)(2,1)} %get-tuple-element.51.refs_0_), channel_id=1, source_target_pairs={{0,8},{1,9},{2,10},{3,11},{4,12},{5,13},{6,14},{7,15},{8,0},{9,1},... | collective-permute-start | bytes 786440 | tf_op jit(solution)/shard_map/ppermute | solution.py:39
  194.8 8.1 %collective-permute-start.37 = (bf16[256,512]{1,0:T(8,128)(2,1)}, bf16[256,512]{1,0:T(8,128)(2,1)S(1)}, u32[]{:S(2)}, u32[]{:S(2)}) collective-permute-start(bf16[256,512]{1,0:T(8,128)(2,1)} %get-tuple-element.51.refs_0_), channel_id=1, source_target_pairs={{0,48},{1,49},{2,50},{3,51},{4,52},{5,53},{6,54},{7,55},{8,56},{9,... | collective-permute-start | bytes 786440 | tf_op jit(solution)/shard_map/ppermute | solution.py:39
  195.1 9.6 %collective-permute-start.36 = (bf16[256,512]{1,0:T(8,128)(2,1)}, bf16[256,512]{1,0:T(8,128)(2,1)S(1)}, u32[]{:S(2)}, u32[]{:S(2)}) collective-permute-start(bf16[256,512]{1,0:T(8,128)(2,1)} %get-tuple-element.51.refs_0_), channel_id=1, source_target_pairs={{0,32},{1,33},{2,34},{3,35},{4,36},{5,37},{6,38},{7,39},{8,40},{9,... | collective-permute-start | bytes 786440 | tf_op jit(solution)/shard_map/ppermute | solution.py:39
  195.8 14.8 %collective-permute-start.35 = (bf16[256,512]{1,0:T(8,128)(2,1)}, bf16[256,512]{1,0:T(8,128)(2,1)S(1)}, u32[]{:S(2)}, u32[]{:S(2)}) collective-permute-start(bf16[256,512]{1,0:T(8,128)(2,1)} %get-tuple-element.51.refs_0_), channel_id=1, source_target_pairs={{0,16},{1,17},{2,18},{3,19},{4,20},{5,21},{6,22},{7,23},{8,24},{9,... | collective-permute-start | bytes 786440 | tf_op jit(solution)/shard_map/ppermute | solution.py:39
  196.7 14.4 %collective-permute-start.45 = (bf16[256,512]{1,0:T(8,128)(2,1)}, bf16[256,512]{1,0:T(8,128)(2,1)S(1)}, u32[]{:S(2)}, u32[]{:S(2)}) collective-permute-start(bf16[256,512]{1,0:T(8,128)(2,1)} %get-tuple-element.52.refs_4_), channel_id=1, source_target_pairs={{0,8},{1,9},{2,10},{3,11},{4,12},{5,13},{6,14},{7,15},{8,0},{9,1},... | collective-permute-start | bytes 786440 | tf_op jit(solution)/shard_map/ppermute | solution.py:39
  197.6 23.0 %copy-start.11 = (bf16[256,512]{1,0:T(8,128)(2,1)}, bf16[256,512]{1,0:T(8,128)(2,1)S(1)}, u32[]{:S(2)}) copy-start(bf16[256,512]{1,0:T(8,128)(2,1)S(1)} %collective-permute-done.41.refs_8_) | copy-start | bytes 786436
  197.6 13.7 %collective-permute-start.40 = (bf16[256,512]{1,0:T(8,128)(2,1)}, bf16[256,512]{1,0:T(8,128)(2,1)S(1)}, u32[]{:S(2)}, u32[]{:S(2)}) collective-permute-start(bf16[256,512]{1,0:T(8,128)(2,1)} %get-tuple-element.52.refs_4_), channel_id=1, source_target_pairs={{0,3},{1,0},{2,1},{3,2},{4,7},{5,4},{6,5},{7,6},{8,11},{9,8},{10,9... | collective-permute-start | bytes 786440 | tf_op jit(solution)/shard_map/ppermute | solution.py:39
  202.9 17.6 %copy-start.12 = (bf16[256,512]{1,0:T(8,128)(2,1)}, bf16[256,512]{1,0:T(8,128)(2,1)S(1)}, u32[]{:S(2)}) copy-start(bf16[256,512]{1,0:T(8,128)(2,1)S(1)} %collective-permute-done.37.refs_3_) | copy-start | bytes 786436
  202.9 8.7 %collective-permute-start.39 = (bf16[256,512]{1,0:T(8,128)(2,1)}, bf16[256,512]{1,0:T(8,128)(2,1)S(1)}, u32[]{:S(2)}, u32[]{:S(2)}) collective-permute-start(bf16[256,512]{1,0:T(8,128)(2,1)} %get-tuple-element.52.refs_4_), channel_id=1, source_target_pairs={{0,2},{1,3},{2,0},{3,1},{4,6},{5,7},{6,4},{7,5},{8,10},{9,11},{10,... | collective-permute-start | bytes 786440 | tf_op jit(solution)/shard_map/ppermute | solution.py:39
  204.7 15.8 %copy-start.13 = (bf16[256,512]{1,0:T(8,128)(2,1)}, bf16[256,512]{1,0:T(8,128)(2,1)S(1)}, u32[]{:S(2)}) copy-start(bf16[256,512]{1,0:T(8,128)(2,1)S(1)} %collective-permute-done.36.refs_2_) | copy-start | bytes 786436
  204.7 13.8 %collective-permute-start.38 = (bf16[256,512]{1,0:T(8,128)(2,1)}, bf16[256,512]{1,0:T(8,128)(2,1)S(1)}, u32[]{:S(2)}, u32[]{:S(2)}) collective-permute-start(bf16[256,512]{1,0:T(8,128)(2,1)} %get-tuple-element.52.refs_4_), channel_id=1, source_target_pairs={{0,1},{1,2},{2,3},{3,0},{4,5},{5,6},{6,7},{7,4},{8,9},{9,10},{10,1... | collective-permute-start | bytes 786440 | tf_op jit(solution)/shard_map/ppermute | solution.py:39
  210.7 9.9 %copy-start.14 = (bf16[256,512]{1,0:T(8,128)(2,1)}, bf16[256,512]{1,0:T(8,128)(2,1)S(1)}, u32[]{:S(2)}) copy-start(bf16[256,512]{1,0:T(8,128)(2,1)S(1)} %collective-permute-done.35.refs_1_) | copy-start | bytes 786436
  210.7 8.3 %collective-permute-start.44 = (bf16[256,512]{1,0:T(8,128)(2,1)S(1)}, bf16[256,512]{1,0:T(8,128)(2,1)S(1)}, u32[]{:S(2)}, u32[]{:S(2)}) collective-permute-start(bf16[256,512]{1,0:T(8,128)(2,1)S(1)} %collective-permute-done.37.refs_3_), channel_id=1, source_target_pairs={{0,8},{1,9},{2,10},{3,11},{4,12},{5,13},{6,14},{7,15},{8,0},{9,1},... | collective-permute-start | bytes 786440 | tf_op jit(solution)/shard_map/ppermute | solution.py:39
  211.1 9.4 %copy-start.15 = (bf16[256,512]{1,0:T(8,128)(2,1)}, bf16[256,512]{1,0:T(8,128)(2,1)S(1)}, u32[]{:S(2)}) copy-start(bf16[256,512]{1,0:T(8,128)(2,1)S(1)} %collective-permute-done.45.refs_12_) | copy-start | bytes 786436
  211.1 7.9 %collective-permute-start.43 = (bf16[256,512]{1,0:T(8,128)(2,1)S(1)}, bf16[256,512]{1,0:T(8,128)(2,1)S(1)}, u32[]{:S(2)}, u32[]{:S(2)}) collective-permute-start(bf16[256,512]{1,0:T(8,128)(2,1)S(1)} %collective-permute-done.36.refs_2_), channel_id=1, source_target_pairs={{0,8},{1,9},{2,10},{3,11},{4,12},{5,13},{6,14},{7,15},{8,0},{9,1},... | collective-permute-start | bytes 786440 | tf_op jit(solution)/shard_map/ppermute | solution.py:39
  211.2 9.3 %copy-start.16 = (bf16[256,512]{1,0:T(8,128)(2,1)}, bf16[256,512]{1,0:T(8,128)(2,1)S(1)}, u32[]{:S(2)}) copy-start(bf16[256,512]{1,0:T(8,128)(2,1)S(1)} %collective-permute-done.40.refs_7_) | copy-start | bytes 786436
  211.2 7.9 %collective-permute-start.42 = (bf16[256,512]{1,0:T(8,128)(2,1)S(1)}, bf16[256,512]{1,0:T(8,128)(2,1)S(1)}, u32[]{:S(2)}, u32[]{:S(2)}) collective-permute-start(bf16[256,512]{1,0:T(8,128)(2,1)S(1)} %collective-permute-done.35.refs_1_), channel_id=1, source_target_pairs={{0,8},{1,9},{2,10},{3,11},{4,12},{5,13},{6,14},{7,15},{8,0},{9,1},... | collective-permute-start | bytes 786440 | tf_op jit(solution)/shard_map/ppermute | solution.py:39
  211.7 8.9 %copy-start.17 = (bf16[256,512]{1,0:T(8,128)(2,1)}, bf16[256,512]{1,0:T(8,128)(2,1)S(1)}, u32[]{:S(2)}) copy-start(bf16[256,512]{1,0:T(8,128)(2,1)S(1)} %collective-permute-done.39.refs_6_) | copy-start | bytes 786436
  211.7 7.4 %collective-permute-start.48 = (bf16[256,512]{1,0:T(8,128)(2,1)S(1)}, bf16[256,512]{1,0:T(8,128)(2,1)S(1)}, u32[]{:S(2)}, u32[]{:S(2)}) collective-permute-start(bf16[256,512]{1,0:T(8,128)(2,1)S(1)} %collective-permute-done.40.refs_7_), channel_id=1, source_target_pairs={{0,8},{1,9},{2,10},{3,11},{4,12},{5,13},{6,14},{7,15},{8,0},{9,1},... | collective-permute-start | bytes 786440 | tf_op jit(solution)/shard_map/ppermute | solution.py:39
  218.5 1.7 collective-permute-start.47
  219.0 1.5 collective-permute-start.46
  (35 other events, 90.2 us)

commit v2 on v1

v2 whole, which is shorter than its diff:
```python
import functools
import math

import jax
import jax.numpy as jnp
from jax import lax
from jax.experimental import pallas as pl
from jax.experimental.pallas import tpu as pltpu
from jax.sharding import Mesh, PartitionSpec as P

QH = 32
KVH = 4
HD = 128
GROUP = QH // KVH
BF = jnp.bfloat16
F32 = jnp.float32
AXES = ("xh", "y", "core", "xl", "z")
FACTOR = HD ** (-0.5)
EXP_SCALE = FACTOR * math.log2(math.e)
NEG = -1e30


def coords(index):
    seq, rest = divmod(index, 8)
    fsdp, z = divmod(rest, 4)
    return seq // 8, (seq // 2) % 4, seq % 2, fsdp, z


def linear(xh, y, core, xl, z):
    return ((xh * 8 + y * 2 + core) * 2 + xl) * 4 + z


def move(value, where):
    pairs = []
    for index in range(128):
        target = where(*coords(index))
        if target is not None:
            pairs.append((index, linear(*target)))
    return lax.ppermute(value, AXES, pairs)


def along_x(xh, y, core, xl, z, step, other=0):
    x = (xh * 2 + xl + step) % 4
    return x // 2, y, core ^ other, x % 2, z


def params(mib):
    return pltpu.CompilerParams(vmem_limit_bytes=mib << 20)


def cost(flops, moved):
    return pl.CostEstimate(flops=int(flops), bytes_accessed=int(moved), transcendentals=0)


def own_half_kernel(place, hidden, weight, out):
    @pl.when(pl.program_id(0) == 0)
    def _():
        out[...] = jnp.zeros_like(out)

    out[...] += jnp.dot(hidden[...], weight[...], preferred_element_type=F32)


def project_own(place, tokens, weight):
    rows, model = tokens.shape
    half, width = weight.shape
    step = half // 4
    return pl.pallas_call(
        own_half_kernel,
        grid_spec=pltpu.PrefetchScalarGridSpec(
            num_scalar_prefetch=1,
            grid=(4,),
            in_specs=[
                pl.BlockSpec((rows, step), lambda i, p: (0, p[0] * 4 + i)),
                pl.BlockSpec((step, width), lambda i, p: (i, 0)),
            ],
            out_specs=pl.BlockSpec((rows, width), lambda i, p: (0, 0)),
        ),
        out_shape=jax.ShapeDtypeStruct((rows, width), F32),
        compiler_params=params(8),
        cost_estimate=cost(2 * rows * half * width, 6 << 20),
        name="project_own",
    )(place, tokens, weight)


def add_kernel(count, place, *refs):
    hidden, weights, total, out = refs[:count], refs[count:2 * count], refs[2 * count], refs[2 * count + 1]
    acc = total[...]
    for h, w in zip(hidden, weights):
        acc = acc + jnp.dot(h[...], w[...], preferred_element_type=F32)
    out[...] = acc.astype(out.dtype)


def project_add(place, tokens, weights, which, total, dtype):
    rows, model = tokens.shape
    step, width = weights[0].shape

    def block(other, chunk):
        def index(i, p):
            return (0, (1 - p[0]) * 4 + ((1 - p[1]) if other else p[1]) * 2 + chunk)

        return index

    whole = lambda i, p: (0, 0)
    return pl.pallas_call(
        functools.partial(add_kernel, len(weights)),
        grid_spec=pltpu.PrefetchScalarGridSpec(
            num_scalar_prefetch=1,
            grid=(1,),
            in_specs=[pl.BlockSpec((rows, step), block(*w)) for w in which]
            + [pl.BlockSpec((step, width), whole) for _ in which]
            + [pl.BlockSpec((rows, width), whole)],
            out_specs=pl.BlockSpec((rows, width), whole),
        ),
        out_shape=jax.ShapeDtypeStruct((rows, width), dtype),
        compiler_params=params(12),
        cost_estimate=cost(2 * len(weights) * rows * step * width, 2 << 20),
        name="project_add",
    )(place, *([tokens] * len(weights)), *weights, total)


def attend_kernel(place, lengths, query, key_own, key_halo, weight, entropy, grad_query, grad_own,
                  grad_halo, bias, keys, keys_t):
    @pl.when(pl.program_id(0) == 0)
    def _():
        base = place[2] * 256
        position = base + lax.broadcasted_iota(jnp.int32, (8, 256), 1)

        def add(i, state):
            end, first = state
            end = end + lengths[0, i]
            return end, jnp.where(position >= end, end, first)

        _, first = lax.fori_loop(
            0, lengths.shape[1], add, (jnp.int32(0), jnp.zeros((8, 256), jnp.int32))
        )
        for half in range(2):
            begin = first[0:1, half * 128:(half + 1) * 128]
            here = position[0:1, half * 128:(half + 1) * 128]
            there = base - 256 + half * 128 + lax.broadcasted_iota(jnp.int32, (384, 128), 0)
            seen = (there >= begin) & (there <= here)
            value = jnp.where(seen, 0.0, NEG)
            bias[half, :, 0:128] = value
            bias[half, :, 128:256] = value

    keys[0:256, :] = key_halo[...]
    keys[256:512, :] = key_own[...]
    keys_t[...] = keys[...].T
    weights = weight[...].astype(F32)
    sums = [None, None]
    for pair in range(GROUP // 2):
        cols = [slice((2 * pair + k) * HD, (2 * pair + k + 1) * HD) for k in range(2)]
        for half in range(2):
            rows = slice(half * 128, (half + 1) * 128)
            window = slice(half * 128, half * 128 + 384)
            stack = jnp.concatenate([query[rows, cols[0]], query[rows, cols[1]]], axis=0)
            raw = lax.dot_general(
                keys[window, :], stack, (((1,), (1,)), ((), ())), preferred_element_type=F32
            ) + bias[half]
            top = jnp.max(raw, axis=0, keepdims=True)
            gap = raw - top
            power = jnp.exp2(gap * EXP_SCALE)
            den = jnp.sum(power, axis=0, keepdims=True)
            mean = jnp.sum(power * gap, axis=0, keepdims=True) / den
            row_weight = jnp.concatenate(
                [weights[2 * pair:2 * pair + 1, rows], weights[2 * pair + 1:2 * pair + 2, rows]], axis=1
            )
            slope_b = row_weight * FACTOR / den
            slope_a = slope_b * mean
            slope = (power * (slope_a - slope_b * gap)).astype(BF)
            level = jnp.log(den) - FACTOR * mean
            entropy[2 * pair:2 * pair + 1, rows] = level[:, 0:128]
            entropy[2 * pair + 1:2 * pair + 2, rows] = level[:, 128:256]
            turned = jnp.dot(keys_t[:, window], slope, preferred_element_type=F32) * FACTOR
            straight = turned.T.astype(BF)
            grad_query[rows, cols[0]] = straight[0:128]
            grad_query[rows, cols[1]] = straight[128:256]
            part = jnp.dot(slope, stack, preferred_element_type=F32)
            sums[half] = part if sums[half] is None else sums[half] + part
    low, high = sums
    grad_halo[0:128, :] = (low[0:128] * FACTOR).astype(grad_halo.dtype)
    grad_halo[128:256, :] = ((low[128:256] + high[0:128]) * FACTOR).astype(grad_halo.dtype)
    grad_own[0:128, :] = (low[256:384] + high[128:256]) * FACTOR
    grad_own[128:256, :] = high[256:384] * FACTOR


def attend(place, lengths, queries, key_own, key_halo, weight):
    rows, width = queries.shape
    wide = GROUP * HD
    by_head = lambda j, p, l: (0, j)
    return pl.pallas_call(
        attend_kernel,
        grid_spec=pltpu.PrefetchScalarGridSpec(
            num_scalar_prefetch=2,
            grid=(KVH,),
            in_specs=[
                pl.BlockSpec((rows, wide), by_head),
                pl.BlockSpec((rows, HD), by_head),
                pl.BlockSpec((rows, HD), by_head),
                pl.BlockSpec((GROUP, rows), lambda j, p, l: (j, 0)),
            ],
            out_specs=[
                pl.BlockSpec((GROUP, rows), lambda j, p, l: (j, 0)),
                pl.BlockSpec((rows, wide), by_head),
                pl.BlockSpec((rows, HD), by_head),
                pl.BlockSpec((rows, HD), by_head),
            ],
            scratch_shapes=[
                pltpu.VMEM((2, 384, 256), F32),
                pltpu.VMEM((512, HD), BF),
                pltpu.VMEM((HD, 512), BF),
            ],
        ),
        out_shape=[
            jax.ShapeDtypeStruct((QH, rows), F32),
            jax.ShapeDtypeStruct((rows, width), BF),
            jax.ShapeDtypeStruct((rows, KVH * HD), F32),
            jax.ShapeDtypeStruct((rows, KVH * HD), BF),
        ],
        compiler_params=params(16),
        cost_estimate=cost(4 << 30, 6 << 20),
        name="attend",
    )(place, lengths, queries, key_own, key_halo, weight)


def weight_grad_kernel(place, *refs):
    hidden, grads, out = refs[0:6], refs[6:12], refs[12]
    total = None
    for piece, grad in zip(hidden, grads):
        part = lax.dot_general(
            piece[...], grad[...], (((0,), (0,)), ((), ())), preferred_element_type=F32
        )
        total = part if total is None else total + part
    out[...] = total.astype(BF)


def weight_grad(place, tokens, pieces, grads):
    whole = lambda i, p: (0, 0)
    return pl.pallas_call(
        weight_grad_kernel,
        grid_spec=pltpu.PrefetchScalarGridSpec(
            num_scalar_prefetch=1,
            grid=(8,),
            in_specs=[pl.BlockSpec((256, 256), lambda i, p: (0, (p[0] * 2 + p[1]) * 8 + i))]
            + [pl.BlockSpec((v.shape[0], 256), lambda i, p: (0, i)) for v in pieces]
            + [pl.BlockSpec(v.shape, whole) for v in grads],
            out_specs=pl.BlockSpec((256, 512), lambda i, p: (i, 0)),
        ),
        out_shape=jax.ShapeDtypeStruct((2048, 512), BF),
        compiler_params=params(16),
        cost_estimate=cost(2 * 1024 * 2048 * 512, 8 << 20),
        name="weight_grad",
    )(place, tokens, *pieces, *grads)


def sum_spread_kernel(scale, parts, out):
    total = parts[0].astype(F32)
    for k in range(1, parts.shape[0]):
        total = total + parts[k].astype(F32)
    low = (total * scale).astype(BF)
    for k in range(parts.shape[0]):
        out[k] = low


def sum_spread(parts, scale):
    count, rows, width = parts.shape
    block = pl.BlockSpec((count, rows // 4, width), lambda i: (0, i, 0))
    return pl.pallas_call(
        functools.partial(sum_spread_kernel, scale),
        grid=(4,),
        in_specs=[block],
        out_specs=block,
        out_shape=jax.ShapeDtypeStruct(parts.shape, BF),
        compiler_params=params(8),
        cost_estimate=cost(2 << 20, 4 << 20),
        name="sum_spread",
    )(parts)


def join_kernel(place, mine, other, out):
    first = pl.program_id(0) < 2
    own = first == (place[1] == 0)

    @pl.when(own)
    def _():
        out[...] = mine[...]

    @pl.when(jnp.logical_not(own))
    def _():
        out[...] = other[...]


def join_cores(place, mine, other):
    rows, width = mine.shape
    step = rows // 2

    def mine_block(i, p):
        return (jnp.where((i < 2) == (p[1] == 0), i % 2, jnp.where(i < 2, 0, 1)), 0)

    def other_block(i, p):
        return (jnp.where((i < 2) == (p[1] == 0), jnp.where(i < 2, 0, 1), i % 2), 0)

    return pl.pallas_call(
        join_kernel,
        grid_spec=pltpu.PrefetchScalarGridSpec(
            num_scalar_prefetch=1,
            grid=(4,),
            in_specs=[pl.BlockSpec((step, width), mine_block), pl.BlockSpec((step, width), other_block)],
            out_specs=pl.BlockSpec((step, width), lambda i, p: (i, 0)),
        ),
        out_shape=jax.ShapeDtypeStruct((2 * rows, width), BF),
        compiler_params=params(10),
        cost_estimate=cost(1 << 20, 8 << 20),
        name="join_cores",
    )(place, mine, other)


def swap_core(xh, y, core, xl, z):
    return xh, y, 1 - core, xl, z


def next_rows(step):
    def where(xh, y, core, xl, z):
        seq = xh * 8 + y * 2 + core + step
        if seq < 0 or seq > 15:
            return None
        return seq // 8, (seq // 2) % 4, seq % 2, xl, z

    return where


def shards(queries, hidden, key_weight, doc_lengths, entropy_cot):
    tokens = hidden[0]
    rows, model = tokens.shape
    half, width = key_weight.shape
    fsdp, core = lax.axis_index("xl"), lax.axis_index("core")
    seq = lax.axis_index(("xh", "y", "core"))
    place = jnp.stack([fsdp, core, seq]).astype(jnp.int32)

    mine = lax.dynamic_slice_in_dim(key_weight, core * (half // 2), half // 2, 0)
    fetch = lambda xh, y, core, xl, z: along_x(xh, y, core, xl, z, 1 - 2 * core)
    got = [move(mine[k * half // 4:(k + 1) * half // 4], fetch) for k in range(2)]
    total = project_own(place, tokens, key_weight)

    quarter = model // 4

    def column(first, last, is_fsdp, is_core):
        start = (is_fsdp * 2 + is_core) * quarter
        return lax.dynamic_slice(tokens, (first, start), (last - first, quarter))

    split = rows // 2
    routes = [swap_core]
    for step in (1, -1):
        for other in (0, 1):
            routes.append(functools.partial(along_x, step=step, other=other))
    columns = [column(0, rows, fsdp, 1 - core)]
    for k, route in enumerate(routes[1:]):
        first = 0 if k < 2 else split
        columns.append(column(first, first + split, 1 - fsdp, core if k % 2 == 0 else 1 - core))

    got[0], total, columns = lax.optimization_barrier((got[0], total, columns))
    swapped = [move(v, swap_core) for v in got]
    total = project_add(place, tokens, got[:1], [(False, 0)], total, F32)
    total = project_add(place, tokens, got[1:], [(False, 1)], total, F32)
    key_own = project_add(place, tokens, swapped, [(True, 0), (True, 1)], total, BF)
    key_halo = move(key_own, next_rows(1))

    columns, _ = lax.optimization_barrier((columns, got[1]))
    pieces = [move(v, route) for v, route in zip(columns, routes)]

    entropy, grad_query, grad_own, grad_halo = attend(
        place, doc_lengths, queries[0], key_own, key_halo, entropy_cot[0].T
    )

    grad_halo, pieces = lax.optimization_barrier((grad_halo, pieces))
    from_next = move(grad_halo, next_rows(-1))
    key_grad = (grad_own + from_next.astype(F32)).astype(BF)
    grads = [key_grad, move(key_grad, routes[0])]
    for k, route in enumerate(routes[1:]):
        first = 0 if k < 2 else split
        grads.append(move(key_grad[first:first + split], route))

    chips = ("xh", "y", "z")
    parts = weight_grad(place, tokens, pieces, grads).reshape(32, 64, width)
    parts = lax.all_to_all(parts, chips, split_axis=0, concat_axis=0, tiled=True)
    spread = sum_spread(parts, (rows * 16 * 8) ** (-0.5))
    final = lax.all_to_all(spread, chips, split_axis=0, concat_axis=0, tiled=True).reshape(2048, width)
    other = move(final, swap_core)
    grad_weight = join_cores(place, final, other)
    return entropy.T[None], grad_query[None], grad_weight


def solution(mesh):
    fine = Mesh(mesh.devices.reshape(2, 4, 2, 2, 4), AXES)
    seq = ("xh", "y", "core")
    both = ("xl", "z")
    return jax.shard_map(
        shards,
        mesh=fine,
        in_specs=(
            P(both, seq, None),
            P(both, seq, None),
            P("xl", None),
            P(both, None),
            P(both, seq, None),
        ),
        out_specs=(P(both, seq, None), P(both, seq, None), P("xl", None)),
        check_vma=False,
    )
```

time: 227 us -> 175 us (0.77)
  blocking collectives: 0 us -> 68.6 us
  starting transfers between devices: 85.2 us -> 31.6 us
  waiting for transfers between devices: 75.3 us -> 35.3 us
  Pallas kernels: 53.7 us -> 31.2 us
  local copies, waits for them, and re-layouts: 10.5 us -> 7.43 us
    all_to_all x0 -> x2, blocking collectives: none -> 68.6 us  [the longest x1 36.2 us: shards(): lax.all_to_all(parts, chips, split_axis=0, concat_axis=0, tiled=True)]
    ppermute x49 -> x17, starting transfers between devices: 85.2 us -> 31.6 us  [move(): return lax.ppermute(value, AXES, pairs)]
    ppermute x49 -> x17, waiting for transfers between devices: 75.3 us -> 35.3 us  [move(): return lax.ppermute(value, AXES, pairs)]
    pallas_call x7 -> x5, Pallas kernels: 20.7 us -> 7.01 us  [the longest x3 3.2 us: project_add(): pl.pallas_call(functools.partial(add_kernel, len(weights)), grid_spec=plt...]
    pallas_call x1, Pallas kernels: 10.4 us -> 6.12 us  [weight_grad(): pl.pallas_call(weight_grad_kernel, grid_spec=pltpu.PrefetchScalarGridSpec...]
    pallas_call x1, Pallas kernels: 5.76 us -> 2.57 us  [project_own(): pl.pallas_call(own_half_kernel, grid_spec=pltpu.PrefetchScalarGridSpec(nu...]
    unnamed x100 -> x12, local copies, waits for them, and re-layouts: 6.71 us -> 4.4 us
  transfers between devices with their start and end apart: 49 -> 17, of which waited for: 23 -> 12; matrix products, arithmetic and copies ran while one was open for 1% -> 0% of each run, Pallas kernels for 12% -> 12%
where the time goes in v2:
time: 175 us
  blocking collectives  68.6 us (39%)
  waiting for transfers between devices  35.3 us (20%)
  starting transfers between devices  31.6 us (18%)
  Pallas kernels  31.2 us (18%)
  local copies, waits for them, and re-layouts  7.43 us (4%)
    all_to_all x1, blocking collectives, shards(): lax.all_to_all(parts, chips, split_axis=0, concat_axis=0, tiled=True)  36.2 us
    ppermute x17, waiting for transfers between devices, move(): return lax.ppermute(value, AXES, pairs)  35.3 us
    all_to_all x1, blocking collectives, shards(): lax.all_to_all(spread, chips, split_axis=0, concat_axis=0, tiled=True)  32.3 us
    ppermute x17, starting transfers between devices, move(): return lax.ppermute(value, AXES, pairs)  31.6 us
    pallas_call x1, Pallas kernels, attend(): pl.pallas_call(attend_kernel, grid_spec=pltpu.PrefetchScalarGridSpec(num_...  15.5 us
    pallas_call x1, Pallas kernels, weight_grad(): pl.pallas_call(weight_grad_kernel, grid_spec=pltpu.PrefetchScalarGridSpec...  6.12 us
    unnamed x12, local copies, waits for them, and re-layouts  4.4 us
  transfers between devices with their start and end apart: 17, of which 12 were waited for; matrix products, arithmetic and copies ran while one was open for 0% of the time, Pallas kernels for 12%

profile of v2, /device:TPU:1, one launch (start us, length us, event | category | flops | bytes accessed | tf_op | source)
XLA Modules:
  0.0 175.0 jit_solution(8003955714140525014)
XLA Ops:
  0.6 2.7 %constant_dynamic-slice_fusion.1 = (bf16[1024,512]{1,0:T(8,128)(2,1)S(1)}, bf16[1024,512]{1,0:T(8,128)(2,1)}) fusion(bf16[4096,512]{1,0:T(8,128)(2,1)} %weight.1, s32[]{:T(128)S(6)} %add.46, s32[]{:T(128)S(6)} %select_n.14), kind=kLoop, calls=%fused_computation.7 | loop fusion | bytes 4194312 | tf_op jit(solution)/shard_map/slice | solution.py:341
  3.3 3.3 %collective-permute-start = (bf16[1024,512]{1,0:T(8,128)(2,1)}, bf16[1024,512]{1,0:T(8,128)(2,1)S(1)}, u32[]{:S(2)}, u32[]{:S(2)}) collective-permute-start(bf16[1024,512]{1,0:T(8,128)(2,1)} %get-tuple-element.48), channel_id=1, source_target_pairs={{0,4},{1,5},{2,6},{3,7},{4,64},{5,65},{6,66},{7,67},{8,76},{9,77},... | collective-permute-start | bytes 3145736 | tf_op jit(solution)/shard_map/ppermute | solution.py:39
  6.6 0.5 collective-permute-start.2
  7.1 0.1 pad_add_fusion.place
  7.2 0.0 copy-start
  7.2 2.2 %copy-done = bf16[1,256,8192]{2,1,0:T(8,128)(2,1)S(1)} copy-done((bf16[1,256,8192]{2,1,0:T(8,128)(2,1)S(1)}, bf16[1,256,8192]{2,1,0:T(8,128)(2,1)}, u32[]{:S(2)}) %copy-start) | copy-done | bytes 4194328
  9.4 0.0 copy-start.2
  9.4 2.2 %copy-done.2 = bf16[4096,512]{1,0:T(8,128)(2,1)S(1)} copy-done((bf16[4096,512]{1,0:T(8,128)(2,1)S(1)}, bf16[4096,512]{1,0:T(8,128)(2,1)}, u32[]{:S(2)}) %copy-start.2) | copy-done | bytes 4194328
  11.6 0.0 copy-start.1
  11.6 2.6 %project_own.1.refs_2_ = f32[256,512]{1,0:T(8,128)S(1)} custom-call(s32[3]{0:T(128)S(1)} %pad_add_fusion.place, bf16[256,8192]{1,0:T(8,128)(2,1)S(1)} %bitcast.24, bf16[4096,512]{1,0:T(8,128)(2,1)S(1)} %copy-done.2), custom_call_target="tpu_custom_call" | custom-call | flops 1073741824 | bytes 6291456 | tf_op jit(solution)/shard_map/project_own/pallas_call | solution.py:67
  14.2 0.0 copy-done.1
  14.2 0.1 dynamic-slice_bitcast_fusion
  14.3 0.2 dynamic-slice_bitcast_fusion.1
  14.6 4.1 %collective-permute-done.refs_1_ = bf16[1024,512]{1,0:T(8,128)(2,1)S(1)} collective-permute-done((bf16[1024,512]{1,0:T(8,128)(2,1)}, bf16[1024,512]{1,0:T(8,128)(2,1)S(1)}, u32[]{:S(2)}, u32[]{:S(2)}) %collective-permute-start) | collective-permute-done | bytes 1048608 | tf_op jit(solution)/shard_map/ppermute | solution.py:39
  18.7 11.1 %collective-permute-done.2.refs_1_ = bf16[1024,512]{1,0:T(8,128)(2,1)S(1)} collective-permute-done((bf16[1024,512]{1,0:T(8,128)(2,1)S(1)}, bf16[1024,512]{1,0:T(8,128)(2,1)S(1)}, u32[]{:S(2)}, u32[]{:S(2)}) %collective-permute-start.2) | collective-permute-done | bytes 1048608 | tf_op jit(solution)/shard_map/ppermute | solution.py:39
  29.8 2.4 %collective-permute-start.3 = (bf16[1024,512]{1,0:T(8,128)(2,1)S(1)}, bf16[1024,512]{1,0:T(8,128)(2,1)S(1)}, u32[]{:S(2)}, u32[]{:S(2)}) collective-permute-start(bf16[1024,512]{1,0:T(8,128)(2,1)S(1)} %collective-permute-done.2.refs_1_), channel_id=1, source_target_pairs={{0,8},{1,9},{2,10},{3,11},{4,12},{5,13},{6,14},{7,15},{8,0},{9,1},... | collective-permute-start | bytes 3145736 | tf_op jit(solution)/shard_map/ppermute | solution.py:39
  32.2 0.0 collective-permute-start.1
  32.2 0.5 collective-permute-start.5
  32.7 1.0 project_add.3.refs_2_
  33.7 1.0 project_add.4.refs_4_
  34.6 0.0 copy-start.3
  34.7 0.0 copy-start.4
  34.7 0.0 copy-start.5
  34.7 0.0 collective-permute-done.3.refs_3_
  34.7 1.3 collective-permute-done.1.refs_2_
  36.0 1.2 project_add.5.key_own
  37.2 3.5 %collective-permute-start.4 = (bf16[256,512]{1,0:T(8,128)(2,1)S(1)}, bf16[256,512]{1,0:T(8,128)(2,1)S(1)}, u32[]{:S(2)}, u32[]{:S(2)}) collective-permute-start(bf16[256,512]{1,0:T(8,128)(2,1)S(1)} %project_add.5.key_own), channel_id=1, source_target_pairs={{0,8},{1,9},{2,10},{3,11},{4,12},{5,13},{6,14},{7,15},{8,16},{9,17... | collective-permute-start | bytes 786440 | tf_op jit(solution)/shard_map/ppermute | solution.py:39
  40.8 0.1 collective-permute-start.6
  40.8 0.3 collective-permute-start.7
  41.2 2.3 %collective-permute-start.8 = (bf16[128,2048]{1,0:T(8,128)(2,1)S(1)}, bf16[128,2048]{1,0:T(8,128)(2,1)S(1)}, u32[]{:S(2)}, u32[]{:S(2)}) collective-permute-start(bf16[128,2048]{1,0:T(8,128)(2,1)S(1)} %get-tuple-element.38), channel_id=1, source_target_pairs={{0,68},{1,69},{2,70},{3,71},{4,0},{5,1},{6,2},{7,3},{8,76},{9,77},... | collective-permute-start | bytes 1572872 | tf_op jit(solution)/shard_map/ppermute | solution.py:39
  43.5 0.5 collective-permute-done.4.key_halo
  44.1 6.3 %collective-permute-start.9 = (bf16[128,2048]{1,0:T(8,128)(2,1)S(1)}, bf16[128,2048]{1,0:T(8,128)(2,1)S(1)}, u32[]{:S(2)}, u32[]{:S(2)}) collective-permute-start(bf16[128,2048]{1,0:T(8,128)(2,1)S(1)} %get-tuple-element.39), channel_id=1, source_target_pairs={{0,76},{1,77},{2,78},{3,79},{4,8},{5,9},{6,10},{7,11},{8,68},{9,69... | collective-permute-start | bytes 1572872 | tf_op jit(solution)/shard_map/ppermute | solution.py:39
  50.4 0.0 copy-done.3
  50.4 0.0 copy-done.4
  50.4 0.0 copy-done.5
  50.4 15.5 %attend.1 = (f32[32,256]{1,0:T(8,128)}, bf16[256,4096]{1,0:T(8,128)(2,1)}, f32[256,512]{1,0:T(8,128)S(1)}, bf16[256,512]{1,0:T(8,128)(2,1)S(1)}) custom-call(s32[3]{0:T(128)S(1)} %pad_add_fusion.place, s32[1,32]{1,0:T(1,128)S(1)} %copy-done.5, bf16[256,4096]{1,0:T(8,128)(2,1)S(1)} %bitcast.33, bf16[256,512]{1,0:T(8,128)(2,1)S(1)} %project_add.5.key_own, ...), custom_call_target="tpu_custom_call" | custom-call | flops 4294967296 | bytes 6291456 | tf_op jit(solution)/shard_map/attend/pallas_call | solution.py:190
  65.9 0.0 collective-permute-done.6.refs_2_
  65.9 0.1 collective-permute-done.7.refs_3_
  66.0 0.0 collective-permute-done.8.refs_4_
  66.0 0.4 collective-permute-done.9.refs_5_
  66.3 0.0 collective-permute-done.5.refs_1_
  66.3 2.5 %collective-permute-start.10 = (bf16[256,512]{1,0:T(8,128)(2,1)S(1)}, bf16[256,512]{1,0:T(8,128)(2,1)S(1)}, u32[]{:S(2)}, u32[]{:S(2)}) collective-permute-start(bf16[256,512]{1,0:T(8,128)(2,1)S(1)} %get-tuple-element.46), channel_id=1, source_target_pairs={{8,0},{9,1},{10,2},{11,3},{12,4},{13,5},{14,6},{15,7},{16,8},{17,9... | collective-permute-start | bytes 786440 | tf_op jit(solution)/shard_map/ppermute | solution.py:39
  68.9 5.3 %collective-permute-done.10 = bf16[256,512]{1,0:T(8,128)(2,1)S(1)} collective-permute-done((bf16[256,512]{1,0:T(8,128)(2,1)S(1)}, bf16[256,512]{1,0:T(8,128)(2,1)S(1)}, u32[]{:S(2)}, u32[]{:S(2)}) %collective-permute-start.10) | collective-permute-done | bytes 262176 | tf_op jit(solution)/shard_map/ppermute | solution.py:39
  74.2 0.1 add_convert_fusion.refs_6_
  74.3 0.1 collective-permute-start.11
  74.4 4.0 %collective-permute-start.15 = (bf16[128,512]{1,0:T(8,128)(2,1)S(1)}, bf16[128,512]{1,0:T(8,128)(2,1)S(1)}, u32[]{:S(2)}, u32[]{:S(2)}) collective-permute-start(bf16[128,512]{1,0:T(8,128)(2,1)S(1)} %get-tuple-element.53), channel_id=1, source_target_pairs={{0,76},{1,77},{2,78},{3,79},{4,8},{5,9},{6,10},{7,11},{8,68},{9,69... | collective-permute-start | bytes 393224 | tf_op jit(solution)/shard_map/ppermute | solution.py:39
  78.4 0.8 collective-permute-start.14
  79.3 1.3 collective-permute-start.13
  80.6 0.0 collective-permute-start.12
  80.6 0.6 collective-permute-done.15.refs_11_
  81.1 2.8 %collective-permute-done.14.refs_10_ = bf16[128,512]{1,0:T(8,128)(2,1)S(1)} collective-permute-done((bf16[128,512]{1,0:T(8,128)(2,1)S(1)}, bf16[128,512]{1,0:T(8,128)(2,1)S(1)}, u32[]{:S(2)}, u32[]{:S(2)}) %collective-permute-start.14) | collective-permute-done | bytes 131104 | tf_op jit(solution)/shard_map/ppermute | solution.py:39
  83.9 2.5 %collective-permute-done.13.refs_9_ = bf16[128,512]{1,0:T(8,128)(2,1)S(1)} collective-permute-done((bf16[128,512]{1,0:T(8,128)(2,1)S(1)}, bf16[128,512]{1,0:T(8,128)(2,1)S(1)}, u32[]{:S(2)}, u32[]{:S(2)}) %collective-permute-start.13) | collective-permute-done | bytes 131104 | tf_op jit(solution)/shard_map/ppermute | solution.py:39
  86.5 2.8 %collective-permute-done.12.refs_8_ = bf16[128,512]{1,0:T(8,128)(2,1)S(1)} collective-permute-done((bf16[128,512]{1,0:T(8,128)(2,1)S(1)}, bf16[128,512]{1,0:T(8,128)(2,1)S(1)}, u32[]{:S(2)}, u32[]{:S(2)}) %collective-permute-start.12) | collective-permute-done | bytes 131104 | tf_op jit(solution)/shard_map/ppermute | solution.py:39
  89.3 0.0 collective-permute-done.11.refs_7_
  89.3 6.1 %weight_grad.1 = bf16[2048,512]{1,0:T(8,128)(2,1)S(1)} custom-call(s32[3]{0:T(128)S(1)} %pad_add_fusion.place, bf16[256,8192]{1,0:T(8,128)(2,1)S(1)} %bitcast.29, bf16[256,2048]{1,0:T(8,128)(2,1)S(1)} %collective-permute-done.5.refs_1_, bf16[128,2048]{1,0:T(8,128)(2,1)S(1)} %collective-permute-done.6.refs_2_, ...), custom_call_target="tpu_custom_call" | custom-call | flops 2147483648 | bytes 8388608 | tf_op jit(solution)/shard_map/weight_grad/pallas_call | solution.py:238
  95.4 36.2 %all_to_all.10.parts = bf16[32,64,512]{2,1,0:T(8,128)(2,1)S(1)} all-to-all(bf16[32,64,512]{2,1,0:T(8,128)(2,1)S(1)} %bitcast.30), channel_id=1, replica_groups=mesh['xh'=2,'y'=4,'core'=2,'xl'=2,'z'=4] {'xh','y','z'}, dimensions={0} | all-to-all | bytes 4194304 | tf_op jit(solution)/shard_map/all_to_all | solution.py:384
  131.6 0.8 sum_spread.1
  132.4 32.3 %all_to_all.11 = bf16[32,64,512]{2,1,0:T(8,128)(2,1)S(1)} all-to-all(bf16[32,64,512]{2,1,0:T(8,128)(2,1)S(1)} %sum_spread.1), channel_id=1, replica_groups=mesh['xh'=2,'y'=4,'core'=2,'xl'=2,'z'=4] {'xh','y','z'}, dimensions={0} | all-to-all | bytes 4194304 | tf_op jit(solution)/shard_map/all_to_all | solution.py:386
  164.8 3.5 %collective-permute-start.16 = (bf16[2048,512]{1,0:T(8,128)(2,1)S(1)}, bf16[2048,512]{1,0:T(8,128)(2,1)S(1)}, u32[]{:S(2)}, u32[]{:S(2)}) collective-permute-start(bf16[2048,512]{1,0:T(8,128)(2,1)S(1)} %bitcast.31), channel_id=1, source_target_pairs={{0,8},{1,9},{2,10},{3,11},{4,12},{5,13},{6,14},{7,15},{8,0},{9,1},... | collective-permute-start | bytes 6291464 | tf_op jit(solution)/shard_map/ppermute | solution.py:39
  168.2 3.8 %collective-permute-done.16.other = bf16[2048,512]{1,0:T(8,128)(2,1)S(1)} collective-permute-done((bf16[2048,512]{1,0:T(8,128)(2,1)S(1)}, bf16[2048,512]{1,0:T(8,128)(2,1)S(1)}, u32[]{:S(2)}, u32[]{:S(2)}) %collective-permute-start.16) | collective-permute-done | bytes 2097184 | tf_op jit(solution)/shard_map/ppermute | solution.py:39
  172.0 3.0 %join_cores.1 = bf16[4096,512]{1,0:T(8,128)(2,1)} custom-call(s32[3]{0:T(128)S(1)} %pad_add_fusion.place, bf16[2048,512]{1,0:T(8,128)(2,1)S(1)} %bitcast.32, bf16[2048,512]{1,0:T(8,128)(2,1)S(1)} %collective-permute-done.16.other), custom_call_target="tpu_custom_call" | custom-call | flops 1048576 | bytes 8388608 | tf_op jit(solution)/shard_map/join_cores/pallas_call | solution.py:302
  (1 shorter events, 0.0 us)
Async XLA Ops:
  3.3 15.4 %collective-permute-start = (bf16[1024,512]{1,0:T(8,128)(2,1)}, bf16[1024,512]{1,0:T(8,128)(2,1)S(1)}, u32[]{:S(2)}, u32[]{:S(2)}) collective-permute-start(bf16[1024,512]{1,0:T(8,128)(2,1)} %get-tuple-element.48), channel_id=1, source_target_pairs={{0,4},{1,5},{2,6},{3,7},{4,64},{5,65},{6,66},{7,67},{8,76},{9,77},... | collective-permute-start | bytes 3145736 | tf_op jit(solution)/shard_map/ppermute | solution.py:39
  6.6 23.2 %collective-permute-start.2 = (bf16[1024,512]{1,0:T(8,128)(2,1)S(1)}, bf16[1024,512]{1,0:T(8,128)(2,1)S(1)}, u32[]{:S(2)}, u32[]{:S(2)}) collective-permute-start(bf16[1024,512]{1,0:T(8,128)(2,1)S(1)} %get-tuple-element.47), channel_id=1, source_target_pairs={{0,4},{1,5},{2,6},{3,7},{4,64},{5,65},{6,66},{7,67},{8,76},{9,77},... | collective-permute-start | bytes 3145736 | tf_op jit(solution)/shard_map/ppermute | solution.py:39
  7.2 2.2 %copy-start = (bf16[1,256,8192]{2,1,0:T(8,128)(2,1)S(1)}, bf16[1,256,8192]{2,1,0:T(8,128)(2,1)}, u32[]{:S(2)}) copy-start(bf16[1,256,8192]{2,1,0:T(8,128)(2,1)} %param.6) | copy-start | bytes 12582916
  9.4 2.2 %copy-start.2 = (bf16[4096,512]{1,0:T(8,128)(2,1)S(1)}, bf16[4096,512]{1,0:T(8,128)(2,1)}, u32[]{:S(2)}) copy-start(bf16[4096,512]{1,0:T(8,128)(2,1)} %weight.1) | copy-start | bytes 12582916
  11.6 2.6 %copy-start.1 = (bf16[1,256,8192]{2,1,0:T(8,128)(2,1)S(1)}, bf16[1,256,8192]{2,1,0:T(8,128)(2,1)}, u32[]{:S(2)}) copy-start(bf16[1,256,8192]{2,1,0:T(8,128)(2,1)} %param.6) | copy-start | bytes 12582916
  29.8 4.9 %collective-permute-start.3 = (bf16[1024,512]{1,0:T(8,128)(2,1)S(1)}, bf16[1024,512]{1,0:T(8,128)(2,1)S(1)}, u32[]{:S(2)}, u32[]{:S(2)}) collective-permute-start(bf16[1024,512]{1,0:T(8,128)(2,1)S(1)} %collective-permute-done.2.refs_1_), channel_id=1, source_target_pairs={{0,8},{1,9},{2,10},{3,11},{4,12},{5,13},{6,14},{7,15},{8,0},{9,1},... | collective-permute-start | bytes 3145736 | tf_op jit(solution)/shard_map/ppermute | solution.py:39
  32.2 3.8 %collective-permute-start.1 = (bf16[1024,512]{1,0:T(8,128)(2,1)S(1)}, bf16[1024,512]{1,0:T(8,128)(2,1)S(1)}, u32[]{:S(2)}, u32[]{:S(2)}) collective-permute-start(bf16[1024,512]{1,0:T(8,128)(2,1)S(1)} %collective-permute-done.refs_1_), channel_id=1, source_target_pairs={{0,8},{1,9},{2,10},{3,11},{4,12},{5,13},{6,14},{7,15},{8,0},{9,1},... | collective-permute-start | bytes 3145736 | tf_op jit(solution)/shard_map/ppermute | solution.py:39
  32.2 34.2 %collective-permute-start.5 = (bf16[256,2048]{1,0:T(8,128)(2,1)S(1)}, bf16[256,2048]{1,0:T(8,128)(2,1)S(1)}, u32[]{:S(2)}, u32[]{:S(2)}) collective-permute-start(bf16[256,2048]{1,0:T(8,128)(2,1)S(1)} %dynamic-slice_bitcast_fusion), channel_id=1, source_target_pairs={{0,8},{1,9},{2,10},{3,11},{4,12},{5,13},{6,14},{7,15},{8,0},{9,1},... | collective-permute-start | bytes 3145736 | tf_op jit(solution)/shard_map/ppermute | solution.py:39
  34.6 15.7 %copy-start.3 = (bf16[1,256,4096]{2,1,0:T(8,128)(2,1)S(1)}, bf16[1,256,4096]{2,1,0:T(8,128)(2,1)}, u32[]{:S(2)}) copy-start(bf16[1,256,4096]{2,1,0:T(8,128)(2,1)} %param.5) | copy-start | bytes 6291460
  34.7 15.7 %copy-start.4 = (bf16[1,256,32]{1,2,0:T(8,128)(2,1)S(1)}, bf16[1,256,32]{1,2,0:T(8,128)(2,1)}, u32[]{:S(2)}) copy-start(bf16[1,256,32]{1,2,0:T(8,128)(2,1)} %param.9) | copy-start | bytes 49156
  34.7 15.7 %copy-start.5 = (s32[1,32]{1,0:T(1,128)S(1)}, s32[1,32]{1,0:T(1,128)}, u32[]{:S(2)}) copy-start(s32[1,32]{1,0:T(1,128)} %lengths.1) | copy-start | bytes 388
  37.2 6.8 %collective-permute-start.4 = (bf16[256,512]{1,0:T(8,128)(2,1)S(1)}, bf16[256,512]{1,0:T(8,128)(2,1)S(1)}, u32[]{:S(2)}, u32[]{:S(2)}) collective-permute-start(bf16[256,512]{1,0:T(8,128)(2,1)S(1)} %project_add.5.key_own), channel_id=1, source_target_pairs={{0,8},{1,9},{2,10},{3,11},{4,12},{5,13},{6,14},{7,15},{8,16},{9,17... | collective-permute-start | bytes 786440 | tf_op jit(solution)/shard_map/ppermute | solution.py:39
  40.8 25.1 %collective-permute-start.6 = (bf16[128,2048]{1,0:T(8,128)(2,1)S(1)}, bf16[128,2048]{1,0:T(8,128)(2,1)S(1)}, u32[]{:S(2)}, u32[]{:S(2)}) collective-permute-start(bf16[128,2048]{1,0:T(8,128)(2,1)S(1)} %get-tuple-element.36), channel_id=1, source_target_pairs={{0,4},{1,5},{2,6},{3,7},{4,64},{5,65},{6,66},{7,67},{8,12},{9,13},... | collective-permute-start | bytes 1572872 | tf_op jit(solution)/shard_map/ppermute | solution.py:39
  40.8 25.1 %collective-permute-start.7 = (bf16[128,2048]{1,0:T(8,128)(2,1)S(1)}, bf16[128,2048]{1,0:T(8,128)(2,1)S(1)}, u32[]{:S(2)}, u32[]{:S(2)}) collective-permute-start(bf16[128,2048]{1,0:T(8,128)(2,1)S(1)} %get-tuple-element.37), channel_id=1, source_target_pairs={{0,12},{1,13},{2,14},{3,15},{4,72},{5,73},{6,74},{7,75},{8,4},{9,5... | collective-permute-start | bytes 1572872 | tf_op jit(solution)/shard_map/ppermute | solution.py:39
  41.2 24.8 %collective-permute-start.8 = (bf16[128,2048]{1,0:T(8,128)(2,1)S(1)}, bf16[128,2048]{1,0:T(8,128)(2,1)S(1)}, u32[]{:S(2)}, u32[]{:S(2)}) collective-permute-start(bf16[128,2048]{1,0:T(8,128)(2,1)S(1)} %get-tuple-element.38), channel_id=1, source_target_pairs={{0,68},{1,69},{2,70},{3,71},{4,0},{5,1},{6,2},{7,3},{8,76},{9,77},... | collective-permute-start | bytes 1572872 | tf_op jit(solution)/shard_map/ppermute | solution.py:39
  44.1 22.3 %collective-permute-start.9 = (bf16[128,2048]{1,0:T(8,128)(2,1)S(1)}, bf16[128,2048]{1,0:T(8,128)(2,1)S(1)}, u32[]{:S(2)}, u32[]{:S(2)}) collective-permute-start(bf16[128,2048]{1,0:T(8,128)(2,1)S(1)} %get-tuple-element.39), channel_id=1, source_target_pairs={{0,76},{1,77},{2,78},{3,79},{4,8},{5,9},{6,10},{7,11},{8,68},{9,69... | collective-permute-start | bytes 1572872 | tf_op jit(solution)/shard_map/ppermute | solution.py:39
  66.3 7.8 %collective-permute-start.10 = (bf16[256,512]{1,0:T(8,128)(2,1)S(1)}, bf16[256,512]{1,0:T(8,128)(2,1)S(1)}, u32[]{:S(2)}, u32[]{:S(2)}) collective-permute-start(bf16[256,512]{1,0:T(8,128)(2,1)S(1)} %get-tuple-element.46), channel_id=1, source_target_pairs={{8,0},{9,1},{10,2},{11,3},{12,4},{13,5},{14,6},{15,7},{16,8},{17,9... | collective-permute-start | bytes 786440 | tf_op jit(solution)/shard_map/ppermute | solution.py:39
  74.3 15.0 %collective-permute-start.11 = (bf16[256,512]{1,0:T(8,128)(2,1)S(1)}, bf16[256,512]{1,0:T(8,128)(2,1)S(1)}, u32[]{:S(2)}, u32[]{:S(2)}) collective-permute-start(bf16[256,512]{1,0:T(8,128)(2,1)S(1)} %add_convert_fusion.refs_6_), channel_id=1, source_target_pairs={{0,8},{1,9},{2,10},{3,11},{4,12},{5,13},{6,14},{7,15},{8,0},{9,1},... | collective-permute-start | bytes 786440 | tf_op jit(solution)/shard_map/ppermute | solution.py:39
  74.4 6.7 %collective-permute-start.15 = (bf16[128,512]{1,0:T(8,128)(2,1)S(1)}, bf16[128,512]{1,0:T(8,128)(2,1)S(1)}, u32[]{:S(2)}, u32[]{:S(2)}) collective-permute-start(bf16[128,512]{1,0:T(8,128)(2,1)S(1)} %get-tuple-element.53), channel_id=1, source_target_pairs={{0,76},{1,77},{2,78},{3,79},{4,8},{5,9},{6,10},{7,11},{8,68},{9,69... | collective-permute-start | bytes 393224 | tf_op jit(solution)/shard_map/ppermute | solution.py:39
  78.4 5.5 %collective-permute-start.14 = (bf16[128,512]{1,0:T(8,128)(2,1)S(1)}, bf16[128,512]{1,0:T(8,128)(2,1)S(1)}, u32[]{:S(2)}, u32[]{:S(2)}) collective-permute-start(bf16[128,512]{1,0:T(8,128)(2,1)S(1)} %get-tuple-element.53), channel_id=1, source_target_pairs={{0,68},{1,69},{2,70},{3,71},{4,0},{5,1},{6,2},{7,3},{8,76},{9,77},... | collective-permute-start | bytes 393224 | tf_op jit(solution)/shard_map/ppermute | solution.py:39
  79.3 7.2 %collective-permute-start.13 = (bf16[128,512]{1,0:T(8,128)(2,1)S(1)}, bf16[128,512]{1,0:T(8,128)(2,1)S(1)}, u32[]{:S(2)}, u32[]{:S(2)}) collective-permute-start(bf16[128,512]{1,0:T(8,128)(2,1)S(1)} %get-tuple-element.54), channel_id=1, source_target_pairs={{0,12},{1,13},{2,14},{3,15},{4,72},{5,73},{6,74},{7,75},{8,4},{9,5... | collective-permute-start | bytes 393224 | tf_op jit(solution)/shard_map/ppermute | solution.py:39
  80.6 8.7 %collective-permute-start.12 = (bf16[128,512]{1,0:T(8,128)(2,1)S(1)}, bf16[128,512]{1,0:T(8,128)(2,1)S(1)}, u32[]{:S(2)}, u32[]{:S(2)}) collective-permute-start(bf16[128,512]{1,0:T(8,128)(2,1)S(1)} %get-tuple-element.54), channel_id=1, source_target_pairs={{0,4},{1,5},{2,6},{3,7},{4,64},{5,65},{6,66},{7,67},{8,12},{9,13},... | collective-permute-start | bytes 393224 | tf_op jit(solution)/shard_map/ppermute | solution.py:39
  164.8 7.2 %collective-permute-start.16 = (bf16[2048,512]{1,0:T(8,128)(2,1)S(1)}, bf16[2048,512]{1,0:T(8,128)(2,1)S(1)}, u32[]{:S(2)}, u32[]{:S(2)}) collective-permute-start(bf16[2048,512]{1,0:T(8,128)(2,1)S(1)} %bitcast.31), channel_id=1, source_target_pairs={{0,8},{1,9},{2,10},{3,11},{4,12},{5,13},{6,14},{7,15},{8,0},{9,1},... | collective-permute-start | bytes 6291464 | tf_op jit(solution)/shard_map/ppermute | solution.py:39

commit v3 on v2

--- a/solution.py
+++ b/solution.py
@@ -82,40 +82,44 @@
     )(place, tokens, weight)
 
 
-def add_kernel(count, place, *refs):
-    hidden, weights, total, out = refs[:count], refs[count:2 * count], refs[2 * count], refs[2 * count + 1]
-    acc = total[...]
-    for h, w in zip(hidden, weights):
-        acc = acc + jnp.dot(h[...], w[...], preferred_element_type=F32)
-    out[...] = acc.astype(out.dtype)
-
-
-def project_add(place, tokens, weights, which, total, dtype):
-    rows, model = tokens.shape
-    step, width = weights[0].shape
-
-    def block(other, chunk):
-        def index(i, p):
-            return (0, (1 - p[0]) * 4 + ((1 - p[1]) if other else p[1]) * 2 + chunk)
-
-        return index
-
-    whole = lambda i, p: (0, 0)
-    return pl.pallas_call(
-        functools.partial(add_kernel, len(weights)),
-        grid_spec=pltpu.PrefetchScalarGridSpec(
-            num_scalar_prefetch=1,
-            grid=(1,),
-            in_specs=[pl.BlockSpec((rows, step), block(*w)) for w in which]
-            + [pl.BlockSpec((step, width), whole) for _ in which]
-            + [pl.BlockSpec((rows, width), whole)],
-            out_specs=pl.BlockSpec((rows, width), whole),
-        ),
-        out_shape=jax.ShapeDtypeStruct((rows, width), dtype),
+def near_kernel(low, high, weight, low_out, high_out, total):
+    rows = jnp.concatenate([low[...], high[...]], axis=0)
+    part = jnp.dot(rows, weight[...], preferred_element_type=F32)
+
+    @pl.when(pl.program_id(0) == 0)
+    def _():
+        total[...] = part
+
+    @pl.when(pl.program_id(0) > 0)
+    def _():
+        total[...] += part
+
+    @pl.when(pl.program_id(0) == pl.num_programs(0) - 1)
+    def _():
+        count = low.shape[0]
+        low_out[...] = total[:count]
+        high_out[...] = total[count:]
+
+
+def project_near(low, high, weight):
+    rows = low.shape[0]
+    half, width = weight.shape
+    step = half // 4
+    return pl.pallas_call(
+        near_kernel,
+        grid=(4,),
+        in_specs=[
+            pl.BlockSpec((rows, step), lambda i: (0, i)),
+            pl.BlockSpec((rows, step), lambda i: (0, i)),
+            pl.BlockSpec((step, width), lambda i: (i, 0)),
+        ],
+        out_specs=[pl.BlockSpec((rows, width), lambda i: (0, 0))] * 2,
+        out_shape=[jax.ShapeDtypeStruct((rows, width), F32)] * 2,
+        scratch_shapes=[pltpu.VMEM((2 * rows, width), F32)],
         compiler_params=params(12),
-        cost_estimate=cost(2 * len(weights) * rows * step * width, 2 << 20),
-        name="project_add",
-    )(place, *([tokens] * len(weights)), *weights, total)
+        cost_estimate=cost(4 * rows * half * width, 6 << 20),
+        name="project_near",
+    )(low, high, weight)
 
 
 def attend_kernel(place, lengths, query, key_own, key_halo, weight, entropy, grad_query, grad_own,
@@ -222,26 +226,24 @@
     )(place, lengths, queries, key_own, key_halo, weight)
 
 
-def weight_grad_kernel(place, *refs):
-    hidden, grads, out = refs[0:6], refs[6:12], refs[12]
-    total = None
-    for piece, grad in zip(hidden, grads):
-        part = lax.dot_general(
-            piece[...], grad[...], (((0,), (0,)), ((), ())), preferred_element_type=F32
-        )
-        total = part if total is None else total + part
+def weight_grad_kernel(count, place, *refs):
+    hidden, grads, out = refs[:count], refs[count:-1], refs[-1]
+    rows = jnp.concatenate([piece[...] for piece in hidden], axis=0)
+    grad = jnp.concatenate([piece[...] for piece in grads], axis=0)
+    total = lax.dot_general(rows, grad, (((0,), (0,)), ((), ())), preferred_element_type=F32)
     out[...] = total.astype(BF)
 
 
-def weight_grad(place, tokens, pieces, grads):
+def weight_grad(place, tokens, near, swapped, grads):
     whole = lambda i, p: (0, 0)
     return pl.pallas_call(
-        weight_grad_kernel,
+        functools.partial(weight_grad_kernel, 1 + len(near) + len(swapped)),
         grid_spec=pltpu.PrefetchScalarGridSpec(
             num_scalar_prefetch=1,
             grid=(8,),
             in_specs=[pl.BlockSpec((256, 256), lambda i, p: (0, (p[0] * 2 + p[1]) * 8 + i))]
-            + [pl.BlockSpec((v.shape[0], 256), lambda i, p: (0, i)) for v in pieces]
+            + [pl.BlockSpec((v.shape[0], 256), lambda i, p: (0, p[1] * 8 + i)) for v in near]
+            + [pl.BlockSpec((v.shape[0], 256), lambda i, p: (0, i)) for v in swapped]
             + [pl.BlockSpec(v.shape, whole) for v in grads],
             out_specs=pl.BlockSpec((256, 512), lambda i, p: (i, 0)),
         ),
@@ -249,7 +251,7 @@
         compiler_params=params(16),
         cost_estimate=cost(2 * 1024 * 2048 * 512, 8 << 20),
         name="weight_grad",
-    )(place, tokens, *pieces, *grads)
+    )(place, tokens, *near, *swapped, *grads)
 
 
 def sum_spread_kernel(scale, parts, out):
@@ -276,42 +278,31 @@
     )(parts)
 
 
-def join_kernel(place, mine, other, out):
-    first = pl.program_id(0) < 2
-    own = first == (place[1] == 0)
-
-    @pl.when(own)
-    def _():
-        out[...] = mine[...]
-
-    @pl.when(jnp.logical_not(own))
-    def _():
-        out[...] = other[...]
-
-
-def join_cores(place, mine, other):
-    rows, width = mine.shape
-    step = rows // 2
-
-    def mine_block(i, p):
-        return (jnp.where((i < 2) == (p[1] == 0), i % 2, jnp.where(i < 2, 0, 1)), 0)
-
-    def other_block(i, p):
-        return (jnp.where((i < 2) == (p[1] == 0), jnp.where(i < 2, 0, 1), i % 2), 0)
-
-    return pl.pallas_call(
-        join_kernel,
+def copy_kernel(place, rows, *refs):
+    refs[-1][...] = rows[...]
+
+
+def write_rows(place, rows, side, held=None):
+    count, width = rows.shape
+    step = count // 2
+    more = {} if held is None else {"input_output_aliases": {2: 0}}
+    return pl.pallas_call(
+        copy_kernel,
         grid_spec=pltpu.PrefetchScalarGridSpec(
             num_scalar_prefetch=1,
-            grid=(4,),
-            in_specs=[pl.BlockSpec((step, width), mine_block), pl.BlockSpec((step, width), other_block)],
-            out_specs=pl.BlockSpec((step, width), lambda i, p: (i, 0)),
-        ),
-        out_shape=jax.ShapeDtypeStruct((2 * rows, width), BF),
-        compiler_params=params(10),
-        cost_estimate=cost(1 << 20, 8 << 20),
-        name="join_cores",
-    )(place, mine, other)
+            grid=(2,),
+            in_specs=[pl.BlockSpec((step, width), lambda i, p: (i, 0))]
+            + ([] if held is None else [pl.BlockSpec(memory_space=pl.ANY)]),
+            out_specs=pl.BlockSpec(
+                (step, width), lambda i, p: ((1 - p[1] if side else p[1]) * 2 + i, 0)
+            ),
+        ),
+        out_shape=jax.ShapeDtypeStruct((2 * count, width), BF),
+        compiler_params=params(8),
+        cost_estimate=cost(1 << 20, 4 << 20),
+        name="write_rows",
+        **more,
+    )(place, rows, *([] if held is None else [held]))
 
 
 def swap_core(xh, y, core, xl, z):
@@ -336,56 +327,47 @@
     seq = lax.axis_index(("xh", "y", "core"))
     place = jnp.stack([fsdp, core, seq]).astype(jnp.int32)
 
-    mine = lax.dynamic_slice_in_dim(key_weight, core * (half // 2), half // 2, 0)
-    fetch = lambda xh, y, core, xl, z: along_x(xh, y, core, xl, z, 1 - 2 * core)
-    got = [move(mine[k * half // 4:(k + 1) * half // 4], fetch) for k in range(2)]
+    quarter = model // 4
+    split = rows // 2
+    forward, backward = (functools.partial(along_x, step=step) for step in (1, -1))
+
+    def column(first, last, start, count):
+        return lax.dynamic_slice(tokens, (first, start), (last - first, count))
+
+    near = [
+        move(column(0, split, (1 - fsdp) * half, half), forward),
+        move(column(split, rows, (1 - fsdp) * half, half), backward),
+    ]
+    passed = [column(0, rows, fsdp * half + (1 - core) * quarter, quarter)]
     total = project_own(place, tokens, key_weight)
-
-    quarter = model // 4
-
-    def column(first, last, is_fsdp, is_core):
-        start = (is_fsdp * 2 + is_core) * quarter
-        return lax.dynamic_slice(tokens, (first, start), (last - first, quarter))
-
-    split = rows // 2
-    routes = [swap_core]
-    for step in (1, -1):
-        for other in (0, 1):
-            routes.append(functools.partial(along_x, step=step, other=other))
-    columns = [column(0, rows, fsdp, 1 - core)]
-    for k, route in enumerate(routes[1:]):
-        first = 0 if k < 2 else split
-        columns.append(column(first, first + split, 1 - fsdp, core if k % 2 == 0 else 1 - core))
-
-    got[0], total, columns = lax.optimization_barrier((got[0], total, columns))
-    swapped = [move(v, swap_core) for v in got]
-    total = project_add(place, tokens, got[:1], [(False, 0)], total, F32)
-    total = project_add(place, tokens, got[1:], [(False, 1)], total, F32)
-    key_own = project_add(place, tokens, swapped, [(True, 0), (True, 1)], total, BF)
+    near, total, passed = lax.optimization_barrier((near, total, passed))
+    low, high = project_near(*near, key_weight)
+    low, high = move(low, backward), move(high, forward)
+    key_own = (total + jnp.concatenate([low, high], axis=0)).astype(BF)
     key_halo = move(key_own, next_rows(1))
 
-    columns, _ = lax.optimization_barrier((columns, got[1]))
-    pieces = [move(v, route) for v, route in zip(columns, routes)]
+    start = (1 - core) * quarter
+    passed += [lax.dynamic_slice(v, (0, start), (split, quarter)) for v in near]
+    across = [move(v, swap_core) for v in passed]
 
     entropy, grad_query, grad_own, grad_halo = attend(
         place, doc_lengths, queries[0], key_own, key_halo, entropy_cot[0].T
     )
 
-    grad_halo, pieces = lax.optimization_barrier((grad_halo, pieces))
+    grad_halo, across = lax.optimization_barrier((grad_halo, across))
     from_next = move(grad_halo, next_rows(-1))
     key_grad = (grad_own + from_next.astype(F32)).astype(BF)
-    grads = [key_grad, move(key_grad, routes[0])]
-    for k, route in enumerate(routes[1:]):
-        first = 0 if k < 2 else split
-        grads.append(move(key_grad[first:first + split], route))
+    grad_near = [move(key_grad[:split], forward), move(key_grad[split:], backward)]
+    grads = [key_grad, *grad_near, move(key_grad, swap_core)]
+    grads += [move(v, swap_core) for v in grad_near]
 
     chips = ("xh", "y", "z")
-    parts = weight_grad(place, tokens, pieces, grads).reshape(32, 64, width)
+    parts = weight_grad(place, tokens, near, across, grads).reshape(32, 64, width)
     parts = lax.all_to_all(parts, chips, split_axis=0, concat_axis=0, tiled=True)
     spread = sum_spread(parts, (rows * 16 * 8) ** (-0.5))
     final = lax.all_to_all(spread, chips, split_axis=0, concat_axis=0, tiled=True).reshape(2048, width)
     other = move(final, swap_core)
-    grad_weight = join_cores(place, final, other)
+    grad_weight = write_rows(place, other, 1, write_rows(place, final, 0))
     return entropy.T[None], grad_query[None], grad_weight
 
 

time: 175 us -> 170 us (0.971)
  starting transfers between devices: 31.6 us -> 23.4 us
  local copies, waits for them, and re-layouts: 7.43 us -> 9.93 us
    ppermute x17 -> x15, starting transfers between devices: 31.6 us -> 23.4 us  [move(): return lax.ppermute(value, AXES, pairs)]
    dynamic_slice x2 -> x4, local copies, waits for them, and re-layouts: 0.36 us -> 5.51 us  [the longest x2 5.43 us: column(): return lax.dynamic_slice(tokens, (first, start), (last - first, count))]
    slice x2 -> x1, local copies, waits for them, and re-layouts: 2.67 us -> 0.02 us  [shards(): key_grad[split:]]
    ppermute x17 -> x15, waiting for transfers between devices: 35.3 us -> 36.4 us  [move(): return lax.ppermute(value, AXES, pairs)]
    pallas_call x5 -> x4, Pallas kernels: 12.3 us -> 11.3 us  [the longest x1 5.25 us: weight_grad(): pl.pallas_call(functools.partial(weight_grad_kernel, 1 + len(near) + len(...]
    unnamed x12 -> x14, local copies, waits for them, and re-layouts: 4.4 us -> 4.4 us
  transfers between devices with their start and end apart: 17 -> 15, of which waited for: 12 -> 10; matrix products, arithmetic and copies ran while one was open for 0% -> 2% of each run, Pallas kernels for 12% -> 12%
where the time goes in v3:
time: 170 us
  blocking collectives  68.1 us (40%)
  waiting for transfers between devices  36.4 us (21%)
  Pallas kernels  30.2 us (18%)
  starting transfers between devices  23.4 us (14%)
  local copies, waits for them, and re-layouts  9.93 us (6%)
    ppermute x15, waiting for transfers between devices, move(): return lax.ppermute(value, AXES, pairs)  36.4 us
    all_to_all x1, blocking collectives, shards(): lax.all_to_all(parts, chips, split_axis=0, concat_axis=0, tiled=True)  36 us
    all_to_all x1, blocking collectives, shards(): lax.all_to_all(spread, chips, split_axis=0, concat_axis=0, tiled=True)  32.1 us
    ppermute x15, starting transfers between devices, move(): return lax.ppermute(value, AXES, pairs)  23.4 us
    pallas_call x1, Pallas kernels, attend(): pl.pallas_call(attend_kernel, grid_spec=pltpu.PrefetchScalarGridSpec(num_...  15.5 us
    dynamic_slice x2, local copies, waits for them, and re-layouts, column(): return lax.dynamic_slice(tokens, (first, start), (last - first, count))  5.43 us
    pallas_call x1, Pallas kernels, weight_grad(): pl.pallas_call(functools.partial(weight_grad_kernel, 1 + len(near) + len(...  5.25 us
    unnamed x14, local copies, waits for them, and re-layouts  4.4 us
  transfers between devices with their start and end apart: 15, of which 10 were waited for; matrix products, arithmetic and copies ran while one was open for 2% of the time, Pallas kernels for 12%

profile of v3, /device:TPU:1, one launch (start us, length us, event | category | flops | bytes accessed | tf_op | source)
XLA Modules:
  0.0 170.0 jit_solution(8229257676129694077)
XLA Ops:
  0.6 3.1 %dynamic-slice_bitcast_fusion.1 = (bf16[128,4096]{1,0:T(8,128)(2,1)}, bf16[128,4096]{1,0:T(8,128)(2,1)}) fusion(bf16[1,256,8192]{2,1,0:T(8,128)(2,1)} %param.6, s32[]{:T(128)S(6)} %select_n.11), kind=kLoop, calls=%fused_computation.1 | loop fusion | bytes 4194308 | tf_op jit(solution)/shard_map/dynamic_slice | solution.py:335
  3.7 3.3 %collective-permute-start.1 = (bf16[128,4096]{1,0:T(8,128)(2,1)}, bf16[128,4096]{1,0:T(8,128)(2,1)S(1)}, u32[]{:S(2)}, u32[]{:S(2)}) collective-permute-start(bf16[128,4096]{1,0:T(8,128)(2,1)} %get-tuple-element.31), channel_id=1, source_target_pairs={{0,68},{1,69},{2,70},{3,71},{4,0},{5,1},{6,2},{7,3},{8,76},{9,77},... | collective-permute-start | bytes 3145736 | tf_op jit(solution)/shard_map/ppermute | solution.py:39
  7.0 0.0 collective-permute-start
  7.0 0.1 pad_add_fusion.place
  7.1 0.0 copy-start
  7.1 2.2 %copy-done = bf16[1,256,8192]{2,1,0:T(8,128)(2,1)S(1)} copy-done((bf16[1,256,8192]{2,1,0:T(8,128)(2,1)S(1)}, bf16[1,256,8192]{2,1,0:T(8,128)(2,1)}, u32[]{:S(2)}) %copy-start) | copy-done | bytes 4194328
  9.3 0.0 copy-start.2
  9.3 2.2 %copy-done.2 = bf16[4096,512]{1,0:T(8,128)(2,1)S(1)} copy-done((bf16[4096,512]{1,0:T(8,128)(2,1)S(1)}, bf16[4096,512]{1,0:T(8,128)(2,1)}, u32[]{:S(2)}) %copy-start.2) | copy-done | bytes 4194328
  11.5 0.0 copy-start.3
  11.5 2.6 %project_own.1 = f32[256,512]{1,0:T(8,128)S(1)} custom-call(s32[3]{0:T(128)S(1)} %pad_add_fusion.place, bf16[256,8192]{1,0:T(8,128)(2,1)S(1)} %bitcast.20, bf16[4096,512]{1,0:T(8,128)(2,1)S(1)} %copy-done.2), custom_call_target="tpu_custom_call" | custom-call | flops 1073741824 | bytes 6291456 | tf_op jit(solution)/shard_map/project_own/pallas_call | solution.py:67
  14.1 2.3 %dynamic-slice_bitcast_fusion = bf16[256,2048]{1,0:T(8,128)(2,1)} fusion(bf16[1,256,8192]{2,1,0:T(8,128)(2,1)} %param.6, s32[]{:T(128)S(6)} %select_n.12), kind=kLoop, calls=%fused_computation | loop fusion | bytes 2097156 | tf_op jit(solution)/shard_map/dynamic_slice | solution.py:335
  16.4 12.7 %collective-permute-done.1.high.refs_2_ = bf16[128,4096]{1,0:T(8,128)(2,1)S(1)} collective-permute-done((bf16[128,4096]{1,0:T(8,128)(2,1)}, bf16[128,4096]{1,0:T(8,128)(2,1)S(1)}, u32[]{:S(2)}, u32[]{:S(2)}) %collective-permute-start.1) | collective-permute-done | bytes 1048608 | tf_op jit(solution)/shard_map/ppermute | solution.py:39
  29.2 3.0 %collective-permute-done.low.refs_1_ = bf16[128,4096]{1,0:T(8,128)(2,1)S(1)} collective-permute-done((bf16[128,4096]{1,0:T(8,128)(2,1)}, bf16[128,4096]{1,0:T(8,128)(2,1)S(1)}, u32[]{:S(2)}, u32[]{:S(2)}) %collective-permute-start) | collective-permute-done | bytes 1048608 | tf_op jit(solution)/shard_map/ppermute | solution.py:39
  32.2 0.0 copy-done.3
  32.2 2.2 %project_near.1 = (f32[128,512]{1,0:T(8,128)S(1)}, f32[128,512]{1,0:T(8,128)S(1)}) custom-call(bf16[128,4096]{1,0:T(8,128)(2,1)S(1)} %collective-permute-done.low.refs_1_, bf16[128,4096]{1,0:T(8,128)(2,1)S(1)} %collective-permute-done.1.high.refs_2_, bf16[4096,512]{1,0:T(8,128)(2,1)S(1)} %copy-done.3), custom_call_target="tpu_custom_call" | custom-call | flops 1073741824 | bytes 6291456 | tf_op jit(solution)/shard_map/project_near/pallas_call | solution.py:108
  34.4 0.0 copy-start.5
  34.4 0.0 copy-start.6
  34.4 0.4 collective-permute-start.2
  34.8 1.1 collective-permute-start.3
  35.9 0.0 copy-start.4
  35.9 2.4 %collective-permute-start.5 = (bf16[256,2048]{1,0:T(8,128)(2,1)}, bf16[256,2048]{1,0:T(8,128)(2,1)S(1)}, u32[]{:S(2)}, u32[]{:S(2)}) collective-permute-start(bf16[256,2048]{1,0:T(8,128)(2,1)} %dynamic-slice_bitcast_fusion), channel_id=1, source_target_pairs={{0,8},{1,9},{2,10},{3,11},{4,12},{5,13},{6,14},{7,15},{8,0},{9,1},... | collective-permute-start | bytes 3145736 | tf_op jit(solution)/shard_map/ppermute | solution.py:39
  38.4 2.0 %collective-permute-done.2 = f32[128,512]{1,0:T(8,128)S(1)} collective-permute-done((f32[128,512]{1,0:T(8,128)S(1)}, f32[128,512]{1,0:T(8,128)S(1)}, u32[]{:S(2)}, u32[]{:S(2)}) %collective-permute-start.2) | collective-permute-done | bytes 262176 | tf_op jit(solution)/shard_map/ppermute | solution.py:39
  40.4 1.7 collective-permute-done.3
  42.1 1.0 fusion.key_own
  43.1 5.8 %collective-permute-start.4 = (bf16[256,512]{1,0:T(8,128)(2,1)S(1)}, bf16[256,512]{1,0:T(8,128)(2,1)S(1)}, u32[]{:S(2)}, u32[]{:S(2)}) collective-permute-start(bf16[256,512]{1,0:T(8,128)(2,1)S(1)} %fusion.key_own), channel_id=1, source_target_pairs={{0,8},{1,9},{2,10},{3,11},{4,12},{5,13},{6,14},{7,15},{8,16},{9,17... | collective-permute-start | bytes 786440 | tf_op jit(solution)/shard_map/ppermute | solution.py:39
  49.0 0.1 collective-permute-start.7
  49.1 0.5 collective-permute-start.6
  49.6 2.6 %collective-permute-done.4.key_halo = bf16[256,512]{1,0:T(8,128)(2,1)S(1)} collective-permute-done((bf16[256,512]{1,0:T(8,128)(2,1)S(1)}, bf16[256,512]{1,0:T(8,128)(2,1)S(1)}, u32[]{:S(2)}, u32[]{:S(2)}) %collective-permute-start.4) | collective-permute-done | bytes 262176 | tf_op jit(solution)/shard_map/ppermute | solution.py:39
  52.2 0.0 copy-done.5
  52.2 0.0 copy-done.6
  52.2 0.0 copy-done.4
  52.2 0.0 copy-start.1
  52.3 15.5 %attend.1 = (f32[32,256]{1,0:T(8,128)}, bf16[256,4096]{1,0:T(8,128)(2,1)}, f32[256,512]{1,0:T(8,128)S(1)}, bf16[256,512]{1,0:T(8,128)(2,1)S(1)}) custom-call(s32[3]{0:T(128)S(1)} %pad_add_fusion.place, s32[1,32]{1,0:T(1,128)S(1)} %copy-done.6, bf16[256,4096]{1,0:T(8,128)(2,1)S(1)} %bitcast.25, bf16[256,512]{1,0:T(8,128)(2,1)S(1)} %fusion.key_own, ...), custom_call_target="tpu_custom_call" | custom-call | flops 4294967296 | bytes 6291456 | tf_op jit(solution)/shard_map/attend/pallas_call | solution.py:194
  67.7 0.0 collective-permute-done.7.refs_5_
  67.7 0.0 collective-permute-done.6.refs_4_
  67.8 0.0 collective-permute-done.5.refs_3_
  67.8 1.9 %collective-permute-start.8 = (bf16[256,512]{1,0:T(8,128)(2,1)S(1)}, bf16[256,512]{1,0:T(8,128)(2,1)S(1)}, u32[]{:S(2)}, u32[]{:S(2)}) collective-permute-start(bf16[256,512]{1,0:T(8,128)(2,1)S(1)} %get-tuple-element.30), channel_id=1, source_target_pairs={{8,0},{9,1},{10,2},{11,3},{12,4},{13,5},{14,6},{15,7},{16,8},{17,9... | collective-permute-start | bytes 786440 | tf_op jit(solution)/shard_map/ppermute | solution.py:39
  69.7 6.5 %collective-permute-done.8 = bf16[256,512]{1,0:T(8,128)(2,1)S(1)} collective-permute-done((bf16[256,512]{1,0:T(8,128)(2,1)S(1)}, bf16[256,512]{1,0:T(8,128)(2,1)S(1)}, u32[]{:S(2)}, u32[]{:S(2)}) %collective-permute-start.8) | collective-permute-done | bytes 262176 | tf_op jit(solution)/shard_map/ppermute | solution.py:39
  76.2 0.1 add_convert_fusion.refs_6_
  76.3 0.1 collective-permute-start.11
  76.4 2.2 %collective-permute-start.10 = (bf16[128,512]{1,0:T(8,128)(2,1)S(1)}, bf16[128,512]{1,0:T(8,128)(2,1)S(1)}, u32[]{:S(2)}, u32[]{:S(2)}) collective-permute-start(bf16[128,512]{1,0:T(8,128)(2,1)S(1)} %get-tuple-element.33), channel_id=1, source_target_pairs={{0,68},{1,69},{2,70},{3,71},{4,0},{5,1},{6,2},{7,3},{8,76},{9,77},... | collective-permute-start | bytes 393224 | tf_op jit(solution)/shard_map/ppermute | solution.py:39
  78.6 0.0 collective-permute-start.9
  78.6 2.8 %collective-permute-done.10.refs_8_ = bf16[128,512]{1,0:T(8,128)(2,1)S(1)} collective-permute-done((bf16[128,512]{1,0:T(8,128)(2,1)S(1)}, bf16[128,512]{1,0:T(8,128)(2,1)S(1)}, u32[]{:S(2)}, u32[]{:S(2)}) %collective-permute-start.10) | collective-permute-done | bytes 131104 | tf_op jit(solution)/shard_map/ppermute | solution.py:39
  81.4 1.0 collective-permute-start.13
  82.4 2.1 %collective-permute-done.9.refs_7_ = bf16[128,512]{1,0:T(8,128)(2,1)S(1)} collective-permute-done((bf16[128,512]{1,0:T(8,128)(2,1)S(1)}, bf16[128,512]{1,0:T(8,128)(2,1)S(1)}, u32[]{:S(2)}, u32[]{:S(2)}) %collective-permute-start.9) | collective-permute-done | bytes 131104 | tf_op jit(solution)/shard_map/ppermute | solution.py:39
  84.5 1.2 collective-permute-start.12
  85.7 0.0 collective-permute-done.11.refs_9_
  85.7 0.0 collective-permute-done.13.refs_11_
  85.7 1.0 collective-permute-done.12.refs_10_
  86.7 0.0 copy-done.1
  86.7 5.3 %weight_grad.1 = bf16[2048,512]{1,0:T(8,128)(2,1)S(1)} custom-call(s32[3]{0:T(128)S(1)} %pad_add_fusion.place, bf16[256,8192]{1,0:T(8,128)(2,1)S(1)} %bitcast.21, bf16[128,4096]{1,0:T(8,128)(2,1)S(1)} %collective-permute-done.low.refs_1_, bf16[128,4096]{1,0:T(8,128)(2,1)S(1)} %collective-permute-done.1.high.refs_2_, ...), custom_call_target="tpu_custom_call" | custom-call | flops 2147483648 | bytes 8388608 | tf_op jit(solution)/shard_map/weight_grad/pallas_call | solution.py:239
  91.9 36.0 %all_to_all.10.parts = bf16[32,64,512]{2,1,0:T(8,128)(2,1)S(1)} all-to-all(bf16[32,64,512]{2,1,0:T(8,128)(2,1)S(1)} %bitcast.24), channel_id=1, replica_groups=mesh['xh'=2,'y'=4,'core'=2,'xl'=2,'z'=4] {'xh','y','z'}, dimensions={0} | all-to-all | bytes 4194304 | tf_op jit(solution)/shard_map/all_to_all | solution.py:366
  128.0 0.8 sum_spread.1
  128.8 32.1 %all_to_all.11 = bf16[32,64,512]{2,1,0:T(8,128)(2,1)S(1)} all-to-all(bf16[32,64,512]{2,1,0:T(8,128)(2,1)S(1)} %sum_spread.1), channel_id=1, replica_groups=mesh['xh'=2,'y'=4,'core'=2,'xl'=2,'z'=4] {'xh','y','z'}, dimensions={0} | all-to-all | bytes 4194304 | tf_op jit(solution)/shard_map/all_to_all | solution.py:368
  160.8 3.4 %collective-permute-start.14 = (bf16[2048,512]{1,0:T(8,128)(2,1)S(1)}, bf16[2048,512]{1,0:T(8,128)(2,1)S(1)}, u32[]{:S(2)}, u32[]{:S(2)}) collective-permute-start(bf16[2048,512]{1,0:T(8,128)(2,1)S(1)} %bitcast.22), channel_id=1, source_target_pairs={{0,8},{1,9},{2,10},{3,11},{4,12},{5,13},{6,14},{7,15},{8,0},{9,1},... | collective-permute-start | bytes 6291464 | tf_op jit(solution)/shard_map/ppermute | solution.py:39
  164.3 1.9 %write_rows.2.refs_0_ = bf16[4096,512]{1,0:T(8,128)(2,1)} custom-call(s32[3]{0:T(128)S(1)} %pad_add_fusion.place, bf16[2048,512]{1,0:T(8,128)(2,1)S(1)} %bitcast.23), custom_call_target="tpu_custom_call" | custom-call | flops 1048576 | bytes 4194304 | tf_op jit(solution)/shard_map/write_rows/pallas_call | solution.py:289
  166.2 1.8 %collective-permute-done.14.rows = bf16[2048,512]{1,0:T(8,128)(2,1)S(1)} collective-permute-done((bf16[2048,512]{1,0:T(8,128)(2,1)S(1)}, bf16[2048,512]{1,0:T(8,128)(2,1)S(1)}, u32[]{:S(2)}, u32[]{:S(2)}) %collective-permute-start.14) | collective-permute-done | bytes 2097184 | tf_op jit(solution)/shard_map/ppermute | solution.py:39
  168.1 1.9 %write_rows.3 = bf16[4096,512]{1,0:T(8,128)(2,1)} custom-call(s32[3]{0:T(128)S(1)} %pad_add_fusion.place, bf16[2048,512]{1,0:T(8,128)(2,1)S(1)} %collective-permute-done.14.rows, bf16[4096,512]{1,0:T(8,128)(2,1)} %write_rows.2.refs_0_), custom_call_target="tpu_custom_call", output_to_operand_aliasing={{}: (2, {})} | custom-call | flops 1048576 | bytes 4194304 | tf_op jit(solution)/shard_map/write_rows/pallas_call | solution.py:289
  (3 shorter events, 0.1 us)
Async XLA Ops:
  3.7 25.5 %collective-permute-start.1 = (bf16[128,4096]{1,0:T(8,128)(2,1)}, bf16[128,4096]{1,0:T(8,128)(2,1)S(1)}, u32[]{:S(2)}, u32[]{:S(2)}) collective-permute-start(bf16[128,4096]{1,0:T(8,128)(2,1)} %get-tuple-element.31), channel_id=1, source_target_pairs={{0,68},{1,69},{2,70},{3,71},{4,0},{5,1},{6,2},{7,3},{8,76},{9,77},... | collective-permute-start | bytes 3145736 | tf_op jit(solution)/shard_map/ppermute | solution.py:39
  7.0 25.1 %collective-permute-start = (bf16[128,4096]{1,0:T(8,128)(2,1)}, bf16[128,4096]{1,0:T(8,128)(2,1)S(1)}, u32[]{:S(2)}, u32[]{:S(2)}) collective-permute-start(bf16[128,4096]{1,0:T(8,128)(2,1)} %get-tuple-element.32), channel_id=1, source_target_pairs={{0,4},{1,5},{2,6},{3,7},{4,64},{5,65},{6,66},{7,67},{8,12},{9,13},... | collective-permute-start | bytes 3145736 | tf_op jit(solution)/shard_map/ppermute | solution.py:39
  7.1 2.2 %copy-start = (bf16[1,256,8192]{2,1,0:T(8,128)(2,1)S(1)}, bf16[1,256,8192]{2,1,0:T(8,128)(2,1)}, u32[]{:S(2)}) copy-start(bf16[1,256,8192]{2,1,0:T(8,128)(2,1)} %param.6) | copy-start | bytes 12582916
  9.3 2.2 %copy-start.2 = (bf16[4096,512]{1,0:T(8,128)(2,1)S(1)}, bf16[4096,512]{1,0:T(8,128)(2,1)}, u32[]{:S(2)}) copy-start(bf16[4096,512]{1,0:T(8,128)(2,1)} %weight.3) | copy-start | bytes 12582916
  11.5 20.7 %copy-start.3 = (bf16[4096,512]{1,0:T(8,128)(2,1)S(1)}, bf16[4096,512]{1,0:T(8,128)(2,1)}, u32[]{:S(2)}) copy-start(bf16[4096,512]{1,0:T(8,128)(2,1)} %weight.3) | copy-start | bytes 12582916
  34.4 17.9 %copy-start.5 = (bf16[1,256,32]{1,2,0:T(8,128)(2,1)S(1)}, bf16[1,256,32]{1,2,0:T(8,128)(2,1)}, u32[]{:S(2)}) copy-start(bf16[1,256,32]{1,2,0:T(8,128)(2,1)} %param.9) | copy-start | bytes 49156
  34.4 17.9 %copy-start.6 = (s32[1,32]{1,0:T(1,128)S(1)}, s32[1,32]{1,0:T(1,128)}, u32[]{:S(2)}) copy-start(s32[1,32]{1,0:T(1,128)} %lengths.1) | copy-start | bytes 388
  34.4 6.0 %collective-permute-start.2 = (f32[128,512]{1,0:T(8,128)S(1)}, f32[128,512]{1,0:T(8,128)S(1)}, u32[]{:S(2)}, u32[]{:S(2)}) collective-permute-start(f32[128,512]{1,0:T(8,128)S(1)} %get-tuple-element.20), channel_id=1, source_target_pairs={{0,68},{1,69},{2,70},{3,71},{4,0},{5,1},{6,2},{7,3},{8,76},{9,77},... | collective-permute-start | bytes 786440 | tf_op jit(solution)/shard_map/ppermute | solution.py:39
  34.8 7.3 %collective-permute-start.3 = (f32[128,512]{1,0:T(8,128)S(1)}, f32[128,512]{1,0:T(8,128)}, u32[]{:S(2)}, u32[]{:S(2)}) collective-permute-start(f32[128,512]{1,0:T(8,128)S(1)} %get-tuple-element.21), channel_id=1, source_target_pairs={{0,4},{1,5},{2,6},{3,7},{4,64},{5,65},{6,66},{7,67},{8,12},{9,13},... | collective-permute-start | bytes 786440 | tf_op jit(solution)/shard_map/ppermute | solution.py:39
  35.9 16.3 %copy-start.4 = (bf16[1,256,4096]{2,1,0:T(8,128)(2,1)S(1)}, bf16[1,256,4096]{2,1,0:T(8,128)(2,1)}, u32[]{:S(2)}) copy-start(bf16[1,256,4096]{2,1,0:T(8,128)(2,1)} %param.5) | copy-start | bytes 6291460
  35.9 31.8 %collective-permute-start.5 = (bf16[256,2048]{1,0:T(8,128)(2,1)}, bf16[256,2048]{1,0:T(8,128)(2,1)S(1)}, u32[]{:S(2)}, u32[]{:S(2)}) collective-permute-start(bf16[256,2048]{1,0:T(8,128)(2,1)} %dynamic-slice_bitcast_fusion), channel_id=1, source_target_pairs={{0,8},{1,9},{2,10},{3,11},{4,12},{5,13},{6,14},{7,15},{8,0},{9,1},... | collective-permute-start | bytes 3145736 | tf_op jit(solution)/shard_map/ppermute | solution.py:39
  43.1 9.1 %collective-permute-start.4 = (bf16[256,512]{1,0:T(8,128)(2,1)S(1)}, bf16[256,512]{1,0:T(8,128)(2,1)S(1)}, u32[]{:S(2)}, u32[]{:S(2)}) collective-permute-start(bf16[256,512]{1,0:T(8,128)(2,1)S(1)} %fusion.key_own), channel_id=1, source_target_pairs={{0,8},{1,9},{2,10},{3,11},{4,12},{5,13},{6,14},{7,15},{8,16},{9,17... | collective-permute-start | bytes 786440 | tf_op jit(solution)/shard_map/ppermute | solution.py:39
  49.0 18.7 %collective-permute-start.7 = (bf16[128,2048]{1,0:T(8,128)(2,1)S(1)}, bf16[128,2048]{1,0:T(8,128)(2,1)S(1)}, u32[]{:S(2)}, u32[]{:S(2)}) collective-permute-start(bf16[128,2048]{1,0:T(8,128)(2,1)S(1)} %constant_dynamic-slice_fusion), channel_id=1, source_target_pairs={{0,8},{1,9},{2,10},{3,11},{4,12},{5,13},{6,14},{7,15},{8,0},{9,1},... | collective-permute-start | bytes 1572872 | tf_op jit(solution)/shard_map/ppermute | solution.py:39
  49.1 18.7 %collective-permute-start.6 = (bf16[128,2048]{1,0:T(8,128)(2,1)S(1)}, bf16[128,2048]{1,0:T(8,128)(2,1)S(1)}, u32[]{:S(2)}, u32[]{:S(2)}) collective-permute-start(bf16[128,2048]{1,0:T(8,128)(2,1)S(1)} %constant_dynamic-slice_fusion.1), channel_id=1, source_target_pairs={{0,8},{1,9},{2,10},{3,11},{4,12},{5,13},{6,14},{7,15},{8,0},{9,1},... | collective-permute-start | bytes 1572872 | tf_op jit(solution)/shard_map/ppermute | solution.py:39
  52.2 34.4 %copy-start.1 = (bf16[1,256,8192]{2,1,0:T(8,128)(2,1)S(1)}, bf16[1,256,8192]{2,1,0:T(8,128)(2,1)}, u32[]{:S(2)}) copy-start(bf16[1,256,8192]{2,1,0:T(8,128)(2,1)} %param.6) | copy-start | bytes 12582916
  67.8 8.4 %collective-permute-start.8 = (bf16[256,512]{1,0:T(8,128)(2,1)S(1)}, bf16[256,512]{1,0:T(8,128)(2,1)S(1)}, u32[]{:S(2)}, u32[]{:S(2)}) collective-permute-start(bf16[256,512]{1,0:T(8,128)(2,1)S(1)} %get-tuple-element.30), channel_id=1, source_target_pairs={{8,0},{9,1},{10,2},{11,3},{12,4},{13,5},{14,6},{15,7},{16,8},{17,9... | collective-permute-start | bytes 786440 | tf_op jit(solution)/shard_map/ppermute | solution.py:39
  76.3 9.4 %collective-permute-start.11 = (bf16[256,512]{1,0:T(8,128)(2,1)S(1)}, bf16[256,512]{1,0:T(8,128)(2,1)S(1)}, u32[]{:S(2)}, u32[]{:S(2)}) collective-permute-start(bf16[256,512]{1,0:T(8,128)(2,1)S(1)} %add_convert_fusion.refs_6_), channel_id=1, source_target_pairs={{0,8},{1,9},{2,10},{3,11},{4,12},{5,13},{6,14},{7,15},{8,0},{9,1},... | collective-permute-start | bytes 786440 | tf_op jit(solution)/shard_map/ppermute | solution.py:39
  76.4 5.0 %collective-permute-start.10 = (bf16[128,512]{1,0:T(8,128)(2,1)S(1)}, bf16[128,512]{1,0:T(8,128)(2,1)S(1)}, u32[]{:S(2)}, u32[]{:S(2)}) collective-permute-start(bf16[128,512]{1,0:T(8,128)(2,1)S(1)} %get-tuple-element.33), channel_id=1, source_target_pairs={{0,68},{1,69},{2,70},{3,71},{4,0},{5,1},{6,2},{7,3},{8,76},{9,77},... | collective-permute-start | bytes 393224 | tf_op jit(solution)/shard_map/ppermute | solution.py:39
  78.6 5.9 %collective-permute-start.9 = (bf16[128,512]{1,0:T(8,128)(2,1)S(1)}, bf16[128,512]{1,0:T(8,128)(2,1)S(1)}, u32[]{:S(2)}, u32[]{:S(2)}) collective-permute-start(bf16[128,512]{1,0:T(8,128)(2,1)S(1)} %get-tuple-element.34), channel_id=1, source_target_pairs={{0,4},{1,5},{2,6},{3,7},{4,64},{5,65},{6,66},{7,67},{8,12},{9,13},... | collective-permute-start | bytes 393224 | tf_op jit(solution)/shard_map/ppermute | solution.py:39
  81.4 4.3 %collective-permute-start.13 = (bf16[128,512]{1,0:T(8,128)(2,1)S(1)}, bf16[128,512]{1,0:T(8,128)(2,1)S(1)}, u32[]{:S(2)}, u32[]{:S(2)}) collective-permute-start(bf16[128,512]{1,0:T(8,128)(2,1)S(1)} %collective-permute-done.10.refs_8_), channel_id=1, source_target_pairs={{0,8},{1,9},{2,10},{3,11},{4,12},{5,13},{6,14},{7,15},{8,0},{9,1},... | collective-permute-start | bytes 393224 | tf_op jit(solution)/shard_map/ppermute | solution.py:39
  84.5 2.2 %collective-permute-start.12 = (bf16[128,512]{1,0:T(8,128)(2,1)S(1)}, bf16[128,512]{1,0:T(8,128)(2,1)S(1)}, u32[]{:S(2)}, u32[]{:S(2)}) collective-permute-start(bf16[128,512]{1,0:T(8,128)(2,1)S(1)} %collective-permute-done.9.refs_7_), channel_id=1, source_target_pairs={{0,8},{1,9},{2,10},{3,11},{4,12},{5,13},{6,14},{7,15},{8,0},{9,1},... | collective-permute-start | bytes 393224 | tf_op jit(solution)/shard_map/ppermute | solution.py:39
  160.8 7.2 %collective-permute-start.14 = (bf16[2048,512]{1,0:T(8,128)(2,1)S(1)}, bf16[2048,512]{1,0:T(8,128)(2,1)S(1)}, u32[]{:S(2)}, u32[]{:S(2)}) collective-permute-start(bf16[2048,512]{1,0:T(8,128)(2,1)S(1)} %bitcast.22), channel_id=1, source_target_pairs={{0,8},{1,9},{2,10},{3,11},{4,12},{5,13},{6,14},{7,15},{8,0},{9,1},... | collective-permute-start | bytes 6291464 | tf_op jit(solution)/shard_map/ppermute | solution.py:39

commit v4 on v3

--- a/solution.py
+++ b/solution.py
@@ -97,8 +97,8 @@
     @pl.when(pl.program_id(0) == pl.num_programs(0) - 1)
     def _():
         count = low.shape[0]
-        low_out[...] = total[:count]
-        high_out[...] = total[count:]
+        low_out[...] = total[:count].astype(BF)
+        high_out[...] = total[count:].astype(BF)
 
 
 def project_near(low, high, weight):
@@ -114,7 +114,7 @@
             pl.BlockSpec((step, width), lambda i: (i, 0)),
         ],
         out_specs=[pl.BlockSpec((rows, width), lambda i: (0, 0))] * 2,
-        out_shape=[jax.ShapeDtypeStruct((rows, width), F32)] * 2,
+        out_shape=[jax.ShapeDtypeStruct((rows, width), BF)] * 2,
         scratch_shapes=[pltpu.VMEM((2 * rows, width), F32)],
         compiler_params=params(12),
         cost_estimate=cost(4 * rows * half * width, 6 << 20),
@@ -150,36 +150,56 @@
     keys[256:512, :] = key_own[...]
     keys_t[...] = keys[...].T
     weights = weight[...].astype(F32)
+    def score(pair, half):
+        cols = [slice((2 * pair + k) * HD, (2 * pair + k + 1) * HD) for k in range(2)]
+        rows = slice(half * 128, (half + 1) * 128)
+        window = slice(half * 128, half * 128 + 384)
+        stack = jnp.concatenate([query[rows, cols[0]], query[rows, cols[1]]], axis=0)
+        raw = lax.dot_general(
+            keys[window, :], stack, (((1,), (1,)), ((), ())), preferred_element_type=F32
+        ) + bias[half]
+        return raw, stack
+
+    def soften(pair, half, raw):
+        rows = slice(half * 128, (half + 1) * 128)
+        top = jnp.max(raw, axis=0, keepdims=True)
+        gap = raw - top
+        power = jnp.exp2(gap * EXP_SCALE)
+        den = jnp.sum(power, axis=0, keepdims=True)
+        mean = jnp.sum(power * gap, axis=0, keepdims=True) / den
+        row_weight = jnp.concatenate(
+            [weights[2 * pair:2 * pair + 1, rows], weights[2 * pair + 1:2 * pair + 2, rows]], axis=1
+        )
+        slope_b = row_weight * FACTOR / den
+        slope_a = slope_b * mean
+        level = jnp.log(den) - FACTOR * mean
+        entropy[2 * pair:2 * pair + 1, rows] = level[:, 0:128]
+        entropy[2 * pair + 1:2 * pair + 2, rows] = level[:, 128:256]
+        return (power * (slope_a - slope_b * gap)).astype(BF)
+
+    def grads(pair, half, slope, stack):
+        cols = [slice((2 * pair + k) * HD, (2 * pair + k + 1) * HD) for k in range(2)]
+        rows = slice(half * 128, (half + 1) * 128)
+        window = slice(half * 128, half * 128 + 384)
+        turned = jnp.dot(keys_t[:, window], slope, preferred_element_type=F32) * FACTOR
+        straight = turned.T.astype(BF)
+        grad_query[rows, cols[0]] = straight[0:128]
+        grad_query[rows, cols[1]] = straight[128:256]
+        part = jnp.dot(slope, stack, preferred_element_type=F32)
+        sums[half] = part if sums[half] is None else sums[half] + part
+
     sums = [None, None]
-    for pair in range(GROUP // 2):
-        cols = [slice((2 * pair + k) * HD, (2 * pair + k + 1) * HD) for k in range(2)]
-        for half in range(2):
-            rows = slice(half * 128, (half + 1) * 128)
-            window = slice(half * 128, half * 128 + 384)
-            stack = jnp.concatenate([query[rows, cols[0]], query[rows, cols[1]]], axis=0)
-            raw = lax.dot_general(
-                keys[window, :], stack, (((1,), (1,)), ((), ())), preferred_element_type=F32
-            ) + bias[half]
-            top = jnp.max(raw, axis=0, keepdims=True)
-            gap = raw - top
-            power = jnp.exp2(gap * EXP_SCALE)
-            den = jnp.sum(power, axis=0, keepdims=True)
-            mean = jnp.sum(power * gap, axis=0, keepdims=True) / den
-            row_weight = jnp.concatenate(
-                [weights[2 * pair:2 * pair + 1, rows], weights[2 * pair + 1:2 * pair + 2, rows]], axis=1
-            )
-            slope_b = row_weight * FACTOR / den
-            slope_a = slope_b * mean
-            slope = (power * (slope_a - slope_b * gap)).astype(BF)
-            level = jnp.log(den) - FACTOR * mean
-            entropy[2 * pair:2 * pair + 1, rows] = level[:, 0:128]
-            entropy[2 * pair + 1:2 * pair + 2, rows] = level[:, 128:256]
-            turned = jnp.dot(keys_t[:, window], slope, preferred_element_type=F32) * FACTOR
-            straight = turned.T.astype(BF)
-            grad_query[rows, cols[0]] = straight[0:128]
-            grad_query[rows, cols[1]] = straight[128:256]
-            part = jnp.dot(slope, stack, preferred_element_type=F32)
-            sums[half] = part if sums[half] is None else sums[half] + part
+    order = [(pair, half) for pair in range(GROUP // 2) for half in range(2)]
+    ahead = score(*order[0])
+    last = None
+    for i, at in enumerate(order):
+        raw, stack = ahead
+        if i + 1 < len(order):
+            ahead = score(*order[i + 1])
+        if last is not None:
+            grads(*last)
+        last = (*at, soften(*at, raw), stack)
+    grads(*last)
     low, high = sums
     grad_halo[0:128, :] = (low[0:128] * FACTOR).astype(grad_halo.dtype)
     grad_halo[128:256, :] = ((low[128:256] + high[0:128]) * FACTOR).astype(grad_halo.dtype)
@@ -240,12 +260,12 @@
         functools.partial(weight_grad_kernel, 1 + len(near) + len(swapped)),
         grid_spec=pltpu.PrefetchScalarGridSpec(
             num_scalar_prefetch=1,
-            grid=(8,),
-            in_specs=[pl.BlockSpec((256, 256), lambda i, p: (0, (p[0] * 2 + p[1]) * 8 + i))]
-            + [pl.BlockSpec((v.shape[0], 256), lambda i, p: (0, p[1] * 8 + i)) for v in near]
-            + [pl.BlockSpec((v.shape[0], 256), lambda i, p: (0, i)) for v in swapped]
+            grid=(4,),
+            in_specs=[pl.BlockSpec((256, 512), lambda i, p: (0, (p[0] * 2 + p[1]) * 4 + i))]
+            + [pl.BlockSpec((v.shape[0], 512), lambda i, p: (0, p[1] * 4 + i)) for v in near]
+            + [pl.BlockSpec((v.shape[0], 512), lambda i, p: (0, i)) for v in swapped]
             + [pl.BlockSpec(v.shape, whole) for v in grads],
-            out_specs=pl.BlockSpec((256, 512), lambda i, p: (i, 0)),
+            out_specs=pl.BlockSpec((512, 512), lambda i, p: (i, 0)),
         ),
         out_shape=jax.ShapeDtypeStruct((2048, 512), BF),
         compiler_params=params(16),
@@ -343,7 +363,7 @@
     near, total, passed = lax.optimization_barrier((near, total, passed))
     low, high = project_near(*near, key_weight)
     low, high = move(low, backward), move(high, forward)
-    key_own = (total + jnp.concatenate([low, high], axis=0)).astype(BF)
+    key_own = (total + jnp.concatenate([low, high], axis=0).astype(F32)).astype(BF)
     key_halo = move(key_own, next_rows(1))
 
     start = (1 - core) * quarter

time: 170 us -> 161 us (0.947)
  Pallas kernels: 30.2 us -> 24.6 us
  local copies, waits for them, and re-layouts: 9.93 us -> 7.31 us
    pallas_call x1, Pallas kernels: 15.5 us -> 11.2 us  [attend(): pl.pallas_call(attend_kernel, grid_spec=pltpu.PrefetchScalarGridSpec(num_...]
    dynamic_slice x2, local copies, waits for them, and re-layouts: 5.43 us -> 2.81 us  [column(): return lax.dynamic_slice(tokens, (first, start), (last - first, count))]
  transfers between devices with their start and end apart: 15 -> 15, of which waited for: 10 -> 9; matrix products, arithmetic and copies ran while one was open for 2% -> 0% of each run, Pallas kernels for 12% -> 10%
where the time goes in v4:
time: 161 us
  blocking collectives  68.1 us (42%)
  waiting for transfers between devices  36.2 us (22%)
  Pallas kernels  24.6 us (15%)
  starting transfers between devices  23.7 us (15%)
  local copies, waits for them, and re-layouts  7.31 us (5%)
    ppermute x15, waiting for transfers between devices, move(): return lax.ppermute(value, AXES, pairs)  36.2 us
    all_to_all x1, blocking collectives, shards(): lax.all_to_all(parts, chips, split_axis=0, concat_axis=0, tiled=True)  36 us
    all_to_all x1, blocking collectives, shards(): lax.all_to_all(spread, chips, split_axis=0, concat_axis=0, tiled=True)  32.1 us
    ppermute x15, starting transfers between devices, move(): return lax.ppermute(value, AXES, pairs)  23.7 us
    pallas_call x1, Pallas kernels, attend(): pl.pallas_call(attend_kernel, grid_spec=pltpu.PrefetchScalarGridSpec(num_...  11.2 us
    unnamed x14, local copies, waits for them, and re-layouts  4.4 us
    pallas_call x1, Pallas kernels, weight_grad(): pl.pallas_call(functools.partial(weight_grad_kernel, 1 + len(near) + len(...  4.02 us
    pallas_call x2, Pallas kernels, write_rows(): pl.pallas_call(copy_kernel, grid_spec=pltpu.PrefetchScalarGridSpec(num_sc...  3.89 us
  transfers between devices with their start and end apart: 15, of which 9 were waited for; matrix products, arithmetic and copies ran while one was open for 0% of the time, Pallas kernels for 10%

profile of v4, /device:TPU:1, one launch (start us, length us, event | category | flops | bytes accessed | tf_op | source)
XLA Modules:
  0.0 160.9 jit_solution(17835615716781919850)
XLA Ops:
  0.6 2.7 %dynamic-slice_bitcast_fusion.1 = (bf16[128,4096]{1,0:T(8,128)(2,1)}, bf16[128,4096]{1,0:T(8,128)(2,1)S(1)}) fusion(bf16[1,256,8192]{2,1,0:T(8,128)(2,1)} %param.6, s32[]{:T(128)S(6)} %select_n.11), kind=kLoop, calls=%fused_computation.1 | loop fusion | bytes 4194308 | tf_op jit(solution)/shard_map/dynamic_slice | solution.py:355
  3.3 3.3 %collective-permute-start.1 = (bf16[128,4096]{1,0:T(8,128)(2,1)}, bf16[128,4096]{1,0:T(8,128)(2,1)S(1)}, u32[]{:S(2)}, u32[]{:S(2)}) collective-permute-start(bf16[128,4096]{1,0:T(8,128)(2,1)} %get-tuple-element.31), channel_id=1, source_target_pairs={{0,68},{1,69},{2,70},{3,71},{4,0},{5,1},{6,2},{7,3},{8,76},{9,77},... | collective-permute-start | bytes 3145736 | tf_op jit(solution)/shard_map/ppermute | solution.py:39
  6.6 0.0 collective-permute-start
  6.6 0.1 pad_add_fusion.place
  6.7 0.0 copy-start
  6.7 2.2 %copy-done = bf16[1,256,8192]{2,1,0:T(8,128)(2,1)S(1)} copy-done((bf16[1,256,8192]{2,1,0:T(8,128)(2,1)S(1)}, bf16[1,256,8192]{2,1,0:T(8,128)(2,1)}, u32[]{:S(2)}) %copy-start) | copy-done | bytes 4194328
  8.9 0.0 copy-start.2
  8.9 2.2 %copy-done.2 = bf16[4096,512]{1,0:T(8,128)(2,1)S(1)} copy-done((bf16[4096,512]{1,0:T(8,128)(2,1)S(1)}, bf16[4096,512]{1,0:T(8,128)(2,1)}, u32[]{:S(2)}) %copy-start.2) | copy-done | bytes 4194328
  11.1 0.0 copy-start.1
  11.1 0.0 copy-start.3
  11.1 2.6 %project_own.1 = f32[256,512]{1,0:T(8,128)S(1)} custom-call(s32[3]{0:T(128)S(1)} %pad_add_fusion.place, bf16[256,8192]{1,0:T(8,128)(2,1)S(1)} %bitcast.20, bf16[4096,512]{1,0:T(8,128)(2,1)S(1)} %copy-done.2), custom_call_target="tpu_custom_call" | custom-call | flops 1073741824 | bytes 6291456 | tf_op jit(solution)/shard_map/project_own/pallas_call | solution.py:67
  13.7 0.0 copy-done.1
  13.7 0.1 dynamic-slice_bitcast_fusion
  13.8 15.0 %collective-permute-done.1.high.refs_2_ = bf16[128,4096]{1,0:T(8,128)(2,1)S(1)} collective-permute-done((bf16[128,4096]{1,0:T(8,128)(2,1)}, bf16[128,4096]{1,0:T(8,128)(2,1)S(1)}, u32[]{:S(2)}, u32[]{:S(2)}) %collective-permute-start.1) | collective-permute-done | bytes 1048608 | tf_op jit(solution)/shard_map/ppermute | solution.py:39
  28.8 2.8 %collective-permute-done.low.refs_1_ = bf16[128,4096]{1,0:T(8,128)(2,1)S(1)} collective-permute-done((bf16[128,4096]{1,0:T(8,128)(2,1)S(1)}, bf16[128,4096]{1,0:T(8,128)(2,1)S(1)}, u32[]{:S(2)}, u32[]{:S(2)}) %collective-permute-start) | collective-permute-done | bytes 1048608 | tf_op jit(solution)/shard_map/ppermute | solution.py:39
  31.6 0.0 copy-done.3
  31.6 2.2 %project_near.1 = (bf16[128,512]{1,0:T(8,128)(2,1)S(1)}, bf16[128,512]{1,0:T(8,128)(2,1)S(1)}) custom-call(bf16[128,4096]{1,0:T(8,128)(2,1)S(1)} %collective-permute-done.low.refs_1_, bf16[128,4096]{1,0:T(8,128)(2,1)S(1)} %collective-permute-done.1.high.refs_2_, bf16[4096,512]{1,0:T(8,128)(2,1)S(1)} %copy-done.3), custom_call_target="tpu_custom_call" | custom-call | flops 1073741824 | bytes 6291456 | tf_op jit(solution)/shard_map/project_near/pallas_call | solution.py:108
  33.7 0.0 copy-start.4
  33.7 0.0 copy-start.5
  33.8 0.0 copy-start.6
  33.8 0.6 collective-permute-start.2
  34.4 0.9 collective-permute-start.3
  35.3 2.4 %collective-permute-start.5 = (bf16[256,2048]{1,0:T(8,128)(2,1)S(1)}, bf16[256,2048]{1,0:T(8,128)(2,1)S(1)}, u32[]{:S(2)}, u32[]{:S(2)}) collective-permute-start(bf16[256,2048]{1,0:T(8,128)(2,1)S(1)} %dynamic-slice_bitcast_fusion), channel_id=1, source_target_pairs={{0,8},{1,9},{2,10},{3,11},{4,12},{5,13},{6,14},{7,15},{8,0},{9,1},... | collective-permute-start | bytes 3145736 | tf_op jit(solution)/shard_map/ppermute | solution.py:39
  37.8 0.0 collective-permute-done.2
  37.8 1.6 %collective-permute-done.3 = bf16[128,512]{1,0:T(8,128)(2,1)S(1)} collective-permute-done((bf16[128,512]{1,0:T(8,128)(2,1)S(1)}, bf16[128,512]{1,0:T(8,128)(2,1)S(1)}, u32[]{:S(2)}, u32[]{:S(2)}) %collective-permute-start.3) | collective-permute-done | bytes 131104 | tf_op jit(solution)/shard_map/ppermute | solution.py:39
  39.4 0.1 add_convert_fusion.1.key_own
  39.5 6.1 %collective-permute-start.4 = (bf16[256,512]{1,0:T(8,128)(2,1)S(1)}, bf16[256,512]{1,0:T(8,128)(2,1)S(1)}, u32[]{:S(2)}, u32[]{:S(2)}) collective-permute-start(bf16[256,512]{1,0:T(8,128)(2,1)S(1)} %add_convert_fusion.1.key_own), channel_id=1, source_target_pairs={{0,8},{1,9},{2,10},{3,11},{4,12},{5,13},{6,14},{7,15},{8,16},{9,17... | collective-permute-start | bytes 786440 | tf_op jit(solution)/shard_map/ppermute | solution.py:39
  45.6 0.1 collective-permute-start.7
  45.7 0.5 collective-permute-start.6
  46.2 2.7 %collective-permute-done.4.key_halo = bf16[256,512]{1,0:T(8,128)(2,1)S(1)} collective-permute-done((bf16[256,512]{1,0:T(8,128)(2,1)S(1)}, bf16[256,512]{1,0:T(8,128)(2,1)S(1)}, u32[]{:S(2)}, u32[]{:S(2)}) %collective-permute-start.4) | collective-permute-done | bytes 262176 | tf_op jit(solution)/shard_map/ppermute | solution.py:39
  48.9 0.0 copy-done.4
  48.9 0.0 copy-done.5
  48.9 0.0 copy-done.6
  48.9 11.2 %attend.1 = (f32[32,256]{1,0:T(8,128)}, bf16[256,4096]{1,0:T(8,128)(2,1)}, f32[256,512]{1,0:T(8,128)S(1)}, bf16[256,512]{1,0:T(8,128)(2,1)S(1)}) custom-call(s32[3]{0:T(128)S(1)} %pad_add_fusion.place, s32[1,32]{1,0:T(1,128)S(1)} %copy-done.6, bf16[256,4096]{1,0:T(8,128)(2,1)S(1)} %bitcast.25, bf16[256,512]{1,0:T(8,128)(2,1)S(1)} %add_convert_fusion.1.key_own, ...), custom_call_target="tpu_custom_call" | custom-call | flops 4294967296 | bytes 6291456 | tf_op jit(solution)/shard_map/attend/pallas_call | solution.py:214
  60.1 0.0 collective-permute-done.7.refs_5_
  60.1 0.0 collective-permute-done.6.refs_4_
  60.1 0.0 collective-permute-done.5.refs_3_
  60.1 1.9 %collective-permute-start.8 = (bf16[256,512]{1,0:T(8,128)(2,1)S(1)}, bf16[256,512]{1,0:T(8,128)(2,1)S(1)}, u32[]{:S(2)}, u32[]{:S(2)}) collective-permute-start(bf16[256,512]{1,0:T(8,128)(2,1)S(1)} %get-tuple-element.30), channel_id=1, source_target_pairs={{8,0},{9,1},{10,2},{11,3},{12,4},{13,5},{14,6},{15,7},{16,8},{17,9... | collective-permute-start | bytes 786440 | tf_op jit(solution)/shard_map/ppermute | solution.py:39
  62.0 6.5 %collective-permute-done.8 = bf16[256,512]{1,0:T(8,128)(2,1)S(1)} collective-permute-done((bf16[256,512]{1,0:T(8,128)(2,1)S(1)}, bf16[256,512]{1,0:T(8,128)(2,1)S(1)}, u32[]{:S(2)}, u32[]{:S(2)}) %collective-permute-start.8) | collective-permute-done | bytes 262176 | tf_op jit(solution)/shard_map/ppermute | solution.py:39
  68.5 0.1 add_convert_fusion.refs_6_
  68.6 0.1 collective-permute-start.11
  68.7 2.0 %collective-permute-start.10 = (bf16[128,512]{1,0:T(8,128)(2,1)S(1)}, bf16[128,512]{1,0:T(8,128)(2,1)S(1)}, u32[]{:S(2)}, u32[]{:S(2)}) collective-permute-start(bf16[128,512]{1,0:T(8,128)(2,1)S(1)} %get-tuple-element.33), channel_id=1, source_target_pairs={{0,68},{1,69},{2,70},{3,71},{4,0},{5,1},{6,2},{7,3},{8,76},{9,77},... | collective-permute-start | bytes 393224 | tf_op jit(solution)/shard_map/ppermute | solution.py:39
  70.7 0.0 collective-permute-start.9
  70.7 2.8 %collective-permute-done.10.refs_8_ = bf16[128,512]{1,0:T(8,128)(2,1)S(1)} collective-permute-done((bf16[128,512]{1,0:T(8,128)(2,1)S(1)}, bf16[128,512]{1,0:T(8,128)(2,1)S(1)}, u32[]{:S(2)}, u32[]{:S(2)}) %collective-permute-start.10) | collective-permute-done | bytes 131104 | tf_op jit(solution)/shard_map/ppermute | solution.py:39
  73.6 1.1 collective-permute-start.13
  74.7 2.0 %collective-permute-done.9.refs_7_ = bf16[128,512]{1,0:T(8,128)(2,1)S(1)} collective-permute-done((bf16[128,512]{1,0:T(8,128)(2,1)S(1)}, bf16[128,512]{1,0:T(8,128)(2,1)S(1)}, u32[]{:S(2)}, u32[]{:S(2)}) %collective-permute-start.9) | collective-permute-done | bytes 131104 | tf_op jit(solution)/shard_map/ppermute | solution.py:39
  76.7 1.2 collective-permute-start.12
  77.9 0.0 collective-permute-done.11.refs_9_
  77.9 0.0 collective-permute-done.13.refs_11_
  77.9 1.0 collective-permute-done.12.refs_10_
  78.8 4.0 %weight_grad.1 = bf16[2048,512]{1,0:T(8,128)(2,1)S(1)} custom-call(s32[3]{0:T(128)S(1)} %pad_add_fusion.place, bf16[256,8192]{1,0:T(8,128)(2,1)S(1)} %bitcast.21, bf16[128,4096]{1,0:T(8,128)(2,1)S(1)} %collective-permute-done.low.refs_1_, bf16[128,4096]{1,0:T(8,128)(2,1)S(1)} %collective-permute-done.1.high.refs_2_, ...), custom_call_target="tpu_custom_call" | custom-call | flops 2147483648 | bytes 8388608 | tf_op jit(solution)/shard_map/weight_grad/pallas_call | solution.py:259
  82.9 36.0 %all_to_all.10.parts = bf16[32,64,512]{2,1,0:T(8,128)(2,1)S(1)} all-to-all(bf16[32,64,512]{2,1,0:T(8,128)(2,1)S(1)} %bitcast.24), channel_id=1, replica_groups=mesh['xh'=2,'y'=4,'core'=2,'xl'=2,'z'=4] {'xh','y','z'}, dimensions={0} | all-to-all | bytes 4194304 | tf_op jit(solution)/shard_map/all_to_all | solution.py:386
  118.9 0.8 sum_spread.1
  119.7 32.1 %all_to_all.11 = bf16[32,64,512]{2,1,0:T(8,128)(2,1)S(1)} all-to-all(bf16[32,64,512]{2,1,0:T(8,128)(2,1)S(1)} %sum_spread.1), channel_id=1, replica_groups=mesh['xh'=2,'y'=4,'core'=2,'xl'=2,'z'=4] {'xh','y','z'}, dimensions={0} | all-to-all | bytes 4194304 | tf_op jit(solution)/shard_map/all_to_all | solution.py:388
  151.7 3.4 %collective-permute-start.14 = (bf16[2048,512]{1,0:T(8,128)(2,1)S(1)}, bf16[2048,512]{1,0:T(8,128)(2,1)S(1)}, u32[]{:S(2)}, u32[]{:S(2)}) collective-permute-start(bf16[2048,512]{1,0:T(8,128)(2,1)S(1)} %bitcast.22), channel_id=1, source_target_pairs={{0,8},{1,9},{2,10},{3,11},{4,12},{5,13},{6,14},{7,15},{8,0},{9,1},... | collective-permute-start | bytes 6291464 | tf_op jit(solution)/shard_map/ppermute | solution.py:39
  155.2 1.9 %write_rows.2.refs_0_ = bf16[4096,512]{1,0:T(8,128)(2,1)} custom-call(s32[3]{0:T(128)S(1)} %pad_add_fusion.place, bf16[2048,512]{1,0:T(8,128)(2,1)S(1)} %bitcast.23), custom_call_target="tpu_custom_call" | custom-call | flops 1048576 | bytes 4194304 | tf_op jit(solution)/shard_map/write_rows/pallas_call | solution.py:309
  157.1 1.8 %collective-permute-done.14.rows = bf16[2048,512]{1,0:T(8,128)(2,1)S(1)} collective-permute-done((bf16[2048,512]{1,0:T(8,128)(2,1)S(1)}, bf16[2048,512]{1,0:T(8,128)(2,1)S(1)}, u32[]{:S(2)}, u32[]{:S(2)}) %collective-permute-start.14) | collective-permute-done | bytes 2097184 | tf_op jit(solution)/shard_map/ppermute | solution.py:39
  159.0 1.9 %write_rows.3 = bf16[4096,512]{1,0:T(8,128)(2,1)} custom-call(s32[3]{0:T(128)S(1)} %pad_add_fusion.place, bf16[2048,512]{1,0:T(8,128)(2,1)S(1)} %collective-permute-done.14.rows, bf16[4096,512]{1,0:T(8,128)(2,1)} %write_rows.2.refs_0_), custom_call_target="tpu_custom_call", output_to_operand_aliasing={{}: (2, {})} | custom-call | flops 1048576 | bytes 4194304 | tf_op jit(solution)/shard_map/write_rows/pallas_call | solution.py:309
  (3 shorter events, 0.1 us)
Async XLA Ops:
  3.3 25.5 %collective-permute-start.1 = (bf16[128,4096]{1,0:T(8,128)(2,1)}, bf16[128,4096]{1,0:T(8,128)(2,1)S(1)}, u32[]{:S(2)}, u32[]{:S(2)}) collective-permute-start(bf16[128,4096]{1,0:T(8,128)(2,1)} %get-tuple-element.31), channel_id=1, source_target_pairs={{0,68},{1,69},{2,70},{3,71},{4,0},{5,1},{6,2},{7,3},{8,76},{9,77},... | collective-permute-start | bytes 3145736 | tf_op jit(solution)/shard_map/ppermute | solution.py:39
  6.6 24.9 %collective-permute-start = (bf16[128,4096]{1,0:T(8,128)(2,1)S(1)}, bf16[128,4096]{1,0:T(8,128)(2,1)S(1)}, u32[]{:S(2)}, u32[]{:S(2)}) collective-permute-start(bf16[128,4096]{1,0:T(8,128)(2,1)S(1)} %get-tuple-element.32), channel_id=1, source_target_pairs={{0,4},{1,5},{2,6},{3,7},{4,64},{5,65},{6,66},{7,67},{8,12},{9,13},... | collective-permute-start | bytes 3145736 | tf_op jit(solution)/shard_map/ppermute | solution.py:39
  6.7 2.2 %copy-start = (bf16[1,256,8192]{2,1,0:T(8,128)(2,1)S(1)}, bf16[1,256,8192]{2,1,0:T(8,128)(2,1)}, u32[]{:S(2)}) copy-start(bf16[1,256,8192]{2,1,0:T(8,128)(2,1)} %param.6) | copy-start | bytes 12582916
  8.9 2.2 %copy-start.2 = (bf16[4096,512]{1,0:T(8,128)(2,1)S(1)}, bf16[4096,512]{1,0:T(8,128)(2,1)}, u32[]{:S(2)}) copy-start(bf16[4096,512]{1,0:T(8,128)(2,1)} %weight.3) | copy-start | bytes 12582916
  11.1 2.6 %copy-start.1 = (bf16[1,256,8192]{2,1,0:T(8,128)(2,1)S(1)}, bf16[1,256,8192]{2,1,0:T(8,128)(2,1)}, u32[]{:S(2)}) copy-start(bf16[1,256,8192]{2,1,0:T(8,128)(2,1)} %param.6) | copy-start | bytes 12582916
  11.1 20.5 %copy-start.3 = (bf16[4096,512]{1,0:T(8,128)(2,1)S(1)}, bf16[4096,512]{1,0:T(8,128)(2,1)}, u32[]{:S(2)}) copy-start(bf16[4096,512]{1,0:T(8,128)(2,1)} %weight.3) | copy-start | bytes 12582916
  33.7 15.1 %copy-start.4 = (bf16[1,256,4096]{2,1,0:T(8,128)(2,1)S(1)}, bf16[1,256,4096]{2,1,0:T(8,128)(2,1)}, u32[]{:S(2)}) copy-start(bf16[1,256,4096]{2,1,0:T(8,128)(2,1)} %param.5) | copy-start | bytes 6291460
  33.7 15.1 %copy-start.5 = (bf16[1,256,32]{1,2,0:T(8,128)(2,1)S(1)}, bf16[1,256,32]{1,2,0:T(8,128)(2,1)}, u32[]{:S(2)}) copy-start(bf16[1,256,32]{1,2,0:T(8,128)(2,1)} %param.9) | copy-start | bytes 49156
  33.8 15.1 %copy-start.6 = (s32[1,32]{1,0:T(1,128)S(1)}, s32[1,32]{1,0:T(1,128)}, u32[]{:S(2)}) copy-start(s32[1,32]{1,0:T(1,128)} %lengths.1) | copy-start | bytes 388
  33.8 4.0 %collective-permute-start.2 = (bf16[128,512]{1,0:T(8,128)(2,1)S(1)}, bf16[128,512]{1,0:T(8,128)(2,1)S(1)}, u32[]{:S(2)}, u32[]{:S(2)}) collective-permute-start(bf16[128,512]{1,0:T(8,128)(2,1)S(1)} %get-tuple-element.20), channel_id=1, source_target_pairs={{0,68},{1,69},{2,70},{3,71},{4,0},{5,1},{6,2},{7,3},{8,76},{9,77},... | collective-permute-start | bytes 393224 | tf_op jit(solution)/shard_map/ppermute | solution.py:39
  34.4 5.0 %collective-permute-start.3 = (bf16[128,512]{1,0:T(8,128)(2,1)S(1)}, bf16[128,512]{1,0:T(8,128)(2,1)S(1)}, u32[]{:S(2)}, u32[]{:S(2)}) collective-permute-start(bf16[128,512]{1,0:T(8,128)(2,1)S(1)} %get-tuple-element.21), channel_id=1, source_target_pairs={{0,4},{1,5},{2,6},{3,7},{4,64},{5,65},{6,66},{7,67},{8,12},{9,13},... | collective-permute-start | bytes 393224 | tf_op jit(solution)/shard_map/ppermute | solution.py:39
  35.3 24.8 %collective-permute-start.5 = (bf16[256,2048]{1,0:T(8,128)(2,1)S(1)}, bf16[256,2048]{1,0:T(8,128)(2,1)S(1)}, u32[]{:S(2)}, u32[]{:S(2)}) collective-permute-start(bf16[256,2048]{1,0:T(8,128)(2,1)S(1)} %dynamic-slice_bitcast_fusion), channel_id=1, source_target_pairs={{0,8},{1,9},{2,10},{3,11},{4,12},{5,13},{6,14},{7,15},{8,0},{9,1},... | collective-permute-start | bytes 3145736 | tf_op jit(solution)/shard_map/ppermute | solution.py:39
  39.5 9.4 %collective-permute-start.4 = (bf16[256,512]{1,0:T(8,128)(2,1)S(1)}, bf16[256,512]{1,0:T(8,128)(2,1)S(1)}, u32[]{:S(2)}, u32[]{:S(2)}) collective-permute-start(bf16[256,512]{1,0:T(8,128)(2,1)S(1)} %add_convert_fusion.1.key_own), channel_id=1, source_target_pairs={{0,8},{1,9},{2,10},{3,11},{4,12},{5,13},{6,14},{7,15},{8,16},{9,17... | collective-permute-start | bytes 786440 | tf_op jit(solution)/shard_map/ppermute | solution.py:39
  45.6 14.5 %collective-permute-start.7 = (bf16[128,2048]{1,0:T(8,128)(2,1)S(1)}, bf16[128,2048]{1,0:T(8,128)(2,1)S(1)}, u32[]{:S(2)}, u32[]{:S(2)}) collective-permute-start(bf16[128,2048]{1,0:T(8,128)(2,1)S(1)} %constant_dynamic-slice_fusion), channel_id=1, source_target_pairs={{0,8},{1,9},{2,10},{3,11},{4,12},{5,13},{6,14},{7,15},{8,0},{9,1},... | collective-permute-start | bytes 1572872 | tf_op jit(solution)/shard_map/ppermute | solution.py:39
  45.7 14.4 %collective-permute-start.6 = (bf16[128,2048]{1,0:T(8,128)(2,1)S(1)}, bf16[128,2048]{1,0:T(8,128)(2,1)S(1)}, u32[]{:S(2)}, u32[]{:S(2)}) collective-permute-start(bf16[128,2048]{1,0:T(8,128)(2,1)S(1)} %constant_dynamic-slice_fusion.1), channel_id=1, source_target_pairs={{0,8},{1,9},{2,10},{3,11},{4,12},{5,13},{6,14},{7,15},{8,0},{9,1},... | collective-permute-start | bytes 1572872 | tf_op jit(solution)/shard_map/ppermute | solution.py:39
  60.1 8.5 %collective-permute-start.8 = (bf16[256,512]{1,0:T(8,128)(2,1)S(1)}, bf16[256,512]{1,0:T(8,128)(2,1)S(1)}, u32[]{:S(2)}, u32[]{:S(2)}) collective-permute-start(bf16[256,512]{1,0:T(8,128)(2,1)S(1)} %get-tuple-element.30), channel_id=1, source_target_pairs={{8,0},{9,1},{10,2},{11,3},{12,4},{13,5},{14,6},{15,7},{16,8},{17,9... | collective-permute-start | bytes 786440 | tf_op jit(solution)/shard_map/ppermute | solution.py:39
  68.6 9.2 %collective-permute-start.11 = (bf16[256,512]{1,0:T(8,128)(2,1)S(1)}, bf16[256,512]{1,0:T(8,128)(2,1)S(1)}, u32[]{:S(2)}, u32[]{:S(2)}) collective-permute-start(bf16[256,512]{1,0:T(8,128)(2,1)S(1)} %add_convert_fusion.refs_6_), channel_id=1, source_target_pairs={{0,8},{1,9},{2,10},{3,11},{4,12},{5,13},{6,14},{7,15},{8,0},{9,1},... | collective-permute-start | bytes 786440 | tf_op jit(solution)/shard_map/ppermute | solution.py:39
  68.7 4.8 %collective-permute-start.10 = (bf16[128,512]{1,0:T(8,128)(2,1)S(1)}, bf16[128,512]{1,0:T(8,128)(2,1)S(1)}, u32[]{:S(2)}, u32[]{:S(2)}) collective-permute-start(bf16[128,512]{1,0:T(8,128)(2,1)S(1)} %get-tuple-element.33), channel_id=1, source_target_pairs={{0,68},{1,69},{2,70},{3,71},{4,0},{5,1},{6,2},{7,3},{8,76},{9,77},... | collective-permute-start | bytes 393224 | tf_op jit(solution)/shard_map/ppermute | solution.py:39
  70.7 5.9 %collective-permute-start.9 = (bf16[128,512]{1,0:T(8,128)(2,1)S(1)}, bf16[128,512]{1,0:T(8,128)(2,1)S(1)}, u32[]{:S(2)}, u32[]{:S(2)}) collective-permute-start(bf16[128,512]{1,0:T(8,128)(2,1)S(1)} %get-tuple-element.34), channel_id=1, source_target_pairs={{0,4},{1,5},{2,6},{3,7},{4,64},{5,65},{6,66},{7,67},{8,12},{9,13},... | collective-permute-start | bytes 393224 | tf_op jit(solution)/shard_map/ppermute | solution.py:39
  73.6 4.3 %collective-permute-start.13 = (bf16[128,512]{1,0:T(8,128)(2,1)S(1)}, bf16[128,512]{1,0:T(8,128)(2,1)S(1)}, u32[]{:S(2)}, u32[]{:S(2)}) collective-permute-start(bf16[128,512]{1,0:T(8,128)(2,1)S(1)} %collective-permute-done.10.refs_8_), channel_id=1, source_target_pairs={{0,8},{1,9},{2,10},{3,11},{4,12},{5,13},{6,14},{7,15},{8,0},{9,1},... | collective-permute-start | bytes 393224 | tf_op jit(solution)/shard_map/ppermute | solution.py:39
  76.7 2.2 %collective-permute-start.12 = (bf16[128,512]{1,0:T(8,128)(2,1)S(1)}, bf16[128,512]{1,0:T(8,128)(2,1)S(1)}, u32[]{:S(2)}, u32[]{:S(2)}) collective-permute-start(bf16[128,512]{1,0:T(8,128)(2,1)S(1)} %collective-permute-done.9.refs_7_), channel_id=1, source_target_pairs={{0,8},{1,9},{2,10},{3,11},{4,12},{5,13},{6,14},{7,15},{8,0},{9,1},... | collective-permute-start | bytes 393224 | tf_op jit(solution)/shard_map/ppermute | solution.py:39
  151.7 7.2 %collective-permute-start.14 = (bf16[2048,512]{1,0:T(8,128)(2,1)S(1)}, bf16[2048,512]{1,0:T(8,128)(2,1)S(1)}, u32[]{:S(2)}, u32[]{:S(2)}) collective-permute-start(bf16[2048,512]{1,0:T(8,128)(2,1)S(1)} %bitcast.22), channel_id=1, source_target_pairs={{0,8},{1,9},{2,10},{3,11},{4,12},{5,13},{6,14},{7,15},{8,0},{9,1},... | collective-permute-start | bytes 6291464 | tf_op jit(solution)/shard_map/ppermute | solution.py:39

commit v5 on v4

--- a/solution.py
+++ b/solution.py
@@ -83,37 +83,28 @@
 
 
 def near_kernel(low, high, weight, low_out, high_out, total):
-    rows = jnp.concatenate([low[...], high[...]], axis=0)
-    part = jnp.dot(rows, weight[...], preferred_element_type=F32)
-
-    @pl.when(pl.program_id(0) == 0)
-    def _():
-        total[...] = part
-
-    @pl.when(pl.program_id(0) > 0)
-    def _():
-        total[...] += part
-
-    @pl.when(pl.program_id(0) == pl.num_programs(0) - 1)
-    def _():
-        count = low.shape[0]
-        low_out[...] = total[:count].astype(BF)
-        high_out[...] = total[count:].astype(BF)
+    step = weight.shape[0] // 4
+    count = low.shape[0]
+    total[...] = jnp.zeros_like(total)
+
+    @pl.loop(0, 4)
+    def _(k):
+        part = pl.ds(pl.multiple_of(k * step, step), step)
+        rows = jnp.concatenate([low[:, part], high[:, part]], axis=0)
+        total[...] += jnp.dot(rows, weight[part, :], preferred_element_type=F32)
+
+    low_out[...] = total[:count].astype(BF)
+    high_out[...] = total[count:].astype(BF)
 
 
 def project_near(low, high, weight):
     rows = low.shape[0]
     half, width = weight.shape
-    step = half // 4
+    here = pl.BlockSpec(memory_space=pltpu.VMEM)
     return pl.pallas_call(
         near_kernel,
-        grid=(4,),
-        in_specs=[
-            pl.BlockSpec((rows, step), lambda i: (0, i)),
-            pl.BlockSpec((rows, step), lambda i: (0, i)),
-            pl.BlockSpec((step, width), lambda i: (i, 0)),
-        ],
-        out_specs=[pl.BlockSpec((rows, width), lambda i: (0, 0))] * 2,
+        in_specs=[here] * 3,
+        out_specs=[here] * 2,
         out_shape=[jax.ShapeDtypeStruct((rows, width), BF)] * 2,
         scratch_shapes=[pltpu.VMEM((2 * rows, width), F32)],
         compiler_params=params(12),
@@ -246,32 +237,36 @@
     )(place, lengths, queries, key_own, key_halo, weight)
 
 
-def weight_grad_kernel(count, place, *refs):
-    hidden, grads, out = refs[:count], refs[count:-1], refs[-1]
-    rows = jnp.concatenate([piece[...] for piece in hidden], axis=0)
-    grad = jnp.concatenate([piece[...] for piece in grads], axis=0)
-    total = lax.dot_general(rows, grad, (((0,), (0,)), ((), ())), preferred_element_type=F32)
-    out[...] = total.astype(BF)
-
-
-def weight_grad(place, tokens, near, swapped, grads):
-    whole = lambda i, p: (0, 0)
-    return pl.pallas_call(
-        functools.partial(weight_grad_kernel, 1 + len(near) + len(swapped)),
-        grid_spec=pltpu.PrefetchScalarGridSpec(
-            num_scalar_prefetch=1,
-            grid=(4,),
-            in_specs=[pl.BlockSpec((256, 512), lambda i, p: (0, (p[0] * 2 + p[1]) * 4 + i))]
-            + [pl.BlockSpec((v.shape[0], 512), lambda i, p: (0, p[1] * 4 + i)) for v in near]
-            + [pl.BlockSpec((v.shape[0], 512), lambda i, p: (0, i)) for v in swapped]
-            + [pl.BlockSpec(v.shape, whole) for v in grads],
-            out_specs=pl.BlockSpec((512, 512), lambda i, p: (i, 0)),
-        ),
+def weight_grad_kernel(count, far, place, *refs):
+    hidden, grads, out, grad = refs[:count], refs[count:-2], refs[-2], refs[-1]
+    grad[...] = jnp.concatenate([piece[...] for piece in grads], axis=0)
+    step = 512
+
+    @pl.loop(0, out.shape[0] // step)
+    def _(i):
+        here = pl.multiple_of(i * step, step)
+        there = pl.multiple_of(place[1] * out.shape[0] + i * step, step)
+        rows = jnp.concatenate(
+            [piece[:, pl.ds(there if far[k] else here, step)] for k, piece in enumerate(hidden)], axis=0
+        )
+        total = lax.dot_general(rows, grad[...], (((0,), (0,)), ((), ())), preferred_element_type=F32)
+        out[pl.ds(here, step), :] = total.astype(BF)
+
+
+def weight_grad(place, own, near, swapped, grads):
+    here = pl.BlockSpec(memory_space=pltpu.VMEM)
+    hidden = [own, *near, *swapped]
+    far = [False] + [True] * len(near) + [False] * len(swapped)
+    return pl.pallas_call(
+        functools.partial(weight_grad_kernel, len(hidden), far),
+        in_specs=[pl.BlockSpec(memory_space=pltpu.SMEM)] + [here] * (len(hidden) + len(grads)),
+        out_specs=here,
         out_shape=jax.ShapeDtypeStruct((2048, 512), BF),
+        scratch_shapes=[pltpu.VMEM((1024, 512), BF)],
         compiler_params=params(16),
         cost_estimate=cost(2 * 1024 * 2048 * 512, 8 << 20),
         name="weight_grad",
-    )(place, tokens, *near, *swapped, *grads)
+    )(place, *hidden, *grads)
 
 
 def sum_spread_kernel(scale, parts, out):
@@ -298,31 +293,31 @@
     )(parts)
 
 
-def copy_kernel(place, rows, *refs):
-    refs[-1][...] = rows[...]
-
-
-def write_rows(place, rows, side, held=None):
+def copy_kernel(side, first, rows, *refs):
+    out, done = refs[-2], refs[-1]
+    core = lax.axis_index("core")
+    start = (1 - core if side else core) * (out.shape[0] // 2) + first
+    start = pl.multiple_of(start, rows.shape[0])
+    copy = pltpu.make_async_copy(rows, out.at[pl.ds(start, rows.shape[0])], done)
+    copy.start()
+    copy.wait()
+
+
+def write_rows(rows, total, side, first, held=None):
     count, width = rows.shape
-    step = count // 2
-    more = {} if held is None else {"input_output_aliases": {2: 0}}
-    return pl.pallas_call(
-        copy_kernel,
-        grid_spec=pltpu.PrefetchScalarGridSpec(
-            num_scalar_prefetch=1,
-            grid=(2,),
-            in_specs=[pl.BlockSpec((step, width), lambda i, p: (i, 0))]
-            + ([] if held is None else [pl.BlockSpec(memory_space=pl.ANY)]),
-            out_specs=pl.BlockSpec(
-                (step, width), lambda i, p: ((1 - p[1] if side else p[1]) * 2 + i, 0)
-            ),
-        ),
-        out_shape=jax.ShapeDtypeStruct((2 * count, width), BF),
-        compiler_params=params(8),
+    anywhere = pl.BlockSpec(memory_space=pl.ANY)
+    given = [rows] if held is None else [rows, held]
+    return pl.pallas_call(
+        functools.partial(copy_kernel, side, first),
+        in_specs=[anywhere] * len(given),
+        out_specs=anywhere,
+        out_shape=jax.ShapeDtypeStruct((total, width), BF),
+        scratch_shapes=[pltpu.SemaphoreType.DMA],
+        input_output_aliases={} if held is None else {1: 0},
+        compiler_params=params(4),
         cost_estimate=cost(1 << 20, 4 << 20),
         name="write_rows",
-        **more,
-    )(place, rows, *([] if held is None else [held]))
+    )(*given)
 
 
 def swap_core(xh, y, core, xl, z):
@@ -359,8 +354,9 @@
         move(column(split, rows, (1 - fsdp) * half, half), backward),
     ]
     passed = [column(0, rows, fsdp * half + (1 - core) * quarter, quarter)]
+    own = column(0, rows, fsdp * half + core * quarter, quarter)
     total = project_own(place, tokens, key_weight)
-    near, total, passed = lax.optimization_barrier((near, total, passed))
+    near, total, passed, own = lax.optimization_barrier((near, total, passed, own))
     low, high = project_near(*near, key_weight)
     low, high = move(low, backward), move(high, forward)
     key_own = (total + jnp.concatenate([low, high], axis=0).astype(F32)).astype(BF)
@@ -382,12 +378,15 @@
     grads += [move(v, swap_core) for v in grad_near]
 
     chips = ("xh", "y", "z")
-    parts = weight_grad(place, tokens, near, across, grads).reshape(32, 64, width)
+    parts = weight_grad(place, own, near, across, grads).reshape(32, 64, width)
     parts = lax.all_to_all(parts, chips, split_axis=0, concat_axis=0, tiled=True)
     spread = sum_spread(parts, (rows * 16 * 8) ** (-0.5))
     final = lax.all_to_all(spread, chips, split_axis=0, concat_axis=0, tiled=True).reshape(2048, width)
-    other = move(final, swap_core)
-    grad_weight = write_rows(place, other, 1, write_rows(place, final, 0))
+    part = 1024
+    others = [move(final[k:k + part], swap_core) for k in range(0, 2048, part)]
+    grad_weight = write_rows(final, half, 0, 0)
+    for k, other in enumerate(others):
+        grad_weight = write_rows(other, half, 1, k * part, grad_weight)
     return entropy.T[None], grad_query[None], grad_weight
 
 

time: 161 us -> 160 us (level)
    pallas_call x4 -> x5, Pallas kernels: 10.1 us -> 8.68 us  [the longest x1 3.59 us: weight_grad(): pl.pallas_call(functools.partial(weight_grad_kernel, len(hidden), far), i...]
    ppermute x15 -> x16, waiting for transfers between devices: 36.2 us -> 35.6 us  [move(): return lax.ppermute(value, AXES, pairs)]
    ppermute x15 -> x16, starting transfers between devices: 23.7 us -> 23.8 us  [move(): return lax.ppermute(value, AXES, pairs)]
  transfers between devices with their start and end apart: 15 -> 16, of which waited for: 9 -> 10; matrix products, arithmetic and copies ran while one was open for 0% -> 0% of each run, Pallas kernels for 10% -> 10%
where the time goes in v5:
time: 160 us; the launch traced here: 159 us
  blocking collectives  68.1 us (43%)
  waiting for transfers between devices  35.6 us (22%)
  starting transfers between devices  23.8 us (15%)
  Pallas kernels  23.3 us (15%)
  local copies, waits for them, and re-layouts  7.65 us (5%)
    all_to_all x1, blocking collectives, shards(): lax.all_to_all(parts, chips, split_axis=0, concat_axis=0, tiled=True)  36 us
    ppermute x16, waiting for transfers between devices, move(): return lax.ppermute(value, AXES, pairs)  35.6 us
    all_to_all x1, blocking collectives, shards(): lax.all_to_all(spread, chips, split_axis=0, concat_axis=0, tiled=True)  32.1 us
    ppermute x16, starting transfers between devices, move(): return lax.ppermute(value, AXES, pairs)  23.8 us
    pallas_call x1, Pallas kernels, attend(): pl.pallas_call(attend_kernel, grid_spec=pltpu.PrefetchScalarGridSpec(num_...  11.2 us
    unnamed x14, local copies, waits for them, and re-layouts  4.4 us
    pallas_call x1, Pallas kernels, weight_grad(): pl.pallas_call(functools.partial(weight_grad_kernel, len(hidden), far), i...  3.59 us
    pallas_call x3, Pallas kernels, write_rows(): pl.pallas_call(functools.partial(copy_kernel, side, first), in_specs=[any...  3.28 us
  transfers between devices with their start and end apart: 16, of which 10 were waited for; matrix products, arithmetic and copies ran while one was open for 0% of the time, Pallas kernels for 10%

profile of v5, /device:TPU:1, one launch (start us, length us, event | category | flops | bytes accessed | tf_op | source)
XLA Modules:
  0.0 159.4 jit_solution(14743787305870897745)
XLA Ops:
  0.6 2.7 %dynamic-slice_bitcast_fusion.2 = (bf16[128,4096]{1,0:T(8,128)(2,1)}, bf16[128,4096]{1,0:T(8,128)(2,1)S(1)}) fusion(bf16[1,256,8192]{2,1,0:T(8,128)(2,1)} %param.6, s32[]{:T(128)S(6)} %select_n.14), kind=kLoop, calls=%fused_computation.2 | loop fusion | bytes 4194308 | tf_op jit(solution)/shard_map/dynamic_slice | solution.py:350
  3.3 3.3 %collective-permute-start.1 = (bf16[128,4096]{1,0:T(8,128)(2,1)}, bf16[128,4096]{1,0:T(8,128)(2,1)S(1)}, u32[]{:S(2)}, u32[]{:S(2)}) collective-permute-start(bf16[128,4096]{1,0:T(8,128)(2,1)} %get-tuple-element.35), channel_id=1, source_target_pairs={{0,68},{1,69},{2,70},{3,71},{4,0},{5,1},{6,2},{7,3},{8,76},{9,77},... | collective-permute-start | bytes 3145736 | tf_op jit(solution)/shard_map/ppermute | solution.py:39
  6.6 0.0 collective-permute-start
  6.6 0.1 pad_add_fusion.place
  6.7 0.0 copy-start
  6.7 2.2 %copy-done = bf16[1,256,8192]{2,1,0:T(8,128)(2,1)S(1)} copy-done((bf16[1,256,8192]{2,1,0:T(8,128)(2,1)S(1)}, bf16[1,256,8192]{2,1,0:T(8,128)(2,1)}, u32[]{:S(2)}) %copy-start) | copy-done | bytes 4194328
  8.9 0.0 copy-start.2
  8.9 2.2 %copy-done.2 = bf16[4096,512]{1,0:T(8,128)(2,1)S(1)} copy-done((bf16[4096,512]{1,0:T(8,128)(2,1)S(1)}, bf16[4096,512]{1,0:T(8,128)(2,1)}, u32[]{:S(2)}) %copy-start.2) | copy-done | bytes 4194328
  11.1 0.0 copy-start.1
  11.1 2.6 %project_own.1 = f32[256,512]{1,0:T(8,128)S(1)} custom-call(s32[3]{0:T(128)S(1)} %pad_add_fusion.place, bf16[256,8192]{1,0:T(8,128)(2,1)S(1)} %bitcast.25, bf16[4096,512]{1,0:T(8,128)(2,1)S(1)} %copy-done.2), custom_call_target="tpu_custom_call" | custom-call | flops 1073741824 | bytes 6291456 | tf_op jit(solution)/shard_map/project_own/pallas_call | solution.py:67
  13.7 0.0 copy-done.1
  13.7 0.0 copy-start.3
  13.7 0.2 dynamic-slice_bitcast_fusion
  13.9 14.8 %collective-permute-done.1.high.refs_2_ = bf16[128,4096]{1,0:T(8,128)(2,1)S(1)} collective-permute-done((bf16[128,4096]{1,0:T(8,128)(2,1)}, bf16[128,4096]{1,0:T(8,128)(2,1)S(1)}, u32[]{:S(2)}, u32[]{:S(2)}) %collective-permute-start.1) | collective-permute-done | bytes 1048608 | tf_op jit(solution)/shard_map/ppermute | solution.py:39
  28.8 2.8 %collective-permute-done.low.refs_1_ = bf16[128,4096]{1,0:T(8,128)(2,1)S(1)} collective-permute-done((bf16[128,4096]{1,0:T(8,128)(2,1)S(1)}, bf16[128,4096]{1,0:T(8,128)(2,1)S(1)}, u32[]{:S(2)}, u32[]{:S(2)}) %collective-permute-start) | collective-permute-done | bytes 1048608 | tf_op jit(solution)/shard_map/ppermute | solution.py:39
  31.6 0.0 copy-done.3
  31.6 0.0 copy-start.4
  31.6 0.0 copy-start.5
  31.6 0.0 copy-start.6
  31.6 1.8 %project_near.1 = (bf16[128,512]{1,0:T(8,128)(2,1)S(1)}, bf16[128,512]{1,0:T(8,128)(2,1)S(1)}) custom-call(bf16[128,4096]{1,0:T(8,128)(2,1)S(1)} %collective-permute-done.low.refs_1_, bf16[128,4096]{1,0:T(8,128)(2,1)S(1)} %collective-permute-done.1.high.refs_2_, bf16[4096,512]{1,0:T(8,128)(2,1)S(1)} %copy-done.3), custom_call_target="tpu_custom_call" | custom-call | flops 1073741824 | bytes 6291456 | tf_op jit(solution)/shard_map/project_near/pallas_call | solution.py:104
  33.4 0.6 collective-permute-start.2
  34.0 0.9 collective-permute-start.3
  34.9 2.4 %collective-permute-start.5 = (bf16[256,2048]{1,0:T(8,128)(2,1)S(1)}, bf16[256,2048]{1,0:T(8,128)(2,1)S(1)}, u32[]{:S(2)}, u32[]{:S(2)}) collective-permute-start(bf16[256,2048]{1,0:T(8,128)(2,1)S(1)} %get-tuple-element.27), channel_id=1, source_target_pairs={{0,8},{1,9},{2,10},{3,11},{4,12},{5,13},{6,14},{7,15},{8,0},{9,1},... | collective-permute-start | bytes 3145736 | tf_op jit(solution)/shard_map/ppermute | solution.py:39
  37.4 0.0 collective-permute-done.2
  37.4 1.6 %collective-permute-done.3 = bf16[128,512]{1,0:T(8,128)(2,1)S(1)} collective-permute-done((bf16[128,512]{1,0:T(8,128)(2,1)S(1)}, bf16[128,512]{1,0:T(8,128)(2,1)S(1)}, u32[]{:S(2)}, u32[]{:S(2)}) %collective-permute-start.3) | collective-permute-done | bytes 131104 | tf_op jit(solution)/shard_map/ppermute | solution.py:39
  39.0 0.1 add_convert_fusion.1.key_own
  39.1 6.1 %collective-permute-start.4 = (bf16[256,512]{1,0:T(8,128)(2,1)S(1)}, bf16[256,512]{1,0:T(8,128)(2,1)S(1)}, u32[]{:S(2)}, u32[]{:S(2)}) collective-permute-start(bf16[256,512]{1,0:T(8,128)(2,1)S(1)} %add_convert_fusion.1.key_own), channel_id=1, source_target_pairs={{0,8},{1,9},{2,10},{3,11},{4,12},{5,13},{6,14},{7,15},{8,16},{9,17... | collective-permute-start | bytes 786440 | tf_op jit(solution)/shard_map/ppermute | solution.py:39
  45.2 0.1 collective-permute-start.7
  45.3 0.5 collective-permute-start.6
  45.8 2.7 %collective-permute-done.4.key_halo = bf16[256,512]{1,0:T(8,128)(2,1)S(1)} collective-permute-done((bf16[256,512]{1,0:T(8,128)(2,1)S(1)}, bf16[256,512]{1,0:T(8,128)(2,1)S(1)}, u32[]{:S(2)}, u32[]{:S(2)}) %collective-permute-start.4) | collective-permute-done | bytes 262176 | tf_op jit(solution)/shard_map/ppermute | solution.py:39
  48.5 0.0 copy-done.4
  48.5 0.0 copy-done.5
  48.5 0.0 copy-done.6
  48.5 11.2 %attend.1 = (f32[32,256]{1,0:T(8,128)}, bf16[256,4096]{1,0:T(8,128)(2,1)}, f32[256,512]{1,0:T(8,128)S(1)}, bf16[256,512]{1,0:T(8,128)(2,1)S(1)}) custom-call(s32[3]{0:T(128)S(1)} %pad_add_fusion.place, s32[1,32]{1,0:T(1,128)S(1)} %copy-done.6, bf16[256,4096]{1,0:T(8,128)(2,1)S(1)} %bitcast.27, bf16[256,512]{1,0:T(8,128)(2,1)S(1)} %add_convert_fusion.1.key_own, ...), custom_call_target="tpu_custom_call" | custom-call | flops 4294967296 | bytes 6291456 | tf_op jit(solution)/shard_map/attend/pallas_call | solution.py:205
  59.7 0.0 collective-permute-done.7.refs_5_
  59.7 0.0 collective-permute-done.6.refs_4_
  59.7 0.0 collective-permute-done.5.refs_3_
  59.7 1.9 %collective-permute-start.8 = (bf16[256,512]{1,0:T(8,128)(2,1)S(1)}, bf16[256,512]{1,0:T(8,128)(2,1)S(1)}, u32[]{:S(2)}, u32[]{:S(2)}) collective-permute-start(bf16[256,512]{1,0:T(8,128)(2,1)S(1)} %get-tuple-element.32), channel_id=1, source_target_pairs={{8,0},{9,1},{10,2},{11,3},{12,4},{13,5},{14,6},{15,7},{16,8},{17,9... | collective-permute-start | bytes 786440 | tf_op jit(solution)/shard_map/ppermute | solution.py:39
  61.7 6.5 %collective-permute-done.8 = bf16[256,512]{1,0:T(8,128)(2,1)S(1)} collective-permute-done((bf16[256,512]{1,0:T(8,128)(2,1)S(1)}, bf16[256,512]{1,0:T(8,128)(2,1)S(1)}, u32[]{:S(2)}, u32[]{:S(2)}) %collective-permute-start.8) | collective-permute-done | bytes 262176 | tf_op jit(solution)/shard_map/ppermute | solution.py:39
  68.2 0.1 add_convert_fusion.refs_6_
  68.3 0.1 collective-permute-start.11
  68.4 2.0 %collective-permute-start.10 = (bf16[128,512]{1,0:T(8,128)(2,1)S(1)}, bf16[128,512]{1,0:T(8,128)(2,1)S(1)}, u32[]{:S(2)}, u32[]{:S(2)}) collective-permute-start(bf16[128,512]{1,0:T(8,128)(2,1)S(1)} %get-tuple-element.39), channel_id=1, source_target_pairs={{0,68},{1,69},{2,70},{3,71},{4,0},{5,1},{6,2},{7,3},{8,76},{9,77},... | collective-permute-start | bytes 393224 | tf_op jit(solution)/shard_map/ppermute | solution.py:39
  70.3 0.0 collective-permute-start.9
  70.3 2.8 %collective-permute-done.10.refs_8_ = bf16[128,512]{1,0:T(8,128)(2,1)S(1)} collective-permute-done((bf16[128,512]{1,0:T(8,128)(2,1)S(1)}, bf16[128,512]{1,0:T(8,128)(2,1)S(1)}, u32[]{:S(2)}, u32[]{:S(2)}) %collective-permute-start.10) | collective-permute-done | bytes 131104 | tf_op jit(solution)/shard_map/ppermute | solution.py:39
  73.2 1.2 collective-permute-start.13
  74.4 1.9 %collective-permute-done.9.refs_7_ = bf16[128,512]{1,0:T(8,128)(2,1)S(1)} collective-permute-done((bf16[128,512]{1,0:T(8,128)(2,1)S(1)}, bf16[128,512]{1,0:T(8,128)(2,1)S(1)}, u32[]{:S(2)}, u32[]{:S(2)}) %collective-permute-start.9) | collective-permute-done | bytes 131104 | tf_op jit(solution)/shard_map/ppermute | solution.py:39
  76.3 1.2 collective-permute-start.12
  77.5 0.0 collective-permute-done.11.refs_9_
  77.5 0.0 collective-permute-done.13.refs_11_
  77.5 1.0 collective-permute-done.12.refs_10_
  78.5 3.6 %weight_grad.1 = bf16[2048,512]{1,0:T(8,128)(2,1)S(1)} custom-call(s32[3]{0:T(128)S(1)} %pad_add_fusion.place, bf16[256,2048]{1,0:T(8,128)(2,1)S(1)} %get-tuple-element.25.refs_0_, bf16[128,4096]{1,0:T(8,128)(2,1)S(1)} %collective-permute-done.low.refs_1_, bf16[128,4096]{1,0:T(8,128)(2,1)S(1)} %collective-permute-done.1.high.refs_2_, ...), custom_call_target="tpu_custom_call" | custom-call | flops 2147483648 | bytes 8388608 | tf_op jit(solution)/shard_map/weight_grad/pallas_call | solution.py:260
  82.1 36.0 %all_to_all.10.parts = bf16[32,64,512]{2,1,0:T(8,128)(2,1)S(1)} all-to-all(bf16[32,64,512]{2,1,0:T(8,128)(2,1)S(1)} %bitcast.26), channel_id=1, replica_groups=mesh['xh'=2,'y'=4,'core'=2,'xl'=2,'z'=4] {'xh','y','z'}, dimensions={0} | all-to-all | bytes 4194304 | tf_op jit(solution)/shard_map/all_to_all | solution.py:382
  118.1 0.8 sum_spread.1
  118.9 32.1 %all_to_all.11 = bf16[32,64,512]{2,1,0:T(8,128)(2,1)S(1)} all-to-all(bf16[32,64,512]{2,1,0:T(8,128)(2,1)S(1)} %sum_spread.1), channel_id=1, replica_groups=mesh['xh'=2,'y'=4,'core'=2,'xl'=2,'z'=4] {'xh','y','z'}, dimensions={0} | all-to-all | bytes 4194304 | tf_op jit(solution)/shard_map/all_to_all | solution.py:384
  151.0 0.2 fusion
  151.2 3.5 %collective-permute-start.15 = (bf16[1024,512]{1,0:T(8,128)(2,1)S(1)}, bf16[1024,512]{1,0:T(8,128)(2,1)S(1)}, u32[]{:S(2)}, u32[]{:S(2)}) collective-permute-start(bf16[1024,512]{1,0:T(8,128)(2,1)S(1)} %bitcast.30), channel_id=1, source_target_pairs={{0,8},{1,9},{2,10},{3,11},{4,12},{5,13},{6,14},{7,15},{8,0},{9,1},... | collective-permute-start | bytes 3145736 | tf_op jit(solution)/shard_map/ppermute | solution.py:39
  154.7 0.1 collective-permute-start.14
  154.8 1.3 write_rows.3.refs_0_
  156.1 0.9 collective-permute-done.15.rows
  157.0 1.0 write_rows.4.refs_0_
  158.0 0.5 collective-permute-done.14.rows
  158.5 1.0 write_rows.5
  (3 shorter events, 0.1 us)
Async XLA Ops:
  3.3 25.5 %collective-permute-start.1 = (bf16[128,4096]{1,0:T(8,128)(2,1)}, bf16[128,4096]{1,0:T(8,128)(2,1)S(1)}, u32[]{:S(2)}, u32[]{:S(2)}) collective-permute-start(bf16[128,4096]{1,0:T(8,128)(2,1)} %get-tuple-element.35), channel_id=1, source_target_pairs={{0,68},{1,69},{2,70},{3,71},{4,0},{5,1},{6,2},{7,3},{8,76},{9,77},... | collective-permute-start | bytes 3145736 | tf_op jit(solution)/shard_map/ppermute | solution.py:39
  6.6 24.9 %collective-permute-start = (bf16[128,4096]{1,0:T(8,128)(2,1)S(1)}, bf16[128,4096]{1,0:T(8,128)(2,1)S(1)}, u32[]{:S(2)}, u32[]{:S(2)}) collective-permute-start(bf16[128,4096]{1,0:T(8,128)(2,1)S(1)} %get-tuple-element.36), channel_id=1, source_target_pairs={{0,4},{1,5},{2,6},{3,7},{4,64},{5,65},{6,66},{7,67},{8,12},{9,13},... | collective-permute-start | bytes 3145736 | tf_op jit(solution)/shard_map/ppermute | solution.py:39
  6.7 2.2 %copy-start = (bf16[1,256,8192]{2,1,0:T(8,128)(2,1)S(1)}, bf16[1,256,8192]{2,1,0:T(8,128)(2,1)}, u32[]{:S(2)}) copy-start(bf16[1,256,8192]{2,1,0:T(8,128)(2,1)} %param.6) | copy-start | bytes 12582916
  8.9 2.2 %copy-start.2 = (bf16[4096,512]{1,0:T(8,128)(2,1)S(1)}, bf16[4096,512]{1,0:T(8,128)(2,1)}, u32[]{:S(2)}) copy-start(bf16[4096,512]{1,0:T(8,128)(2,1)} %weight.3) | copy-start | bytes 12582916
  11.1 2.6 %copy-start.1 = (bf16[1,256,8192]{2,1,0:T(8,128)(2,1)S(1)}, bf16[1,256,8192]{2,1,0:T(8,128)(2,1)}, u32[]{:S(2)}) copy-start(bf16[1,256,8192]{2,1,0:T(8,128)(2,1)} %param.6) | copy-start | bytes 12582916
  13.7 17.9 %copy-start.3 = (bf16[4096,512]{1,0:T(8,128)(2,1)S(1)}, bf16[4096,512]{1,0:T(8,128)(2,1)}, u32[]{:S(2)}) copy-start(bf16[4096,512]{1,0:T(8,128)(2,1)} %weight.3) | copy-start | bytes 12582916
  31.6 16.9 %copy-start.4 = (bf16[1,256,4096]{2,1,0:T(8,128)(2,1)S(1)}, bf16[1,256,4096]{2,1,0:T(8,128)(2,1)}, u32[]{:S(2)}) copy-start(bf16[1,256,4096]{2,1,0:T(8,128)(2,1)} %param.5) | copy-start | bytes 6291460
  31.6 16.9 %copy-start.5 = (bf16[1,256,32]{1,2,0:T(8,128)(2,1)S(1)}, bf16[1,256,32]{1,2,0:T(8,128)(2,1)}, u32[]{:S(2)}) copy-start(bf16[1,256,32]{1,2,0:T(8,128)(2,1)} %param.9) | copy-start | bytes 49156
  31.6 16.9 %copy-start.6 = (s32[1,32]{1,0:T(1,128)S(1)}, s32[1,32]{1,0:T(1,128)}, u32[]{:S(2)}) copy-start(s32[1,32]{1,0:T(1,128)} %lengths.1) | copy-start | bytes 388
  33.4 4.0 %collective-permute-start.2 = (bf16[128,512]{1,0:T(8,128)(2,1)S(1)}, bf16[128,512]{1,0:T(8,128)(2,1)S(1)}, u32[]{:S(2)}, u32[]{:S(2)}) collective-permute-start(bf16[128,512]{1,0:T(8,128)(2,1)S(1)} %get-tuple-element.21), channel_id=1, source_target_pairs={{0,68},{1,69},{2,70},{3,71},{4,0},{5,1},{6,2},{7,3},{8,76},{9,77},... | collective-permute-start | bytes 393224 | tf_op jit(solution)/shard_map/ppermute | solution.py:39
  34.0 5.0 %collective-permute-start.3 = (bf16[128,512]{1,0:T(8,128)(2,1)S(1)}, bf16[128,512]{1,0:T(8,128)(2,1)S(1)}, u32[]{:S(2)}, u32[]{:S(2)}) collective-permute-start(bf16[128,512]{1,0:T(8,128)(2,1)S(1)} %get-tuple-element.22), channel_id=1, source_target_pairs={{0,4},{1,5},{2,6},{3,7},{4,64},{5,65},{6,66},{7,67},{8,12},{9,13},... | collective-permute-start | bytes 393224 | tf_op jit(solution)/shard_map/ppermute | solution.py:39
  34.9 24.8 %collective-permute-start.5 = (bf16[256,2048]{1,0:T(8,128)(2,1)S(1)}, bf16[256,2048]{1,0:T(8,128)(2,1)S(1)}, u32[]{:S(2)}, u32[]{:S(2)}) collective-permute-start(bf16[256,2048]{1,0:T(8,128)(2,1)S(1)} %get-tuple-element.27), channel_id=1, source_target_pairs={{0,8},{1,9},{2,10},{3,11},{4,12},{5,13},{6,14},{7,15},{8,0},{9,1},... | collective-permute-start | bytes 3145736 | tf_op jit(solution)/shard_map/ppermute | solution.py:39
  39.1 9.4 %collective-permute-start.4 = (bf16[256,512]{1,0:T(8,128)(2,1)S(1)}, bf16[256,512]{1,0:T(8,128)(2,1)S(1)}, u32[]{:S(2)}, u32[]{:S(2)}) collective-permute-start(bf16[256,512]{1,0:T(8,128)(2,1)S(1)} %add_convert_fusion.1.key_own), channel_id=1, source_target_pairs={{0,8},{1,9},{2,10},{3,11},{4,12},{5,13},{6,14},{7,15},{8,16},{9,17... | collective-permute-start | bytes 786440 | tf_op jit(solution)/shard_map/ppermute | solution.py:39
  45.2 14.5 %collective-permute-start.7 = (bf16[128,2048]{1,0:T(8,128)(2,1)S(1)}, bf16[128,2048]{1,0:T(8,128)(2,1)S(1)}, u32[]{:S(2)}, u32[]{:S(2)}) collective-permute-start(bf16[128,2048]{1,0:T(8,128)(2,1)S(1)} %constant_dynamic-slice_fusion), channel_id=1, source_target_pairs={{0,8},{1,9},{2,10},{3,11},{4,12},{5,13},{6,14},{7,15},{8,0},{9,1},... | collective-permute-start | bytes 1572872 | tf_op jit(solution)/shard_map/ppermute | solution.py:39
  45.3 14.4 %collective-permute-start.6 = (bf16[128,2048]{1,0:T(8,128)(2,1)S(1)}, bf16[128,2048]{1,0:T(8,128)(2,1)S(1)}, u32[]{:S(2)}, u32[]{:S(2)}) collective-permute-start(bf16[128,2048]{1,0:T(8,128)(2,1)S(1)} %constant_dynamic-slice_fusion.1), channel_id=1, source_target_pairs={{0,8},{1,9},{2,10},{3,11},{4,12},{5,13},{6,14},{7,15},{8,0},{9,1},... | collective-permute-start | bytes 1572872 | tf_op jit(solution)/shard_map/ppermute | solution.py:39
  59.7 8.4 %collective-permute-start.8 = (bf16[256,512]{1,0:T(8,128)(2,1)S(1)}, bf16[256,512]{1,0:T(8,128)(2,1)S(1)}, u32[]{:S(2)}, u32[]{:S(2)}) collective-permute-start(bf16[256,512]{1,0:T(8,128)(2,1)S(1)} %get-tuple-element.32), channel_id=1, source_target_pairs={{8,0},{9,1},{10,2},{11,3},{12,4},{13,5},{14,6},{15,7},{16,8},{17,9... | collective-permute-start | bytes 786440 | tf_op jit(solution)/shard_map/ppermute | solution.py:39
  68.3 9.2 %collective-permute-start.11 = (bf16[256,512]{1,0:T(8,128)(2,1)S(1)}, bf16[256,512]{1,0:T(8,128)(2,1)S(1)}, u32[]{:S(2)}, u32[]{:S(2)}) collective-permute-start(bf16[256,512]{1,0:T(8,128)(2,1)S(1)} %add_convert_fusion.refs_6_), channel_id=1, source_target_pairs={{0,8},{1,9},{2,10},{3,11},{4,12},{5,13},{6,14},{7,15},{8,0},{9,1},... | collective-permute-start | bytes 786440 | tf_op jit(solution)/shard_map/ppermute | solution.py:39
  68.4 4.8 %collective-permute-start.10 = (bf16[128,512]{1,0:T(8,128)(2,1)S(1)}, bf16[128,512]{1,0:T(8,128)(2,1)S(1)}, u32[]{:S(2)}, u32[]{:S(2)}) collective-permute-start(bf16[128,512]{1,0:T(8,128)(2,1)S(1)} %get-tuple-element.39), channel_id=1, source_target_pairs={{0,68},{1,69},{2,70},{3,71},{4,0},{5,1},{6,2},{7,3},{8,76},{9,77},... | collective-permute-start | bytes 393224 | tf_op jit(solution)/shard_map/ppermute | solution.py:39
  70.3 5.9 %collective-permute-start.9 = (bf16[128,512]{1,0:T(8,128)(2,1)S(1)}, bf16[128,512]{1,0:T(8,128)(2,1)S(1)}, u32[]{:S(2)}, u32[]{:S(2)}) collective-permute-start(bf16[128,512]{1,0:T(8,128)(2,1)S(1)} %get-tuple-element.40), channel_id=1, source_target_pairs={{0,4},{1,5},{2,6},{3,7},{4,64},{5,65},{6,66},{7,67},{8,12},{9,13},... | collective-permute-start | bytes 393224 | tf_op jit(solution)/shard_map/ppermute | solution.py:39
  73.2 4.3 %collective-permute-start.13 = (bf16[128,512]{1,0:T(8,128)(2,1)S(1)}, bf16[128,512]{1,0:T(8,128)(2,1)S(1)}, u32[]{:S(2)}, u32[]{:S(2)}) collective-permute-start(bf16[128,512]{1,0:T(8,128)(2,1)S(1)} %collective-permute-done.10.refs_8_), channel_id=1, source_target_pairs={{0,8},{1,9},{2,10},{3,11},{4,12},{5,13},{6,14},{7,15},{8,0},{9,1},... | collective-permute-start | bytes 393224 | tf_op jit(solution)/shard_map/ppermute | solution.py:39
  76.3 2.2 %collective-permute-start.12 = (bf16[128,512]{1,0:T(8,128)(2,1)S(1)}, bf16[128,512]{1,0:T(8,128)(2,1)S(1)}, u32[]{:S(2)}, u32[]{:S(2)}) collective-permute-start(bf16[128,512]{1,0:T(8,128)(2,1)S(1)} %collective-permute-done.9.refs_7_), channel_id=1, source_target_pairs={{0,8},{1,9},{2,10},{3,11},{4,12},{5,13},{6,14},{7,15},{8,0},{9,1},... | collective-permute-start | bytes 393224 | tf_op jit(solution)/shard_map/ppermute | solution.py:39
  151.2 5.8 %collective-permute-start.15 = (bf16[1024,512]{1,0:T(8,128)(2,1)S(1)}, bf16[1024,512]{1,0:T(8,128)(2,1)S(1)}, u32[]{:S(2)}, u32[]{:S(2)}) collective-permute-start(bf16[1024,512]{1,0:T(8,128)(2,1)S(1)} %bitcast.30), channel_id=1, source_target_pairs={{0,8},{1,9},{2,10},{3,11},{4,12},{5,13},{6,14},{7,15},{8,0},{9,1},... | collective-permute-start | bytes 3145736 | tf_op jit(solution)/shard_map/ppermute | solution.py:39
  154.7 3.8 %collective-permute-start.14 = (bf16[1024,512]{1,0:T(8,128)(2,1)S(1)}, bf16[1024,512]{1,0:T(8,128)(2,1)S(1)}, u32[]{:S(2)}, u32[]{:S(2)}) collective-permute-start(bf16[1024,512]{1,0:T(8,128)(2,1)S(1)} %bitcast.29), channel_id=1, source_target_pairs={{0,8},{1,9},{2,10},{3,11},{4,12},{5,13},{6,14},{7,15},{8,0},{9,1},... | collective-permute-start | bytes 3145736 | tf_op jit(solution)/shard_map/ppermute | solution.py:39

commit v6 on v5

--- a/solution.py
+++ b/solution.py
@@ -113,8 +113,15 @@
     )(low, high, weight)
 
 
+TILE = 64
+WINDOW = 256 + TILE
+STACK = 256 // TILE
+
+
 def attend_kernel(place, lengths, query, key_own, key_halo, weight, entropy, grad_query, grad_own,
-                  grad_halo, bias, keys, keys_t):
+                  grad_halo, bias, keys, keys_t, total):
+    tiles = 256 // TILE
+
     @pl.when(pl.program_id(0) == 0)
     def _():
         base = place[2] * 256
@@ -128,59 +135,60 @@
         _, first = lax.fori_loop(
             0, lengths.shape[1], add, (jnp.int32(0), jnp.zeros((8, 256), jnp.int32))
         )
-        for half in range(2):
-            begin = first[0:1, half * 128:(half + 1) * 128]
-            here = position[0:1, half * 128:(half + 1) * 128]
-            there = base - 256 + half * 128 + lax.broadcasted_iota(jnp.int32, (384, 128), 0)
-            seen = (there >= begin) & (there <= here)
-            value = jnp.where(seen, 0.0, NEG)
-            bias[half, :, 0:128] = value
-            bias[half, :, 128:256] = value
+        for tile in range(tiles):
+            rows = slice(tile * TILE, (tile + 1) * TILE)
+            begin = jnp.concatenate([first[0:1, rows]] * STACK, axis=1)
+            here = jnp.concatenate([position[0:1, rows]] * STACK, axis=1)
+            there = base - 256 + tile * TILE + lax.broadcasted_iota(jnp.int32, (WINDOW, 256), 0)
+            bias[tile] = jnp.where((there >= begin) & (there <= here), 0.0, NEG)
 
     keys[0:256, :] = key_halo[...]
     keys[256:512, :] = key_own[...]
-    keys_t[...] = keys[...].T
+    keys_t[0] = keys[...].T
+    keys_t[1, :, 0:512 - TILE] = keys[TILE:512, :].T
     weights = weight[...].astype(F32)
-    def score(pair, half):
-        cols = [slice((2 * pair + k) * HD, (2 * pair + k + 1) * HD) for k in range(2)]
-        rows = slice(half * 128, (half + 1) * 128)
-        window = slice(half * 128, half * 128 + 384)
-        stack = jnp.concatenate([query[rows, cols[0]], query[rows, cols[1]]], axis=0)
+    total[...] = jnp.zeros_like(total)
+
+    def score(group, tile):
+        rows = slice(tile * TILE, (tile + 1) * TILE)
+        window = slice(tile * TILE, tile * TILE + WINDOW)
+        heads = range(group * STACK, (group + 1) * STACK)
+        stack = jnp.concatenate([query[rows, h * HD:(h + 1) * HD] for h in heads], axis=0)
         raw = lax.dot_general(
             keys[window, :], stack, (((1,), (1,)), ((), ())), preferred_element_type=F32
-        ) + bias[half]
+        ) + bias[tile]
         return raw, stack
 
-    def soften(pair, half, raw):
-        rows = slice(half * 128, (half + 1) * 128)
+    def soften(group, tile, raw):
+        rows = slice(tile * TILE, (tile + 1) * TILE)
+        heads = range(group * STACK, (group + 1) * STACK)
         top = jnp.max(raw, axis=0, keepdims=True)
         gap = raw - top
         power = jnp.exp2(gap * EXP_SCALE)
         den = jnp.sum(power, axis=0, keepdims=True)
         mean = jnp.sum(power * gap, axis=0, keepdims=True) / den
-        row_weight = jnp.concatenate(
-            [weights[2 * pair:2 * pair + 1, rows], weights[2 * pair + 1:2 * pair + 2, rows]], axis=1
-        )
+        row_weight = jnp.concatenate([weights[h:h + 1, rows] for h in heads], axis=1)
         slope_b = row_weight * FACTOR / den
         slope_a = slope_b * mean
         level = jnp.log(den) - FACTOR * mean
-        entropy[2 * pair:2 * pair + 1, rows] = level[:, 0:128]
-        entropy[2 * pair + 1:2 * pair + 2, rows] = level[:, 128:256]
+        for k, h in enumerate(heads):
+            entropy[h:h + 1, rows] = level[:, k * TILE:(k + 1) * TILE]
         return (power * (slope_a - slope_b * gap)).astype(BF)
 
-    def grads(pair, half, slope, stack):
-        cols = [slice((2 * pair + k) * HD, (2 * pair + k + 1) * HD) for k in range(2)]
-        rows = slice(half * 128, (half + 1) * 128)
-        window = slice(half * 128, half * 128 + 384)
-        turned = jnp.dot(keys_t[:, window], slope, preferred_element_type=F32) * FACTOR
+    def grads(group, tile, slope, stack):
+        rows = slice(tile * TILE, (tile + 1) * TILE)
+        start = tile // 2 * 2 * TILE
+        turned = jnp.dot(
+            keys_t[tile % 2, :, start:start + WINDOW], slope, preferred_element_type=F32
+        ) * FACTOR
         straight = turned.T.astype(BF)
-        grad_query[rows, cols[0]] = straight[0:128]
-        grad_query[rows, cols[1]] = straight[128:256]
-        part = jnp.dot(slope, stack, preferred_element_type=F32)
-        sums[half] = part if sums[half] is None else sums[half] + part
-
-    sums = [None, None]
-    order = [(pair, half) for pair in range(GROUP // 2) for half in range(2)]
+        for k in range(STACK):
+            h = group * STACK + k
+            grad_query[rows, h * HD:(h + 1) * HD] = straight[k * TILE:(k + 1) * TILE]
+        window = slice(tile * TILE, tile * TILE + WINDOW)
+        total[window, :] += jnp.dot(slope, stack, preferred_element_type=F32)
+
+    order = [(group, tile) for group in range(GROUP // STACK) for tile in range(tiles)]
     ahead = score(*order[0])
     last = None
     for i, at in enumerate(order):
@@ -191,11 +199,8 @@
             grads(*last)
         last = (*at, soften(*at, raw), stack)
     grads(*last)
-    low, high = sums
-    grad_halo[0:128, :] = (low[0:128] * FACTOR).astype(grad_halo.dtype)
-    grad_halo[128:256, :] = ((low[128:256] + high[0:128]) * FACTOR).astype(grad_halo.dtype)
-    grad_own[0:128, :] = (low[256:384] + high[128:256]) * FACTOR
-    grad_own[128:256, :] = high[256:384] * FACTOR
+    grad_halo[...] = (total[0:256, :] * FACTOR).astype(grad_halo.dtype)
+    grad_own[...] = total[256:512, :] * FACTOR
 
 
 def attend(place, lengths, queries, key_own, key_halo, weight):
@@ -220,9 +225,10 @@
                 pl.BlockSpec((rows, HD), by_head),
             ],
             scratch_shapes=[
-                pltpu.VMEM((2, 384, 256), F32),
+                pltpu.VMEM((256 // TILE, WINDOW, 256), F32),
                 pltpu.VMEM((512, HD), BF),
-                pltpu.VMEM((HD, 512), BF),
+                pltpu.VMEM((2, HD, 512), BF),
+                pltpu.VMEM((512, HD), F32),
             ],
         ),
         out_shape=[

time: 160 us -> 159 us (level)
  transfers between devices with their start and end apart: 16 -> 16, of which waited for: 10 -> 10; matrix products, arithmetic and copies ran while one was open for 0% -> 0% of each run, Pallas kernels for 10% -> 9%
where the time goes in v6:
time: 159 us; the launch traced here: 158 us
  blocking collectives  68.1 us (43%)
  waiting for transfers between devices  35.6 us (22%)
  starting transfers between devices  23.8 us (15%)
  Pallas kernels  22.2 us (14%)
  local copies, waits for them, and re-layouts  7.65 us (5%)
    all_to_all x1, blocking collectives, shards(): lax.all_to_all(parts, chips, split_axis=0, concat_axis=0, tiled=True)  36 us
    ppermute x16, waiting for transfers between devices, move(): return lax.ppermute(value, AXES, pairs)  35.6 us
    all_to_all x1, blocking collectives, shards(): lax.all_to_all(spread, chips, split_axis=0, concat_axis=0, tiled=True)  32.1 us
    ppermute x16, starting transfers between devices, move(): return lax.ppermute(value, AXES, pairs)  23.8 us
    pallas_call x1, Pallas kernels, attend(): pl.pallas_call(attend_kernel, grid_spec=pltpu.PrefetchScalarGridSpec(num_...  10.1 us
    unnamed x14, local copies, waits for them, and re-layouts  4.4 us
    pallas_call x1, Pallas kernels, weight_grad(): pl.pallas_call(functools.partial(weight_grad_kernel, len(hidden), far), i...  3.6 us
    pallas_call x3, Pallas kernels, write_rows(): pl.pallas_call(functools.partial(copy_kernel, side, first), in_specs=[any...  3.28 us
  transfers between devices with their start and end apart: 16, of which 10 were waited for; matrix products, arithmetic and copies ran while one was open for 0% of the time, Pallas kernels for 9%

profile of v6, /device:TPU:1, one launch (start us, length us, event | category | flops | bytes accessed | tf_op | source)
XLA Modules:
  0.0 158.4 jit_solution(9794661866175988395)
XLA Ops:
  0.6 2.7 %dynamic-slice_bitcast_fusion.2 = (bf16[128,4096]{1,0:T(8,128)(2,1)}, bf16[128,4096]{1,0:T(8,128)(2,1)S(1)}) fusion(bf16[1,256,8192]{2,1,0:T(8,128)(2,1)} %param.6, s32[]{:T(128)S(6)} %select_n.14), kind=kLoop, calls=%fused_computation.2 | loop fusion | bytes 4194308 | tf_op jit(solution)/shard_map/dynamic_slice | solution.py:356
  3.3 3.3 %collective-permute-start.1 = (bf16[128,4096]{1,0:T(8,128)(2,1)}, bf16[128,4096]{1,0:T(8,128)(2,1)S(1)}, u32[]{:S(2)}, u32[]{:S(2)}) collective-permute-start(bf16[128,4096]{1,0:T(8,128)(2,1)} %get-tuple-element.35), channel_id=1, source_target_pairs={{0,68},{1,69},{2,70},{3,71},{4,0},{5,1},{6,2},{7,3},{8,76},{9,77},... | collective-permute-start | bytes 3145736 | tf_op jit(solution)/shard_map/ppermute | solution.py:39
  6.6 0.0 collective-permute-start
  6.6 0.1 pad_add_fusion.place
  6.7 0.0 copy-start
  6.7 2.2 %copy-done = bf16[1,256,8192]{2,1,0:T(8,128)(2,1)S(1)} copy-done((bf16[1,256,8192]{2,1,0:T(8,128)(2,1)S(1)}, bf16[1,256,8192]{2,1,0:T(8,128)(2,1)}, u32[]{:S(2)}) %copy-start) | copy-done | bytes 4194328
  8.9 0.0 copy-start.2
  8.9 2.2 %copy-done.2 = bf16[4096,512]{1,0:T(8,128)(2,1)S(1)} copy-done((bf16[4096,512]{1,0:T(8,128)(2,1)S(1)}, bf16[4096,512]{1,0:T(8,128)(2,1)}, u32[]{:S(2)}) %copy-start.2) | copy-done | bytes 4194328
  11.1 0.0 copy-start.1
  11.1 2.6 %project_own.1 = f32[256,512]{1,0:T(8,128)S(1)} custom-call(s32[3]{0:T(128)S(1)} %pad_add_fusion.place, bf16[256,8192]{1,0:T(8,128)(2,1)S(1)} %bitcast.25, bf16[4096,512]{1,0:T(8,128)(2,1)S(1)} %copy-done.2), custom_call_target="tpu_custom_call" | custom-call | flops 1073741824 | bytes 6291456 | tf_op jit(solution)/shard_map/project_own/pallas_call | solution.py:67
  13.7 0.0 copy-done.1
  13.7 0.0 copy-start.3
  13.7 0.2 dynamic-slice_bitcast_fusion
  13.9 14.8 %collective-permute-done.1.high.refs_2_ = bf16[128,4096]{1,0:T(8,128)(2,1)S(1)} collective-permute-done((bf16[128,4096]{1,0:T(8,128)(2,1)}, bf16[128,4096]{1,0:T(8,128)(2,1)S(1)}, u32[]{:S(2)}, u32[]{:S(2)}) %collective-permute-start.1) | collective-permute-done | bytes 1048608 | tf_op jit(solution)/shard_map/ppermute | solution.py:39
  28.8 2.8 %collective-permute-done.low.refs_1_ = bf16[128,4096]{1,0:T(8,128)(2,1)S(1)} collective-permute-done((bf16[128,4096]{1,0:T(8,128)(2,1)S(1)}, bf16[128,4096]{1,0:T(8,128)(2,1)S(1)}, u32[]{:S(2)}, u32[]{:S(2)}) %collective-permute-start) | collective-permute-done | bytes 1048608 | tf_op jit(solution)/shard_map/ppermute | solution.py:39
  31.6 0.0 copy-done.3
  31.6 0.0 copy-start.4
  31.6 0.0 copy-start.5
  31.6 0.0 copy-start.6
  31.6 1.8 %project_near.1 = (bf16[128,512]{1,0:T(8,128)(2,1)S(1)}, bf16[128,512]{1,0:T(8,128)(2,1)S(1)}) custom-call(bf16[128,4096]{1,0:T(8,128)(2,1)S(1)} %collective-permute-done.low.refs_1_, bf16[128,4096]{1,0:T(8,128)(2,1)S(1)} %collective-permute-done.1.high.refs_2_, bf16[4096,512]{1,0:T(8,128)(2,1)S(1)} %copy-done.3), custom_call_target="tpu_custom_call" | custom-call | flops 1073741824 | bytes 6291456 | tf_op jit(solution)/shard_map/project_near/pallas_call | solution.py:104
  33.4 0.6 collective-permute-start.2
  34.0 0.9 collective-permute-start.3
  34.9 2.4 %collective-permute-start.5 = (bf16[256,2048]{1,0:T(8,128)(2,1)S(1)}, bf16[256,2048]{1,0:T(8,128)(2,1)S(1)}, u32[]{:S(2)}, u32[]{:S(2)}) collective-permute-start(bf16[256,2048]{1,0:T(8,128)(2,1)S(1)} %get-tuple-element.27), channel_id=1, source_target_pairs={{0,8},{1,9},{2,10},{3,11},{4,12},{5,13},{6,14},{7,15},{8,0},{9,1},... | collective-permute-start | bytes 3145736 | tf_op jit(solution)/shard_map/ppermute | solution.py:39
  37.4 0.0 collective-permute-done.2
  37.4 1.6 %collective-permute-done.3 = bf16[128,512]{1,0:T(8,128)(2,1)S(1)} collective-permute-done((bf16[128,512]{1,0:T(8,128)(2,1)S(1)}, bf16[128,512]{1,0:T(8,128)(2,1)S(1)}, u32[]{:S(2)}, u32[]{:S(2)}) %collective-permute-start.3) | collective-permute-done | bytes 131104 | tf_op jit(solution)/shard_map/ppermute | solution.py:39
  39.0 0.1 add_convert_fusion.1.key_own
  39.1 6.1 %collective-permute-start.4 = (bf16[256,512]{1,0:T(8,128)(2,1)S(1)}, bf16[256,512]{1,0:T(8,128)(2,1)S(1)}, u32[]{:S(2)}, u32[]{:S(2)}) collective-permute-start(bf16[256,512]{1,0:T(8,128)(2,1)S(1)} %add_convert_fusion.1.key_own), channel_id=1, source_target_pairs={{0,8},{1,9},{2,10},{3,11},{4,12},{5,13},{6,14},{7,15},{8,16},{9,17... | collective-permute-start | bytes 786440 | tf_op jit(solution)/shard_map/ppermute | solution.py:39
  45.2 0.1 collective-permute-start.7
  45.3 0.5 collective-permute-start.6
  45.8 2.7 %collective-permute-done.4.key_halo = bf16[256,512]{1,0:T(8,128)(2,1)S(1)} collective-permute-done((bf16[256,512]{1,0:T(8,128)(2,1)S(1)}, bf16[256,512]{1,0:T(8,128)(2,1)S(1)}, u32[]{:S(2)}, u32[]{:S(2)}) %collective-permute-start.4) | collective-permute-done | bytes 262176 | tf_op jit(solution)/shard_map/ppermute | solution.py:39
  48.5 0.0 copy-done.4
  48.5 0.0 copy-done.5
  48.5 0.0 copy-done.6
  48.5 10.1 %attend.1 = (f32[32,256]{1,0:T(8,128)}, bf16[256,4096]{1,0:T(8,128)(2,1)}, f32[256,512]{1,0:T(8,128)S(1)}, bf16[256,512]{1,0:T(8,128)(2,1)S(1)}) custom-call(s32[3]{0:T(128)S(1)} %pad_add_fusion.place, s32[1,32]{1,0:T(1,128)S(1)} %copy-done.6, bf16[256,4096]{1,0:T(8,128)(2,1)S(1)} %bitcast.27, bf16[256,512]{1,0:T(8,128)(2,1)S(1)} %add_convert_fusion.1.key_own, ...), custom_call_target="tpu_custom_call" | custom-call | flops 4294967296 | bytes 6291456 | tf_op jit(solution)/shard_map/attend/pallas_call | solution.py:210
  58.6 0.0 collective-permute-done.7.refs_5_
  58.6 0.0 collective-permute-done.6.refs_4_
  58.6 0.0 collective-permute-done.5.refs_3_
  58.6 1.9 %collective-permute-start.8 = (bf16[256,512]{1,0:T(8,128)(2,1)S(1)}, bf16[256,512]{1,0:T(8,128)(2,1)S(1)}, u32[]{:S(2)}, u32[]{:S(2)}) collective-permute-start(bf16[256,512]{1,0:T(8,128)(2,1)S(1)} %get-tuple-element.32), channel_id=1, source_target_pairs={{8,0},{9,1},{10,2},{11,3},{12,4},{13,5},{14,6},{15,7},{16,8},{17,9... | collective-permute-start | bytes 786440 | tf_op jit(solution)/shard_map/ppermute | solution.py:39
  60.6 6.5 %collective-permute-done.8 = bf16[256,512]{1,0:T(8,128)(2,1)S(1)} collective-permute-done((bf16[256,512]{1,0:T(8,128)(2,1)S(1)}, bf16[256,512]{1,0:T(8,128)(2,1)S(1)}, u32[]{:S(2)}, u32[]{:S(2)}) %collective-permute-start.8) | collective-permute-done | bytes 262176 | tf_op jit(solution)/shard_map/ppermute | solution.py:39
  67.1 0.1 add_convert_fusion.refs_6_
  67.2 0.1 collective-permute-start.11
  67.3 2.0 %collective-permute-start.10 = (bf16[128,512]{1,0:T(8,128)(2,1)S(1)}, bf16[128,512]{1,0:T(8,128)(2,1)S(1)}, u32[]{:S(2)}, u32[]{:S(2)}) collective-permute-start(bf16[128,512]{1,0:T(8,128)(2,1)S(1)} %get-tuple-element.39), channel_id=1, source_target_pairs={{0,68},{1,69},{2,70},{3,71},{4,0},{5,1},{6,2},{7,3},{8,76},{9,77},... | collective-permute-start | bytes 393224 | tf_op jit(solution)/shard_map/ppermute | solution.py:39
  69.3 0.0 collective-permute-start.9
  69.3 2.8 %collective-permute-done.10.refs_8_ = bf16[128,512]{1,0:T(8,128)(2,1)S(1)} collective-permute-done((bf16[128,512]{1,0:T(8,128)(2,1)S(1)}, bf16[128,512]{1,0:T(8,128)(2,1)S(1)}, u32[]{:S(2)}, u32[]{:S(2)}) %collective-permute-start.10) | collective-permute-done | bytes 131104 | tf_op jit(solution)/shard_map/ppermute | solution.py:39
  72.1 1.1 collective-permute-start.13
  73.3 2.0 %collective-permute-done.9.refs_7_ = bf16[128,512]{1,0:T(8,128)(2,1)S(1)} collective-permute-done((bf16[128,512]{1,0:T(8,128)(2,1)S(1)}, bf16[128,512]{1,0:T(8,128)(2,1)S(1)}, u32[]{:S(2)}, u32[]{:S(2)}) %collective-permute-start.9) | collective-permute-done | bytes 131104 | tf_op jit(solution)/shard_map/ppermute | solution.py:39
  75.2 1.2 collective-permute-start.12
  76.4 0.0 collective-permute-done.11.refs_9_
  76.4 0.0 collective-permute-done.13.refs_11_
  76.4 1.0 collective-permute-done.12.refs_10_
  77.4 3.6 %weight_grad.1 = bf16[2048,512]{1,0:T(8,128)(2,1)S(1)} custom-call(s32[3]{0:T(128)S(1)} %pad_add_fusion.place, bf16[256,2048]{1,0:T(8,128)(2,1)S(1)} %get-tuple-element.25.refs_0_, bf16[128,4096]{1,0:T(8,128)(2,1)S(1)} %collective-permute-done.low.refs_1_, bf16[128,4096]{1,0:T(8,128)(2,1)S(1)} %collective-permute-done.1.high.refs_2_, ...), custom_call_target="tpu_custom_call" | custom-call | flops 2147483648 | bytes 8388608 | tf_op jit(solution)/shard_map/weight_grad/pallas_call | solution.py:266
  81.0 36.0 %all_to_all.10.parts = bf16[32,64,512]{2,1,0:T(8,128)(2,1)S(1)} all-to-all(bf16[32,64,512]{2,1,0:T(8,128)(2,1)S(1)} %bitcast.26), channel_id=1, replica_groups=mesh['xh'=2,'y'=4,'core'=2,'xl'=2,'z'=4] {'xh','y','z'}, dimensions={0} | all-to-all | bytes 4194304 | tf_op jit(solution)/shard_map/all_to_all | solution.py:388
  117.0 0.8 sum_spread.1
  117.8 32.1 %all_to_all.11 = bf16[32,64,512]{2,1,0:T(8,128)(2,1)S(1)} all-to-all(bf16[32,64,512]{2,1,0:T(8,128)(2,1)S(1)} %sum_spread.1), channel_id=1, replica_groups=mesh['xh'=2,'y'=4,'core'=2,'xl'=2,'z'=4] {'xh','y','z'}, dimensions={0} | all-to-all | bytes 4194304 | tf_op jit(solution)/shard_map/all_to_all | solution.py:390
  149.9 0.2 fusion
  150.1 3.5 %collective-permute-start.15 = (bf16[1024,512]{1,0:T(8,128)(2,1)S(1)}, bf16[1024,512]{1,0:T(8,128)(2,1)S(1)}, u32[]{:S(2)}, u32[]{:S(2)}) collective-permute-start(bf16[1024,512]{1,0:T(8,128)(2,1)S(1)} %bitcast.30), channel_id=1, source_target_pairs={{0,8},{1,9},{2,10},{3,11},{4,12},{5,13},{6,14},{7,15},{8,0},{9,1},... | collective-permute-start | bytes 3145736 | tf_op jit(solution)/shard_map/ppermute | solution.py:39
  153.6 0.1 collective-permute-start.14
  153.7 1.3 write_rows.3.refs_0_
  155.0 0.9 collective-permute-done.15.rows
  155.9 1.0 write_rows.4.refs_0_
  156.9 0.5 collective-permute-done.14.rows
  157.4 1.0 write_rows.5
  (3 shorter events, 0.1 us)
Async XLA Ops:
  3.3 25.5 %collective-permute-start.1 = (bf16[128,4096]{1,0:T(8,128)(2,1)}, bf16[128,4096]{1,0:T(8,128)(2,1)S(1)}, u32[]{:S(2)}, u32[]{:S(2)}) collective-permute-start(bf16[128,4096]{1,0:T(8,128)(2,1)} %get-tuple-element.35), channel_id=1, source_target_pairs={{0,68},{1,69},{2,70},{3,71},{4,0},{5,1},{6,2},{7,3},{8,76},{9,77},... | collective-permute-start | bytes 3145736 | tf_op jit(solution)/shard_map/ppermute | solution.py:39
  6.6 24.9 %collective-permute-start = (bf16[128,4096]{1,0:T(8,128)(2,1)S(1)}, bf16[128,4096]{1,0:T(8,128)(2,1)S(1)}, u32[]{:S(2)}, u32[]{:S(2)}) collective-permute-start(bf16[128,4096]{1,0:T(8,128)(2,1)S(1)} %get-tuple-element.36), channel_id=1, source_target_pairs={{0,4},{1,5},{2,6},{3,7},{4,64},{5,65},{6,66},{7,67},{8,12},{9,13},... | collective-permute-start | bytes 3145736 | tf_op jit(solution)/shard_map/ppermute | solution.py:39
  6.7 2.2 %copy-start = (bf16[1,256,8192]{2,1,0:T(8,128)(2,1)S(1)}, bf16[1,256,8192]{2,1,0:T(8,128)(2,1)}, u32[]{:S(2)}) copy-start(bf16[1,256,8192]{2,1,0:T(8,128)(2,1)} %param.6) | copy-start | bytes 12582916
  8.9 2.2 %copy-start.2 = (bf16[4096,512]{1,0:T(8,128)(2,1)S(1)}, bf16[4096,512]{1,0:T(8,128)(2,1)}, u32[]{:S(2)}) copy-start(bf16[4096,512]{1,0:T(8,128)(2,1)} %weight.3) | copy-start | bytes 12582916
  11.1 2.6 %copy-start.1 = (bf16[1,256,8192]{2,1,0:T(8,128)(2,1)S(1)}, bf16[1,256,8192]{2,1,0:T(8,128)(2,1)}, u32[]{:S(2)}) copy-start(bf16[1,256,8192]{2,1,0:T(8,128)(2,1)} %param.6) | copy-start | bytes 12582916
  13.7 17.9 %copy-start.3 = (bf16[4096,512]{1,0:T(8,128)(2,1)S(1)}, bf16[4096,512]{1,0:T(8,128)(2,1)}, u32[]{:S(2)}) copy-start(bf16[4096,512]{1,0:T(8,128)(2,1)} %weight.3) | copy-start | bytes 12582916
  31.6 16.9 %copy-start.4 = (bf16[1,256,4096]{2,1,0:T(8,128)(2,1)S(1)}, bf16[1,256,4096]{2,1,0:T(8,128)(2,1)}, u32[]{:S(2)}) copy-start(bf16[1,256,4096]{2,1,0:T(8,128)(2,1)} %param.5) | copy-start | bytes 6291460
  31.6 16.9 %copy-start.5 = (bf16[1,256,32]{1,2,0:T(8,128)(2,1)S(1)}, bf16[1,256,32]{1,2,0:T(8,128)(2,1)}, u32[]{:S(2)}) copy-start(bf16[1,256,32]{1,2,0:T(8,128)(2,1)} %param.9) | copy-start | bytes 49156
  31.6 16.9 %copy-start.6 = (s32[1,32]{1,0:T(1,128)S(1)}, s32[1,32]{1,0:T(1,128)}, u32[]{:S(2)}) copy-start(s32[1,32]{1,0:T(1,128)} %lengths.1) | copy-start | bytes 388
  33.4 4.0 %collective-permute-start.2 = (bf16[128,512]{1,0:T(8,128)(2,1)S(1)}, bf16[128,512]{1,0:T(8,128)(2,1)S(1)}, u32[]{:S(2)}, u32[]{:S(2)}) collective-permute-start(bf16[128,512]{1,0:T(8,128)(2,1)S(1)} %get-tuple-element.21), channel_id=1, source_target_pairs={{0,68},{1,69},{2,70},{3,71},{4,0},{5,1},{6,2},{7,3},{8,76},{9,77},... | collective-permute-start | bytes 393224 | tf_op jit(solution)/shard_map/ppermute | solution.py:39
  34.0 5.0 %collective-permute-start.3 = (bf16[128,512]{1,0:T(8,128)(2,1)S(1)}, bf16[128,512]{1,0:T(8,128)(2,1)S(1)}, u32[]{:S(2)}, u32[]{:S(2)}) collective-permute-start(bf16[128,512]{1,0:T(8,128)(2,1)S(1)} %get-tuple-element.22), channel_id=1, source_target_pairs={{0,4},{1,5},{2,6},{3,7},{4,64},{5,65},{6,66},{7,67},{8,12},{9,13},... | collective-permute-start | bytes 393224 | tf_op jit(solution)/shard_map/ppermute | solution.py:39
  34.9 23.7 %collective-permute-start.5 = (bf16[256,2048]{1,0:T(8,128)(2,1)S(1)}, bf16[256,2048]{1,0:T(8,128)(2,1)S(1)}, u32[]{:S(2)}, u32[]{:S(2)}) collective-permute-start(bf16[256,2048]{1,0:T(8,128)(2,1)S(1)} %get-tuple-element.27), channel_id=1, source_target_pairs={{0,8},{1,9},{2,10},{3,11},{4,12},{5,13},{6,14},{7,15},{8,0},{9,1},... | collective-permute-start | bytes 3145736 | tf_op jit(solution)/shard_map/ppermute | solution.py:39
  39.1 9.4 %collective-permute-start.4 = (bf16[256,512]{1,0:T(8,128)(2,1)S(1)}, bf16[256,512]{1,0:T(8,128)(2,1)S(1)}, u32[]{:S(2)}, u32[]{:S(2)}) collective-permute-start(bf16[256,512]{1,0:T(8,128)(2,1)S(1)} %add_convert_fusion.1.key_own), channel_id=1, source_target_pairs={{0,8},{1,9},{2,10},{3,11},{4,12},{5,13},{6,14},{7,15},{8,16},{9,17... | collective-permute-start | bytes 786440 | tf_op jit(solution)/shard_map/ppermute | solution.py:39
  45.2 13.4 %collective-permute-start.7 = (bf16[128,2048]{1,0:T(8,128)(2,1)S(1)}, bf16[128,2048]{1,0:T(8,128)(2,1)S(1)}, u32[]{:S(2)}, u32[]{:S(2)}) collective-permute-start(bf16[128,2048]{1,0:T(8,128)(2,1)S(1)} %constant_dynamic-slice_fusion), channel_id=1, source_target_pairs={{0,8},{1,9},{2,10},{3,11},{4,12},{5,13},{6,14},{7,15},{8,0},{9,1},... | collective-permute-start | bytes 1572872 | tf_op jit(solution)/shard_map/ppermute | solution.py:39
  45.3 13.3 %collective-permute-start.6 = (bf16[128,2048]{1,0:T(8,128)(2,1)S(1)}, bf16[128,2048]{1,0:T(8,128)(2,1)S(1)}, u32[]{:S(2)}, u32[]{:S(2)}) collective-permute-start(bf16[128,2048]{1,0:T(8,128)(2,1)S(1)} %constant_dynamic-slice_fusion.1), channel_id=1, source_target_pairs={{0,8},{1,9},{2,10},{3,11},{4,12},{5,13},{6,14},{7,15},{8,0},{9,1},... | collective-permute-start | bytes 1572872 | tf_op jit(solution)/shard_map/ppermute | solution.py:39
  58.6 8.4 %collective-permute-start.8 = (bf16[256,512]{1,0:T(8,128)(2,1)S(1)}, bf16[256,512]{1,0:T(8,128)(2,1)S(1)}, u32[]{:S(2)}, u32[]{:S(2)}) collective-permute-start(bf16[256,512]{1,0:T(8,128)(2,1)S(1)} %get-tuple-element.32), channel_id=1, source_target_pairs={{8,0},{9,1},{10,2},{11,3},{12,4},{13,5},{14,6},{15,7},{16,8},{17,9... | collective-permute-start | bytes 786440 | tf_op jit(solution)/shard_map/ppermute | solution.py:39
  67.2 9.2 %collective-permute-start.11 = (bf16[256,512]{1,0:T(8,128)(2,1)S(1)}, bf16[256,512]{1,0:T(8,128)(2,1)S(1)}, u32[]{:S(2)}, u32[]{:S(2)}) collective-permute-start(bf16[256,512]{1,0:T(8,128)(2,1)S(1)} %add_convert_fusion.refs_6_), channel_id=1, source_target_pairs={{0,8},{1,9},{2,10},{3,11},{4,12},{5,13},{6,14},{7,15},{8,0},{9,1},... | collective-permute-start | bytes 786440 | tf_op jit(solution)/shard_map/ppermute | solution.py:39
  67.3 4.8 %collective-permute-start.10 = (bf16[128,512]{1,0:T(8,128)(2,1)S(1)}, bf16[128,512]{1,0:T(8,128)(2,1)S(1)}, u32[]{:S(2)}, u32[]{:S(2)}) collective-permute-start(bf16[128,512]{1,0:T(8,128)(2,1)S(1)} %get-tuple-element.39), channel_id=1, source_target_pairs={{0,68},{1,69},{2,70},{3,71},{4,0},{5,1},{6,2},{7,3},{8,76},{9,77},... | collective-permute-start | bytes 393224 | tf_op jit(solution)/shard_map/ppermute | solution.py:39
  69.3 5.9 %collective-permute-start.9 = (bf16[128,512]{1,0:T(8,128)(2,1)S(1)}, bf16[128,512]{1,0:T(8,128)(2,1)S(1)}, u32[]{:S(2)}, u32[]{:S(2)}) collective-permute-start(bf16[128,512]{1,0:T(8,128)(2,1)S(1)} %get-tuple-element.40), channel_id=1, source_target_pairs={{0,4},{1,5},{2,6},{3,7},{4,64},{5,65},{6,66},{7,67},{8,12},{9,13},... | collective-permute-start | bytes 393224 | tf_op jit(solution)/shard_map/ppermute | solution.py:39
  72.1 4.3 %collective-permute-start.13 = (bf16[128,512]{1,0:T(8,128)(2,1)S(1)}, bf16[128,512]{1,0:T(8,128)(2,1)S(1)}, u32[]{:S(2)}, u32[]{:S(2)}) collective-permute-start(bf16[128,512]{1,0:T(8,128)(2,1)S(1)} %collective-permute-done.10.refs_8_), channel_id=1, source_target_pairs={{0,8},{1,9},{2,10},{3,11},{4,12},{5,13},{6,14},{7,15},{8,0},{9,1},... | collective-permute-start | bytes 393224 | tf_op jit(solution)/shard_map/ppermute | solution.py:39
  75.2 2.2 %collective-permute-start.12 = (bf16[128,512]{1,0:T(8,128)(2,1)S(1)}, bf16[128,512]{1,0:T(8,128)(2,1)S(1)}, u32[]{:S(2)}, u32[]{:S(2)}) collective-permute-start(bf16[128,512]{1,0:T(8,128)(2,1)S(1)} %collective-permute-done.9.refs_7_), channel_id=1, source_target_pairs={{0,8},{1,9},{2,10},{3,11},{4,12},{5,13},{6,14},{7,15},{8,0},{9,1},... | collective-permute-start | bytes 393224 | tf_op jit(solution)/shard_map/ppermute | solution.py:39
  150.1 5.8 %collective-permute-start.15 = (bf16[1024,512]{1,0:T(8,128)(2,1)S(1)}, bf16[1024,512]{1,0:T(8,128)(2,1)S(1)}, u32[]{:S(2)}, u32[]{:S(2)}) collective-permute-start(bf16[1024,512]{1,0:T(8,128)(2,1)S(1)} %bitcast.30), channel_id=1, source_target_pairs={{0,8},{1,9},{2,10},{3,11},{4,12},{5,13},{6,14},{7,15},{8,0},{9,1},... | collective-permute-start | bytes 3145736 | tf_op jit(solution)/shard_map/ppermute | solution.py:39
  153.6 3.8 %collective-permute-start.14 = (bf16[1024,512]{1,0:T(8,128)(2,1)S(1)}, bf16[1024,512]{1,0:T(8,128)(2,1)S(1)}, u32[]{:S(2)}, u32[]{:S(2)}) collective-permute-start(bf16[1024,512]{1,0:T(8,128)(2,1)S(1)} %bitcast.29), channel_id=1, source_target_pairs={{0,8},{1,9},{2,10},{3,11},{4,12},{5,13},{6,14},{7,15},{8,0},{9,1},... | collective-permute-start | bytes 3145736 | tf_op jit(solution)/shard_map/ppermute | solution.py:39

commit v7 on v6

--- a/solution.py
+++ b/solution.py
@@ -83,11 +83,11 @@
 
 
 def near_kernel(low, high, weight, low_out, high_out, total):
-    step = weight.shape[0] // 4
+    step = weight.shape[0] // 2
     count = low.shape[0]
     total[...] = jnp.zeros_like(total)
 
-    @pl.loop(0, 4)
+    @pl.loop(0, 2)
     def _(k):
         part = pl.ds(pl.multiple_of(k * step, step), step)
         rows = jnp.concatenate([low[:, part], high[:, part]], axis=0)
@@ -113,7 +113,7 @@
     )(low, high, weight)
 
 
-TILE = 64
+TILE = 32
 WINDOW = 256 + TILE
 STACK = 256 // TILE
 
@@ -145,7 +145,8 @@
     keys[0:256, :] = key_halo[...]
     keys[256:512, :] = key_own[...]
     keys_t[0] = keys[...].T
-    keys_t[1, :, 0:512 - TILE] = keys[TILE:512, :].T
+    for k in range(1, 128 // TILE):
+        keys_t[k, :, 0:512 - k * TILE] = keys[k * TILE:512, :].T
     weights = weight[...].astype(F32)
     total[...] = jnp.zeros_like(total)
 
@@ -177,9 +178,9 @@
 
     def grads(group, tile, slope, stack):
         rows = slice(tile * TILE, (tile + 1) * TILE)
-        start = tile // 2 * 2 * TILE
+        start = tile * TILE // 128 * 128
         turned = jnp.dot(
-            keys_t[tile % 2, :, start:start + WINDOW], slope, preferred_element_type=F32
+            keys_t[tile % (128 // TILE), :, start:start + WINDOW], slope, preferred_element_type=F32
         ) * FACTOR
         straight = turned.T.astype(BF)
         for k in range(STACK):
@@ -227,7 +228,7 @@
             scratch_shapes=[
                 pltpu.VMEM((256 // TILE, WINDOW, 256), F32),
                 pltpu.VMEM((512, HD), BF),
-                pltpu.VMEM((2, HD, 512), BF),
+                pltpu.VMEM((128 // TILE, HD, 512), BF),
                 pltpu.VMEM((512, HD), F32),
             ],
         ),
@@ -243,8 +244,8 @@
     )(place, lengths, queries, key_own, key_halo, weight)
 
 
-def weight_grad_kernel(count, far, place, *refs):
-    hidden, grads, out, grad = refs[:count], refs[count:-2], refs[-2], refs[-1]
+def weight_grad_kernel(count, far, more, place, *refs):
+    hidden, grads, out, grad = refs[:count], refs[count:2 * count], refs[-2], refs[-1]
     grad[...] = jnp.concatenate([piece[...] for piece in grads], axis=0)
     step = 512
 
@@ -256,23 +257,25 @@
             [piece[:, pl.ds(there if far[k] else here, step)] for k, piece in enumerate(hidden)], axis=0
         )
         total = lax.dot_general(rows, grad[...], (((0,), (0,)), ((), ())), preferred_element_type=F32)
-        out[pl.ds(here, step), :] = total.astype(BF)
-
-
-def weight_grad(place, own, near, swapped, grads):
+        if more:
+            total = total + refs[2 * count][pl.ds(here, step), :]
+        out[pl.ds(here, step), :] = total.astype(out.dtype)
+
+
+def weight_grad(place, hidden, far, grads, dtype, held=None):
     here = pl.BlockSpec(memory_space=pltpu.VMEM)
-    hidden = [own, *near, *swapped]
-    far = [False] + [True] * len(near) + [False] * len(swapped)
-    return pl.pallas_call(
-        functools.partial(weight_grad_kernel, len(hidden), far),
-        in_specs=[pl.BlockSpec(memory_space=pltpu.SMEM)] + [here] * (len(hidden) + len(grads)),
+    more = [] if held is None else [held]
+    count = sum(v.shape[0] for v in grads)
+    return pl.pallas_call(
+        functools.partial(weight_grad_kernel, len(hidden), far, len(more)),
+        in_specs=[pl.BlockSpec(memory_space=pltpu.SMEM)] + [here] * (2 * len(hidden) + len(more)),
         out_specs=here,
-        out_shape=jax.ShapeDtypeStruct((2048, 512), BF),
-        scratch_shapes=[pltpu.VMEM((1024, 512), BF)],
+        out_shape=jax.ShapeDtypeStruct((2048, 512), dtype),
+        scratch_shapes=[pltpu.VMEM((count, 512), BF)],
         compiler_params=params(16),
-        cost_estimate=cost(2 * 1024 * 2048 * 512, 8 << 20),
+        cost_estimate=cost(2 * count * 2048 * 512, 8 << 20),
         name="weight_grad",
-    )(place, *hidden, *grads)
+    )(place, *hidden, *grads, *more)
 
 
 def sum_spread_kernel(scale, parts, out):
@@ -380,12 +383,15 @@
     from_next = move(grad_halo, next_rows(-1))
     key_grad = (grad_own + from_next.astype(F32)).astype(BF)
     grad_near = [move(key_grad[:split], forward), move(key_grad[split:], backward)]
-    grads = [key_grad, *grad_near, move(key_grad, swap_core)]
-    grads += [move(v, swap_core) for v in grad_near]
+    grads = [key_grad, move(key_grad, swap_core)]
+    parts = weight_grad(place, [own, across[0]], [False, False], grads, F32)
+    grad_near, parts = lax.optimization_barrier((grad_near, parts))
+    grads = [*grad_near, *(move(v, swap_core) for v in grad_near)]
+    far = [True, True, False, False]
+    parts = weight_grad(place, [*near, *across[1:]], far, grads, BF, parts)
 
     chips = ("xh", "y", "z")
-    parts = weight_grad(place, own, near, across, grads).reshape(32, 64, width)
-    parts = lax.all_to_all(parts, chips, split_axis=0, concat_axis=0, tiled=True)
+    parts = lax.all_to_all(parts.reshape(32, 64, width), chips, split_axis=0, concat_axis=0, tiled=True)
     spread = sum_spread(parts, (rows * 16 * 8) ** (-0.5))
     final = lax.all_to_all(spread, chips, split_axis=0, concat_axis=0, tiled=True).reshape(2048, width)
     part = 1024

time: 159 us -> 158 us (level)
    pallas_call x1 -> x2, Pallas kernels: 3.6 us -> 4.99 us  [weight_grad(): pl.pallas_call(functools.partial(weight_grad_kernel, len(hidden), far, le...]
  transfers between devices with their start and end apart: 16 -> 16, of which waited for: 10 -> 11; matrix products, arithmetic and copies ran while one was open for 0% -> 0% of each run, Pallas kernels for 9% -> 11%
where the time goes in v7:
time: 158 us; the launch traced here: 157 us
  blocking collectives  68.9 us (44%)
  waiting for transfers between devices  34.6 us (22%)
  Pallas kernels  22.9 us (14%)
  starting transfers between devices  22.3 us (14%)
  local copies, waits for them, and re-layouts  7.65 us (5%)
    all_to_all x1, blocking collectives, shards(): lax.all_to_all(parts.reshape(32, 64, width), chips, split_axis=0, concat_...  36.3 us
    ppermute x16, waiting for transfers between devices, move(): return lax.ppermute(value, AXES, pairs)  34.6 us
    all_to_all x1, blocking collectives, shards(): lax.all_to_all(spread, chips, split_axis=0, concat_axis=0, tiled=True)  32.6 us
    ppermute x16, starting transfers between devices, move(): return lax.ppermute(value, AXES, pairs)  22.3 us
    pallas_call x1, Pallas kernels, attend(): pl.pallas_call(attend_kernel, grid_spec=pltpu.PrefetchScalarGridSpec(num_...  9.74 us
    pallas_call x2, Pallas kernels, weight_grad(): pl.pallas_call(functools.partial(weight_grad_kernel, len(hidden), far, le...  4.99 us
    unnamed x14, local copies, waits for them, and re-layouts  4.4 us
    pallas_call x3, Pallas kernels, write_rows(): pl.pallas_call(functools.partial(copy_kernel, side, first), in_specs=[any...  3.28 us
  transfers between devices with their start and end apart: 16, of which 11 were waited for; matrix products, arithmetic and copies ran while one was open for 0% of the time, Pallas kernels for 11%

profile of v7, /device:TPU:1, one launch (start us, length us, event | category | flops | bytes accessed | tf_op | source)
XLA Modules:
  0.0 157.3 jit_solution(5162790563605407986)
XLA Ops:
  0.6 2.7 %dynamic-slice_bitcast_fusion.2 = (bf16[128,4096]{1,0:T(8,128)(2,1)}, bf16[128,4096]{1,0:T(8,128)(2,1)S(1)}) fusion(bf16[1,256,8192]{2,1,0:T(8,128)(2,1)} %param.6, s32[]{:T(128)S(6)} %select_n.14), kind=kLoop, calls=%fused_computation.2 | loop fusion | bytes 4194308 | tf_op jit(solution)/shard_map/dynamic_slice | solution.py:359
  3.3 3.3 %collective-permute-start.1 = (bf16[128,4096]{1,0:T(8,128)(2,1)}, bf16[128,4096]{1,0:T(8,128)(2,1)S(1)}, u32[]{:S(2)}, u32[]{:S(2)}) collective-permute-start(bf16[128,4096]{1,0:T(8,128)(2,1)} %get-tuple-element.41), channel_id=1, source_target_pairs={{0,68},{1,69},{2,70},{3,71},{4,0},{5,1},{6,2},{7,3},{8,76},{9,77},... | collective-permute-start | bytes 3145736 | tf_op jit(solution)/shard_map/ppermute | solution.py:39
  6.6 0.0 collective-permute-start
  6.6 0.1 pad_add_fusion.place
  6.7 0.0 copy-start
  6.7 2.2 %copy-done = bf16[1,256,8192]{2,1,0:T(8,128)(2,1)S(1)} copy-done((bf16[1,256,8192]{2,1,0:T(8,128)(2,1)S(1)}, bf16[1,256,8192]{2,1,0:T(8,128)(2,1)}, u32[]{:S(2)}) %copy-start) | copy-done | bytes 4194328
  8.9 0.0 copy-start.2
  8.9 2.2 %copy-done.2 = bf16[4096,512]{1,0:T(8,128)(2,1)S(1)} copy-done((bf16[4096,512]{1,0:T(8,128)(2,1)S(1)}, bf16[4096,512]{1,0:T(8,128)(2,1)}, u32[]{:S(2)}) %copy-start.2) | copy-done | bytes 4194328
  11.1 0.0 copy-start.1
  11.1 2.6 %project_own.1 = f32[256,512]{1,0:T(8,128)S(1)} custom-call(s32[3]{0:T(128)S(1)} %pad_add_fusion.place, bf16[256,8192]{1,0:T(8,128)(2,1)S(1)} %bitcast.25, bf16[4096,512]{1,0:T(8,128)(2,1)S(1)} %copy-done.2), custom_call_target="tpu_custom_call" | custom-call | flops 1073741824 | bytes 6291456 | tf_op jit(solution)/shard_map/project_own/pallas_call | solution.py:67
  13.7 0.0 copy-done.1
  13.7 0.0 copy-start.3
  13.7 0.2 dynamic-slice_bitcast_fusion
  13.9 14.8 %collective-permute-done.1.high.refs_1_ = bf16[128,4096]{1,0:T(8,128)(2,1)S(1)} collective-permute-done((bf16[128,4096]{1,0:T(8,128)(2,1)}, bf16[128,4096]{1,0:T(8,128)(2,1)S(1)}, u32[]{:S(2)}, u32[]{:S(2)}) %collective-permute-start.1) | collective-permute-done | bytes 1048608 | tf_op jit(solution)/shard_map/ppermute | solution.py:39
  28.8 2.8 %collective-permute-done.low.refs_0_ = bf16[128,4096]{1,0:T(8,128)(2,1)S(1)} collective-permute-done((bf16[128,4096]{1,0:T(8,128)(2,1)S(1)}, bf16[128,4096]{1,0:T(8,128)(2,1)S(1)}, u32[]{:S(2)}, u32[]{:S(2)}) %collective-permute-start) | collective-permute-done | bytes 1048608 | tf_op jit(solution)/shard_map/ppermute | solution.py:39
  31.6 0.0 copy-done.3
  31.6 0.0 copy-start.4
  31.6 0.0 copy-start.5
  31.6 0.0 copy-start.6
  31.6 1.5 project_near.1
  33.1 0.6 collective-permute-start.2
  33.7 0.9 collective-permute-start.3
  34.6 2.4 %collective-permute-start.5 = (bf16[256,2048]{1,0:T(8,128)(2,1)S(1)}, bf16[256,2048]{1,0:T(8,128)(2,1)S(1)}, u32[]{:S(2)}, u32[]{:S(2)}) collective-permute-start(bf16[256,2048]{1,0:T(8,128)(2,1)S(1)} %get-tuple-element.29), channel_id=1, source_target_pairs={{0,8},{1,9},{2,10},{3,11},{4,12},{5,13},{6,14},{7,15},{8,0},{9,1},... | collective-permute-start | bytes 3145736 | tf_op jit(solution)/shard_map/ppermute | solution.py:39
  37.1 0.0 collective-permute-done.2
  37.1 1.6 %collective-permute-done.3 = bf16[128,512]{1,0:T(8,128)(2,1)S(1)} collective-permute-done((bf16[128,512]{1,0:T(8,128)(2,1)S(1)}, bf16[128,512]{1,0:T(8,128)(2,1)S(1)}, u32[]{:S(2)}, u32[]{:S(2)}) %collective-permute-start.3) | collective-permute-done | bytes 131104 | tf_op jit(solution)/shard_map/ppermute | solution.py:39
  38.7 0.1 add_convert_fusion.1.key_own
  38.8 6.1 %collective-permute-start.4 = (bf16[256,512]{1,0:T(8,128)(2,1)S(1)}, bf16[256,512]{1,0:T(8,128)(2,1)S(1)}, u32[]{:S(2)}, u32[]{:S(2)}) collective-permute-start(bf16[256,512]{1,0:T(8,128)(2,1)S(1)} %add_convert_fusion.1.key_own), channel_id=1, source_target_pairs={{0,8},{1,9},{2,10},{3,11},{4,12},{5,13},{6,14},{7,15},{8,16},{9,17... | collective-permute-start | bytes 786440 | tf_op jit(solution)/shard_map/ppermute | solution.py:39
  44.9 0.1 collective-permute-start.7
  45.0 0.5 collective-permute-start.6
  45.5 2.7 %collective-permute-done.4.key_halo = bf16[256,512]{1,0:T(8,128)(2,1)S(1)} collective-permute-done((bf16[256,512]{1,0:T(8,128)(2,1)S(1)}, bf16[256,512]{1,0:T(8,128)(2,1)S(1)}, u32[]{:S(2)}, u32[]{:S(2)}) %collective-permute-start.4) | collective-permute-done | bytes 262176 | tf_op jit(solution)/shard_map/ppermute | solution.py:39
  48.1 0.0 copy-done.4
  48.1 0.0 copy-done.5
  48.1 0.0 copy-done.6
  48.2 9.7 %attend.1 = (f32[32,256]{1,0:T(8,128)}, bf16[256,4096]{1,0:T(8,128)(2,1)}, f32[256,512]{1,0:T(8,128)S(1)}, bf16[256,512]{1,0:T(8,128)(2,1)S(1)}) custom-call(s32[3]{0:T(128)S(1)} %pad_add_fusion.place, s32[1,32]{1,0:T(1,128)S(1)} %copy-done.6, bf16[256,4096]{1,0:T(8,128)(2,1)S(1)} %bitcast.27, bf16[256,512]{1,0:T(8,128)(2,1)S(1)} %add_convert_fusion.1.key_own, ...), custom_call_target="tpu_custom_call" | custom-call | flops 4294967296 | bytes 6291456 | tf_op jit(solution)/shard_map/attend/pallas_call | solution.py:211
  57.9 0.0 collective-permute-done.7.refs_3_
  57.9 0.0 collective-permute-done.6.refs_2_
  57.9 0.0 collective-permute-done.5.refs_1_
  57.9 1.9 %collective-permute-start.8 = (bf16[256,512]{1,0:T(8,128)(2,1)S(1)}, bf16[256,512]{1,0:T(8,128)(2,1)S(1)}, u32[]{:S(2)}, u32[]{:S(2)}) collective-permute-start(bf16[256,512]{1,0:T(8,128)(2,1)S(1)} %get-tuple-element.33), channel_id=1, source_target_pairs={{8,0},{9,1},{10,2},{11,3},{12,4},{13,5},{14,6},{15,7},{16,8},{17,9... | collective-permute-start | bytes 786440 | tf_op jit(solution)/shard_map/ppermute | solution.py:39
  59.8 6.5 %collective-permute-done.8 = bf16[256,512]{1,0:T(8,128)(2,1)S(1)} collective-permute-done((bf16[256,512]{1,0:T(8,128)(2,1)S(1)}, bf16[256,512]{1,0:T(8,128)(2,1)S(1)}, u32[]{:S(2)}, u32[]{:S(2)}) %collective-permute-start.8) | collective-permute-done | bytes 262176 | tf_op jit(solution)/shard_map/ppermute | solution.py:39
  66.3 0.1 add_convert_fusion.refs_2_
  66.4 0.1 collective-permute-start.11
  66.5 2.0 %collective-permute-start.10 = (bf16[128,512]{1,0:T(8,128)(2,1)S(1)}, bf16[128,512]{1,0:T(8,128)(2,1)S(1)}, u32[]{:S(2)}, u32[]{:S(2)}) collective-permute-start(bf16[128,512]{1,0:T(8,128)(2,1)S(1)} %get-tuple-element.45), channel_id=1, source_target_pairs={{0,68},{1,69},{2,70},{3,71},{4,0},{5,1},{6,2},{7,3},{8,76},{9,77},... | collective-permute-start | bytes 393224 | tf_op jit(solution)/shard_map/ppermute | solution.py:39
  68.6 0.0 collective-permute-start.9
  68.6 0.0 collective-permute-done.11.refs_3_
  68.6 2.5 %weight_grad.2.refs_8_ = f32[2048,512]{1,0:T(8,128)S(1)} custom-call(s32[3]{0:T(128)S(1)} %pad_add_fusion.place, bf16[256,2048]{1,0:T(8,128)(2,1)S(1)} %get-tuple-element.34.refs_0_, bf16[256,2048]{1,0:T(8,128)(2,1)S(1)} %collective-permute-done.5.refs_1_, bf16[256,512]{1,0:T(8,128)(2,1)S(1)} %add_convert_fusion.refs_2_, ...), custom_call_target="tpu_custom_call" | custom-call | flops 1073741824 | bytes 8388608 | tf_op jit(solution)/shard_map/weight_grad/pallas_call | solution.py:269
  71.1 0.4 collective-permute-done.10.refs_5_
  71.5 3.1 %collective-permute-done.9.refs_4_ = bf16[128,512]{1,0:T(8,128)(2,1)S(1)} collective-permute-done((bf16[128,512]{1,0:T(8,128)(2,1)S(1)}, bf16[128,512]{1,0:T(8,128)(2,1)S(1)}, u32[]{:S(2)}, u32[]{:S(2)}) %collective-permute-start.9) | collective-permute-done | bytes 131104 | tf_op jit(solution)/shard_map/ppermute | solution.py:39
  74.6 1.1 collective-permute-start.12
  75.7 0.0 collective-permute-start.13
  75.7 1.0 collective-permute-done.12.refs_6_
  76.7 0.4 collective-permute-done.13.refs_7_
  77.0 2.5 %weight_grad.3 = bf16[2048,512]{1,0:T(8,128)(2,1)S(1)} custom-call(s32[3]{0:T(128)S(1)} %pad_add_fusion.place, bf16[128,4096]{1,0:T(8,128)(2,1)S(1)} %collective-permute-done.low.refs_0_, bf16[128,4096]{1,0:T(8,128)(2,1)S(1)} %collective-permute-done.1.high.refs_1_, bf16[128,2048]{1,0:T(8,128)(2,1)S(1)} %collective-permute-done.6.refs_2_, ...), custom_call_target="tpu_custom_call" | custom-call | flops 1073741824 | bytes 8388608 | tf_op jit(solution)/shard_map/weight_grad/pallas_call | solution.py:269
  79.6 36.3 %all_to_all.10.parts = bf16[32,64,512]{2,1,0:T(8,128)(2,1)S(1)} all-to-all(bf16[32,64,512]{2,1,0:T(8,128)(2,1)S(1)} %bitcast.26), channel_id=1, replica_groups=mesh['xh'=2,'y'=4,'core'=2,'xl'=2,'z'=4] {'xh','y','z'}, dimensions={0} | all-to-all | bytes 4194304 | tf_op jit(solution)/shard_map/all_to_all | solution.py:394
  115.8 0.8 sum_spread.1
  116.7 32.6 %all_to_all.11 = bf16[32,64,512]{2,1,0:T(8,128)(2,1)S(1)} all-to-all(bf16[32,64,512]{2,1,0:T(8,128)(2,1)S(1)} %sum_spread.1), channel_id=1, replica_groups=mesh['xh'=2,'y'=4,'core'=2,'xl'=2,'z'=4] {'xh','y','z'}, dimensions={0} | all-to-all | bytes 4194304 | tf_op jit(solution)/shard_map/all_to_all | solution.py:396
  149.2 0.2 fusion
  149.5 3.1 %collective-permute-start.15 = (bf16[1024,512]{1,0:T(8,128)(2,1)S(1)}, bf16[1024,512]{1,0:T(8,128)(2,1)S(1)}, u32[]{:S(2)}, u32[]{:S(2)}) collective-permute-start(bf16[1024,512]{1,0:T(8,128)(2,1)S(1)} %bitcast.30), channel_id=1, source_target_pairs={{0,8},{1,9},{2,10},{3,11},{4,12},{5,13},{6,14},{7,15},{8,0},{9,1},... | collective-permute-start | bytes 3145736 | tf_op jit(solution)/shard_map/ppermute | solution.py:39
  152.5 0.1 collective-permute-start.14
  152.6 1.3 write_rows.3.refs_0_
  154.0 0.9 collective-permute-done.15.rows
  154.8 1.0 write_rows.4.refs_0_
  155.8 0.5 collective-permute-done.14.rows
  156.3 1.0 write_rows.5
  (3 shorter events, 0.1 us)
Async XLA Ops:
  3.3 25.5 %collective-permute-start.1 = (bf16[128,4096]{1,0:T(8,128)(2,1)}, bf16[128,4096]{1,0:T(8,128)(2,1)S(1)}, u32[]{:S(2)}, u32[]{:S(2)}) collective-permute-start(bf16[128,4096]{1,0:T(8,128)(2,1)} %get-tuple-element.41), channel_id=1, source_target_pairs={{0,68},{1,69},{2,70},{3,71},{4,0},{5,1},{6,2},{7,3},{8,76},{9,77},... | collective-permute-start | bytes 3145736 | tf_op jit(solution)/shard_map/ppermute | solution.py:39
  6.6 24.9 %collective-permute-start = (bf16[128,4096]{1,0:T(8,128)(2,1)S(1)}, bf16[128,4096]{1,0:T(8,128)(2,1)S(1)}, u32[]{:S(2)}, u32[]{:S(2)}) collective-permute-start(bf16[128,4096]{1,0:T(8,128)(2,1)S(1)} %get-tuple-element.42), channel_id=1, source_target_pairs={{0,4},{1,5},{2,6},{3,7},{4,64},{5,65},{6,66},{7,67},{8,12},{9,13},... | collective-permute-start | bytes 3145736 | tf_op jit(solution)/shard_map/ppermute | solution.py:39
  6.7 2.2 %copy-start = (bf16[1,256,8192]{2,1,0:T(8,128)(2,1)S(1)}, bf16[1,256,8192]{2,1,0:T(8,128)(2,1)}, u32[]{:S(2)}) copy-start(bf16[1,256,8192]{2,1,0:T(8,128)(2,1)} %param.6) | copy-start | bytes 12582916
  8.9 2.2 %copy-start.2 = (bf16[4096,512]{1,0:T(8,128)(2,1)S(1)}, bf16[4096,512]{1,0:T(8,128)(2,1)}, u32[]{:S(2)}) copy-start(bf16[4096,512]{1,0:T(8,128)(2,1)} %weight.3) | copy-start | bytes 12582916
  11.1 2.6 %copy-start.1 = (bf16[1,256,8192]{2,1,0:T(8,128)(2,1)S(1)}, bf16[1,256,8192]{2,1,0:T(8,128)(2,1)}, u32[]{:S(2)}) copy-start(bf16[1,256,8192]{2,1,0:T(8,128)(2,1)} %param.6) | copy-start | bytes 12582916
  13.7 17.9 %copy-start.3 = (bf16[4096,512]{1,0:T(8,128)(2,1)S(1)}, bf16[4096,512]{1,0:T(8,128)(2,1)}, u32[]{:S(2)}) copy-start(bf16[4096,512]{1,0:T(8,128)(2,1)} %weight.3) | copy-start | bytes 12582916
  31.6 16.6 %copy-start.4 = (bf16[1,256,4096]{2,1,0:T(8,128)(2,1)S(1)}, bf16[1,256,4096]{2,1,0:T(8,128)(2,1)}, u32[]{:S(2)}) copy-start(bf16[1,256,4096]{2,1,0:T(8,128)(2,1)} %param.5) | copy-start | bytes 6291460
  31.6 16.6 %copy-start.5 = (bf16[1,256,32]{1,2,0:T(8,128)(2,1)S(1)}, bf16[1,256,32]{1,2,0:T(8,128)(2,1)}, u32[]{:S(2)}) copy-start(bf16[1,256,32]{1,2,0:T(8,128)(2,1)} %param.9) | copy-start | bytes 49156
  31.6 16.6 %copy-start.6 = (s32[1,32]{1,0:T(1,128)S(1)}, s32[1,32]{1,0:T(1,128)}, u32[]{:S(2)}) copy-start(s32[1,32]{1,0:T(1,128)} %lengths.1) | copy-start | bytes 388
  33.1 4.0 %collective-permute-start.2 = (bf16[128,512]{1,0:T(8,128)(2,1)S(1)}, bf16[128,512]{1,0:T(8,128)(2,1)S(1)}, u32[]{:S(2)}, u32[]{:S(2)}) collective-permute-start(bf16[128,512]{1,0:T(8,128)(2,1)S(1)} %get-tuple-element.24), channel_id=1, source_target_pairs={{0,68},{1,69},{2,70},{3,71},{4,0},{5,1},{6,2},{7,3},{8,76},{9,77},... | collective-permute-start | bytes 393224 | tf_op jit(solution)/shard_map/ppermute | solution.py:39
  33.7 5.0 %collective-permute-start.3 = (bf16[128,512]{1,0:T(8,128)(2,1)S(1)}, bf16[128,512]{1,0:T(8,128)(2,1)S(1)}, u32[]{:S(2)}, u32[]{:S(2)}) collective-permute-start(bf16[128,512]{1,0:T(8,128)(2,1)S(1)} %get-tuple-element.25), channel_id=1, source_target_pairs={{0,4},{1,5},{2,6},{3,7},{4,64},{5,65},{6,66},{7,67},{8,12},{9,13},... | collective-permute-start | bytes 393224 | tf_op jit(solution)/shard_map/ppermute | solution.py:39
  34.6 23.3 %collective-permute-start.5 = (bf16[256,2048]{1,0:T(8,128)(2,1)S(1)}, bf16[256,2048]{1,0:T(8,128)(2,1)S(1)}, u32[]{:S(2)}, u32[]{:S(2)}) collective-permute-start(bf16[256,2048]{1,0:T(8,128)(2,1)S(1)} %get-tuple-element.29), channel_id=1, source_target_pairs={{0,8},{1,9},{2,10},{3,11},{4,12},{5,13},{6,14},{7,15},{8,0},{9,1},... | collective-permute-start | bytes 3145736 | tf_op jit(solution)/shard_map/ppermute | solution.py:39
  38.8 9.4 %collective-permute-start.4 = (bf16[256,512]{1,0:T(8,128)(2,1)S(1)}, bf16[256,512]{1,0:T(8,128)(2,1)S(1)}, u32[]{:S(2)}, u32[]{:S(2)}) collective-permute-start(bf16[256,512]{1,0:T(8,128)(2,1)S(1)} %add_convert_fusion.1.key_own), channel_id=1, source_target_pairs={{0,8},{1,9},{2,10},{3,11},{4,12},{5,13},{6,14},{7,15},{8,16},{9,17... | collective-permute-start | bytes 786440 | tf_op jit(solution)/shard_map/ppermute | solution.py:39
  44.9 13.0 %collective-permute-start.7 = (bf16[128,2048]{1,0:T(8,128)(2,1)S(1)}, bf16[128,2048]{1,0:T(8,128)(2,1)S(1)}, u32[]{:S(2)}, u32[]{:S(2)}) collective-permute-start(bf16[128,2048]{1,0:T(8,128)(2,1)S(1)} %constant_dynamic-slice_fusion), channel_id=1, source_target_pairs={{0,8},{1,9},{2,10},{3,11},{4,12},{5,13},{6,14},{7,15},{8,0},{9,1},... | collective-permute-start | bytes 1572872 | tf_op jit(solution)/shard_map/ppermute | solution.py:39
  45.0 12.9 %collective-permute-start.6 = (bf16[128,2048]{1,0:T(8,128)(2,1)S(1)}, bf16[128,2048]{1,0:T(8,128)(2,1)S(1)}, u32[]{:S(2)}, u32[]{:S(2)}) collective-permute-start(bf16[128,2048]{1,0:T(8,128)(2,1)S(1)} %constant_dynamic-slice_fusion.1), channel_id=1, source_target_pairs={{0,8},{1,9},{2,10},{3,11},{4,12},{5,13},{6,14},{7,15},{8,0},{9,1},... | collective-permute-start | bytes 1572872 | tf_op jit(solution)/shard_map/ppermute | solution.py:39
  57.9 8.4 %collective-permute-start.8 = (bf16[256,512]{1,0:T(8,128)(2,1)S(1)}, bf16[256,512]{1,0:T(8,128)(2,1)S(1)}, u32[]{:S(2)}, u32[]{:S(2)}) collective-permute-start(bf16[256,512]{1,0:T(8,128)(2,1)S(1)} %get-tuple-element.33), channel_id=1, source_target_pairs={{8,0},{9,1},{10,2},{11,3},{12,4},{13,5},{14,6},{15,7},{16,8},{17,9... | collective-permute-start | bytes 786440 | tf_op jit(solution)/shard_map/ppermute | solution.py:39
  66.4 2.2 %collective-permute-start.11 = (bf16[256,512]{1,0:T(8,128)(2,1)S(1)}, bf16[256,512]{1,0:T(8,128)(2,1)S(1)}, u32[]{:S(2)}, u32[]{:S(2)}) collective-permute-start(bf16[256,512]{1,0:T(8,128)(2,1)S(1)} %add_convert_fusion.refs_2_), channel_id=1, source_target_pairs={{0,8},{1,9},{2,10},{3,11},{4,12},{5,13},{6,14},{7,15},{8,0},{9,1},... | collective-permute-start | bytes 786440 | tf_op jit(solution)/shard_map/ppermute | solution.py:39
  66.5 5.0 %collective-permute-start.10 = (bf16[128,512]{1,0:T(8,128)(2,1)S(1)}, bf16[128,512]{1,0:T(8,128)(2,1)S(1)}, u32[]{:S(2)}, u32[]{:S(2)}) collective-permute-start(bf16[128,512]{1,0:T(8,128)(2,1)S(1)} %get-tuple-element.45), channel_id=1, source_target_pairs={{0,68},{1,69},{2,70},{3,71},{4,0},{5,1},{6,2},{7,3},{8,76},{9,77},... | collective-permute-start | bytes 393224 | tf_op jit(solution)/shard_map/ppermute | solution.py:39
  68.6 6.0 %collective-permute-start.9 = (bf16[128,512]{1,0:T(8,128)(2,1)S(1)}, bf16[128,512]{1,0:T(8,128)(2,1)S(1)}, u32[]{:S(2)}, u32[]{:S(2)}) collective-permute-start(bf16[128,512]{1,0:T(8,128)(2,1)S(1)} %get-tuple-element.46), channel_id=1, source_target_pairs={{0,4},{1,5},{2,6},{3,7},{4,64},{5,65},{6,66},{7,67},{8,12},{9,13},... | collective-permute-start | bytes 393224 | tf_op jit(solution)/shard_map/ppermute | solution.py:39
  74.6 2.1 %collective-permute-start.12 = (bf16[128,512]{1,0:T(8,128)(2,1)S(1)}, bf16[128,512]{1,0:T(8,128)(2,1)S(1)}, u32[]{:S(2)}, u32[]{:S(2)}) collective-permute-start(bf16[128,512]{1,0:T(8,128)(2,1)S(1)} %collective-permute-done.9.refs_4_), channel_id=1, source_target_pairs={{0,8},{1,9},{2,10},{3,11},{4,12},{5,13},{6,14},{7,15},{8,0},{9,1},... | collective-permute-start | bytes 393224 | tf_op jit(solution)/shard_map/ppermute | solution.py:39
  75.7 1.3 collective-permute-start.13
  149.5 5.4 %collective-permute-start.15 = (bf16[1024,512]{1,0:T(8,128)(2,1)S(1)}, bf16[1024,512]{1,0:T(8,128)(2,1)S(1)}, u32[]{:S(2)}, u32[]{:S(2)}) collective-permute-start(bf16[1024,512]{1,0:T(8,128)(2,1)S(1)} %bitcast.30), channel_id=1, source_target_pairs={{0,8},{1,9},{2,10},{3,11},{4,12},{5,13},{6,14},{7,15},{8,0},{9,1},... | collective-permute-start | bytes 3145736 | tf_op jit(solution)/shard_map/ppermute | solution.py:39
  152.5 3.8 %collective-permute-start.14 = (bf16[1024,512]{1,0:T(8,128)(2,1)S(1)}, bf16[1024,512]{1,0:T(8,128)(2,1)S(1)}, u32[]{:S(2)}, u32[]{:S(2)}) collective-permute-start(bf16[1024,512]{1,0:T(8,128)(2,1)S(1)} %bitcast.29), channel_id=1, source_target_pairs={{0,8},{1,9},{2,10},{3,11},{4,12},{5,13},{6,14},{7,15},{8,0},{9,1},... | collective-permute-start | bytes 3145736 | tf_op jit(solution)/shard_map/ppermute | solution.py:39

commit v8 on v7

--- a/solution.py
+++ b/solution.py
@@ -247,7 +247,7 @@
 def weight_grad_kernel(count, far, more, place, *refs):
     hidden, grads, out, grad = refs[:count], refs[count:2 * count], refs[-2], refs[-1]
     grad[...] = jnp.concatenate([piece[...] for piece in grads], axis=0)
-    step = 512
+    step = 1024
 
     @pl.loop(0, out.shape[0] // step)
     def _(i):

time: 158 us -> 157 us (level)
  no operation moved by 1% of the time
where the time goes in v8:
time: 157 us
  blocking collectives  68.9 us (44%)
  waiting for transfers between devices  35 us (22%)
  starting transfers between devices  22.3 us (14%)
  Pallas kernels  22 us (14%)
  local copies, waits for them, and re-layouts  7.65 us (5%)
    all_to_all x1, blocking collectives, shards(): lax.all_to_all(parts.reshape(32, 64, width), chips, split_axis=0, concat_...  36.3 us
    ppermute x16, waiting for transfers between devices, move(): return lax.ppermute(value, AXES, pairs)  35 us
    all_to_all x1, blocking collectives, shards(): lax.all_to_all(spread, chips, split_axis=0, concat_axis=0, tiled=True)  32.6 us
    ppermute x16, starting transfers between devices, move(): return lax.ppermute(value, AXES, pairs)  22.3 us
    pallas_call x1, Pallas kernels, attend(): pl.pallas_call(attend_kernel, grid_spec=pltpu.PrefetchScalarGridSpec(num_...  9.74 us
    unnamed x14, local copies, waits for them, and re-layouts  4.4 us
    pallas_call x2, Pallas kernels, weight_grad(): pl.pallas_call(functools.partial(weight_grad_kernel, len(hidden), far, le...  4.14 us
    pallas_call x3, Pallas kernels, write_rows(): pl.pallas_call(functools.partial(copy_kernel, side, first), in_specs=[any...  3.28 us
  transfers between devices with their start and end apart: 16, of which 11 were waited for; matrix products, arithmetic and copies ran while one was open for 0% of the time, Pallas kernels for 11%

profile of v8, /device:TPU:1, one launch (start us, length us, event | category | flops | bytes accessed | tf_op | source)
XLA Modules:
  0.0 156.9 jit_solution(5604727401885329616)
XLA Ops:
  0.6 2.7 %dynamic-slice_bitcast_fusion.2 = (bf16[128,4096]{1,0:T(8,128)(2,1)}, bf16[128,4096]{1,0:T(8,128)(2,1)S(1)}) fusion(bf16[1,256,8192]{2,1,0:T(8,128)(2,1)} %param.6, s32[]{:T(128)S(6)} %select_n.14), kind=kLoop, calls=%fused_computation.2 | loop fusion | bytes 4194308 | tf_op jit(solution)/shard_map/dynamic_slice | solution.py:359
  3.3 3.3 %collective-permute-start.1 = (bf16[128,4096]{1,0:T(8,128)(2,1)}, bf16[128,4096]{1,0:T(8,128)(2,1)S(1)}, u32[]{:S(2)}, u32[]{:S(2)}) collective-permute-start(bf16[128,4096]{1,0:T(8,128)(2,1)} %get-tuple-element.41), channel_id=1, source_target_pairs={{0,68},{1,69},{2,70},{3,71},{4,0},{5,1},{6,2},{7,3},{8,76},{9,77},... | collective-permute-start | bytes 3145736 | tf_op jit(solution)/shard_map/ppermute | solution.py:39
  6.6 0.0 collective-permute-start
  6.6 0.1 pad_add_fusion.place
  6.7 0.0 copy-start
  6.7 2.2 %copy-done = bf16[1,256,8192]{2,1,0:T(8,128)(2,1)S(1)} copy-done((bf16[1,256,8192]{2,1,0:T(8,128)(2,1)S(1)}, bf16[1,256,8192]{2,1,0:T(8,128)(2,1)}, u32[]{:S(2)}) %copy-start) | copy-done | bytes 4194328
  8.9 0.0 copy-start.2
  8.9 2.2 %copy-done.2 = bf16[4096,512]{1,0:T(8,128)(2,1)S(1)} copy-done((bf16[4096,512]{1,0:T(8,128)(2,1)S(1)}, bf16[4096,512]{1,0:T(8,128)(2,1)}, u32[]{:S(2)}) %copy-start.2) | copy-done | bytes 4194328
  11.1 0.0 copy-start.1
  11.1 2.6 %project_own.1 = f32[256,512]{1,0:T(8,128)S(1)} custom-call(s32[3]{0:T(128)S(1)} %pad_add_fusion.place, bf16[256,8192]{1,0:T(8,128)(2,1)S(1)} %bitcast.25, bf16[4096,512]{1,0:T(8,128)(2,1)S(1)} %copy-done.2), custom_call_target="tpu_custom_call" | custom-call | flops 1073741824 | bytes 6291456 | tf_op jit(solution)/shard_map/project_own/pallas_call | solution.py:67
  13.7 0.0 copy-done.1
  13.7 0.0 copy-start.3
  13.7 0.2 dynamic-slice_bitcast_fusion
  13.9 14.8 %collective-permute-done.1.high.refs_1_ = bf16[128,4096]{1,0:T(8,128)(2,1)S(1)} collective-permute-done((bf16[128,4096]{1,0:T(8,128)(2,1)}, bf16[128,4096]{1,0:T(8,128)(2,1)S(1)}, u32[]{:S(2)}, u32[]{:S(2)}) %collective-permute-start.1) | collective-permute-done | bytes 1048608 | tf_op jit(solution)/shard_map/ppermute | solution.py:39
  28.8 2.8 %collective-permute-done.low.refs_0_ = bf16[128,4096]{1,0:T(8,128)(2,1)S(1)} collective-permute-done((bf16[128,4096]{1,0:T(8,128)(2,1)S(1)}, bf16[128,4096]{1,0:T(8,128)(2,1)S(1)}, u32[]{:S(2)}, u32[]{:S(2)}) %collective-permute-start) | collective-permute-done | bytes 1048608 | tf_op jit(solution)/shard_map/ppermute | solution.py:39
  31.6 0.0 copy-done.3
  31.6 0.0 copy-start.4
  31.6 0.0 copy-start.5
  31.6 0.0 copy-start.6
  31.6 1.5 project_near.1
  33.1 0.6 collective-permute-start.2
  33.7 0.9 collective-permute-start.3
  34.6 2.4 %collective-permute-start.5 = (bf16[256,2048]{1,0:T(8,128)(2,1)S(1)}, bf16[256,2048]{1,0:T(8,128)(2,1)S(1)}, u32[]{:S(2)}, u32[]{:S(2)}) collective-permute-start(bf16[256,2048]{1,0:T(8,128)(2,1)S(1)} %get-tuple-element.29), channel_id=1, source_target_pairs={{0,8},{1,9},{2,10},{3,11},{4,12},{5,13},{6,14},{7,15},{8,0},{9,1},... | collective-permute-start | bytes 3145736 | tf_op jit(solution)/shard_map/ppermute | solution.py:39
  37.1 0.0 collective-permute-done.2
  37.1 1.6 %collective-permute-done.3 = bf16[128,512]{1,0:T(8,128)(2,1)S(1)} collective-permute-done((bf16[128,512]{1,0:T(8,128)(2,1)S(1)}, bf16[128,512]{1,0:T(8,128)(2,1)S(1)}, u32[]{:S(2)}, u32[]{:S(2)}) %collective-permute-start.3) | collective-permute-done | bytes 131104 | tf_op jit(solution)/shard_map/ppermute | solution.py:39
  38.7 0.1 add_convert_fusion.1.key_own
  38.8 6.1 %collective-permute-start.4 = (bf16[256,512]{1,0:T(8,128)(2,1)S(1)}, bf16[256,512]{1,0:T(8,128)(2,1)S(1)}, u32[]{:S(2)}, u32[]{:S(2)}) collective-permute-start(bf16[256,512]{1,0:T(8,128)(2,1)S(1)} %add_convert_fusion.1.key_own), channel_id=1, source_target_pairs={{0,8},{1,9},{2,10},{3,11},{4,12},{5,13},{6,14},{7,15},{8,16},{9,17... | collective-permute-start | bytes 786440 | tf_op jit(solution)/shard_map/ppermute | solution.py:39
  44.9 0.1 collective-permute-start.7
  45.0 0.5 collective-permute-start.6
  45.5 2.7 %collective-permute-done.4.key_halo = bf16[256,512]{1,0:T(8,128)(2,1)S(1)} collective-permute-done((bf16[256,512]{1,0:T(8,128)(2,1)S(1)}, bf16[256,512]{1,0:T(8,128)(2,1)S(1)}, u32[]{:S(2)}, u32[]{:S(2)}) %collective-permute-start.4) | collective-permute-done | bytes 262176 | tf_op jit(solution)/shard_map/ppermute | solution.py:39
  48.1 0.0 copy-done.4
  48.1 0.0 copy-done.5
  48.1 0.0 copy-done.6
  48.2 9.7 %attend.1 = (f32[32,256]{1,0:T(8,128)}, bf16[256,4096]{1,0:T(8,128)(2,1)}, f32[256,512]{1,0:T(8,128)S(1)}, bf16[256,512]{1,0:T(8,128)(2,1)S(1)}) custom-call(s32[3]{0:T(128)S(1)} %pad_add_fusion.place, s32[1,32]{1,0:T(1,128)S(1)} %copy-done.6, bf16[256,4096]{1,0:T(8,128)(2,1)S(1)} %bitcast.27, bf16[256,512]{1,0:T(8,128)(2,1)S(1)} %add_convert_fusion.1.key_own, ...), custom_call_target="tpu_custom_call" | custom-call | flops 4294967296 | bytes 6291456 | tf_op jit(solution)/shard_map/attend/pallas_call | solution.py:211
  57.9 0.0 collective-permute-done.7.refs_3_
  57.9 0.0 collective-permute-done.6.refs_2_
  57.9 0.0 collective-permute-done.5.refs_1_
  57.9 1.9 %collective-permute-start.8 = (bf16[256,512]{1,0:T(8,128)(2,1)S(1)}, bf16[256,512]{1,0:T(8,128)(2,1)S(1)}, u32[]{:S(2)}, u32[]{:S(2)}) collective-permute-start(bf16[256,512]{1,0:T(8,128)(2,1)S(1)} %get-tuple-element.33), channel_id=1, source_target_pairs={{8,0},{9,1},{10,2},{11,3},{12,4},{13,5},{14,6},{15,7},{16,8},{17,9... | collective-permute-start | bytes 786440 | tf_op jit(solution)/shard_map/ppermute | solution.py:39
  59.8 6.5 %collective-permute-done.8 = bf16[256,512]{1,0:T(8,128)(2,1)S(1)} collective-permute-done((bf16[256,512]{1,0:T(8,128)(2,1)S(1)}, bf16[256,512]{1,0:T(8,128)(2,1)S(1)}, u32[]{:S(2)}, u32[]{:S(2)}) %collective-permute-start.8) | collective-permute-done | bytes 262176 | tf_op jit(solution)/shard_map/ppermute | solution.py:39
  66.3 0.1 add_convert_fusion.refs_2_
  66.4 0.1 collective-permute-start.11
  66.5 2.0 %collective-permute-start.10 = (bf16[128,512]{1,0:T(8,128)(2,1)S(1)}, bf16[128,512]{1,0:T(8,128)(2,1)S(1)}, u32[]{:S(2)}, u32[]{:S(2)}) collective-permute-start(bf16[128,512]{1,0:T(8,128)(2,1)S(1)} %get-tuple-element.45), channel_id=1, source_target_pairs={{0,68},{1,69},{2,70},{3,71},{4,0},{5,1},{6,2},{7,3},{8,76},{9,77},... | collective-permute-start | bytes 393224 | tf_op jit(solution)/shard_map/ppermute | solution.py:39
  68.6 0.0 collective-permute-start.9
  68.6 0.0 collective-permute-done.11.refs_3_
  68.6 2.1 %weight_grad.2.refs_8_ = f32[2048,512]{1,0:T(8,128)S(1)} custom-call(s32[3]{0:T(128)S(1)} %pad_add_fusion.place, bf16[256,2048]{1,0:T(8,128)(2,1)S(1)} %get-tuple-element.34.refs_0_, bf16[256,2048]{1,0:T(8,128)(2,1)S(1)} %collective-permute-done.5.refs_1_, bf16[256,512]{1,0:T(8,128)(2,1)S(1)} %add_convert_fusion.refs_2_, ...), custom_call_target="tpu_custom_call" | custom-call | flops 1073741824 | bytes 8388608 | tf_op jit(solution)/shard_map/weight_grad/pallas_call | solution.py:269
  70.7 0.8 collective-permute-done.10.refs_5_
  71.5 3.1 %collective-permute-done.9.refs_4_ = bf16[128,512]{1,0:T(8,128)(2,1)S(1)} collective-permute-done((bf16[128,512]{1,0:T(8,128)(2,1)S(1)}, bf16[128,512]{1,0:T(8,128)(2,1)S(1)}, u32[]{:S(2)}, u32[]{:S(2)}) %collective-permute-start.9) | collective-permute-done | bytes 131104 | tf_op jit(solution)/shard_map/ppermute | solution.py:39
  74.6 1.1 collective-permute-start.12
  75.7 0.0 collective-permute-start.13
  75.7 1.0 collective-permute-done.12.refs_6_
  76.7 0.4 collective-permute-done.13.refs_7_
  77.0 2.1 %weight_grad.3 = bf16[2048,512]{1,0:T(8,128)(2,1)S(1)} custom-call(s32[3]{0:T(128)S(1)} %pad_add_fusion.place, bf16[128,4096]{1,0:T(8,128)(2,1)S(1)} %collective-permute-done.low.refs_0_, bf16[128,4096]{1,0:T(8,128)(2,1)S(1)} %collective-permute-done.1.high.refs_1_, bf16[128,2048]{1,0:T(8,128)(2,1)S(1)} %collective-permute-done.6.refs_2_, ...), custom_call_target="tpu_custom_call" | custom-call | flops 1073741824 | bytes 8388608 | tf_op jit(solution)/shard_map/weight_grad/pallas_call | solution.py:269
  79.1 36.3 %all_to_all.10.parts = bf16[32,64,512]{2,1,0:T(8,128)(2,1)S(1)} all-to-all(bf16[32,64,512]{2,1,0:T(8,128)(2,1)S(1)} %bitcast.26), channel_id=1, replica_groups=mesh['xh'=2,'y'=4,'core'=2,'xl'=2,'z'=4] {'xh','y','z'}, dimensions={0} | all-to-all | bytes 4194304 | tf_op jit(solution)/shard_map/all_to_all | solution.py:394
  115.4 0.8 sum_spread.1
  116.2 32.6 %all_to_all.11 = bf16[32,64,512]{2,1,0:T(8,128)(2,1)S(1)} all-to-all(bf16[32,64,512]{2,1,0:T(8,128)(2,1)S(1)} %sum_spread.1), channel_id=1, replica_groups=mesh['xh'=2,'y'=4,'core'=2,'xl'=2,'z'=4] {'xh','y','z'}, dimensions={0} | all-to-all | bytes 4194304 | tf_op jit(solution)/shard_map/all_to_all | solution.py:396
  148.8 0.2 fusion
  149.0 3.1 %collective-permute-start.15 = (bf16[1024,512]{1,0:T(8,128)(2,1)S(1)}, bf16[1024,512]{1,0:T(8,128)(2,1)S(1)}, u32[]{:S(2)}, u32[]{:S(2)}) collective-permute-start(bf16[1024,512]{1,0:T(8,128)(2,1)S(1)} %bitcast.30), channel_id=1, source_target_pairs={{0,8},{1,9},{2,10},{3,11},{4,12},{5,13},{6,14},{7,15},{8,0},{9,1},... | collective-permute-start | bytes 3145736 | tf_op jit(solution)/shard_map/ppermute | solution.py:39
  152.1 0.1 collective-permute-start.14
  152.2 1.3 write_rows.3.refs_0_
  153.5 0.9 collective-permute-done.15.rows
  154.4 1.0 write_rows.4.refs_0_
  155.4 0.5 collective-permute-done.14.rows
  155.9 1.0 write_rows.5
  (3 shorter events, 0.1 us)
Async XLA Ops:
  3.3 25.5 %collective-permute-start.1 = (bf16[128,4096]{1,0:T(8,128)(2,1)}, bf16[128,4096]{1,0:T(8,128)(2,1)S(1)}, u32[]{:S(2)}, u32[]{:S(2)}) collective-permute-start(bf16[128,4096]{1,0:T(8,128)(2,1)} %get-tuple-element.41), channel_id=1, source_target_pairs={{0,68},{1,69},{2,70},{3,71},{4,0},{5,1},{6,2},{7,3},{8,76},{9,77},... | collective-permute-start | bytes 3145736 | tf_op jit(solution)/shard_map/ppermute | solution.py:39
  6.6 24.9 %collective-permute-start = (bf16[128,4096]{1,0:T(8,128)(2,1)S(1)}, bf16[128,4096]{1,0:T(8,128)(2,1)S(1)}, u32[]{:S(2)}, u32[]{:S(2)}) collective-permute-start(bf16[128,4096]{1,0:T(8,128)(2,1)S(1)} %get-tuple-element.42), channel_id=1, source_target_pairs={{0,4},{1,5},{2,6},{3,7},{4,64},{5,65},{6,66},{7,67},{8,12},{9,13},... | collective-permute-start | bytes 3145736 | tf_op jit(solution)/shard_map/ppermute | solution.py:39
  6.7 2.2 %copy-start = (bf16[1,256,8192]{2,1,0:T(8,128)(2,1)S(1)}, bf16[1,256,8192]{2,1,0:T(8,128)(2,1)}, u32[]{:S(2)}) copy-start(bf16[1,256,8192]{2,1,0:T(8,128)(2,1)} %param.6) | copy-start | bytes 12582916
  8.9 2.2 %copy-start.2 = (bf16[4096,512]{1,0:T(8,128)(2,1)S(1)}, bf16[4096,512]{1,0:T(8,128)(2,1)}, u32[]{:S(2)}) copy-start(bf16[4096,512]{1,0:T(8,128)(2,1)} %weight.3) | copy-start | bytes 12582916
  11.1 2.6 %copy-start.1 = (bf16[1,256,8192]{2,1,0:T(8,128)(2,1)S(1)}, bf16[1,256,8192]{2,1,0:T(8,128)(2,1)}, u32[]{:S(2)}) copy-start(bf16[1,256,8192]{2,1,0:T(8,128)(2,1)} %param.6) | copy-start | bytes 12582916
  13.7 17.9 %copy-start.3 = (bf16[4096,512]{1,0:T(8,128)(2,1)S(1)}, bf16[4096,512]{1,0:T(8,128)(2,1)}, u32[]{:S(2)}) copy-start(bf16[4096,512]{1,0:T(8,128)(2,1)} %weight.3) | copy-start | bytes 12582916
  31.6 16.6 %copy-start.4 = (bf16[1,256,4096]{2,1,0:T(8,128)(2,1)S(1)}, bf16[1,256,4096]{2,1,0:T(8,128)(2,1)}, u32[]{:S(2)}) copy-start(bf16[1,256,4096]{2,1,0:T(8,128)(2,1)} %param.5) | copy-start | bytes 6291460
  31.6 16.6 %copy-start.5 = (bf16[1,256,32]{1,2,0:T(8,128)(2,1)S(1)}, bf16[1,256,32]{1,2,0:T(8,128)(2,1)}, u32[]{:S(2)}) copy-start(bf16[1,256,32]{1,2,0:T(8,128)(2,1)} %param.9) | copy-start | bytes 49156
  31.6 16.6 %copy-start.6 = (s32[1,32]{1,0:T(1,128)S(1)}, s32[1,32]{1,0:T(1,128)}, u32[]{:S(2)}) copy-start(s32[1,32]{1,0:T(1,128)} %lengths.1) | copy-start | bytes 388
  33.1 4.0 %collective-permute-start.2 = (bf16[128,512]{1,0:T(8,128)(2,1)S(1)}, bf16[128,512]{1,0:T(8,128)(2,1)S(1)}, u32[]{:S(2)}, u32[]{:S(2)}) collective-permute-start(bf16[128,512]{1,0:T(8,128)(2,1)S(1)} %get-tuple-element.24), channel_id=1, source_target_pairs={{0,68},{1,69},{2,70},{3,71},{4,0},{5,1},{6,2},{7,3},{8,76},{9,77},... | collective-permute-start | bytes 393224 | tf_op jit(solution)/shard_map/ppermute | solution.py:39
  33.7 5.0 %collective-permute-start.3 = (bf16[128,512]{1,0:T(8,128)(2,1)S(1)}, bf16[128,512]{1,0:T(8,128)(2,1)S(1)}, u32[]{:S(2)}, u32[]{:S(2)}) collective-permute-start(bf16[128,512]{1,0:T(8,128)(2,1)S(1)} %get-tuple-element.25), channel_id=1, source_target_pairs={{0,4},{1,5},{2,6},{3,7},{4,64},{5,65},{6,66},{7,67},{8,12},{9,13},... | collective-permute-start | bytes 393224 | tf_op jit(solution)/shard_map/ppermute | solution.py:39
  34.6 23.3 %collective-permute-start.5 = (bf16[256,2048]{1,0:T(8,128)(2,1)S(1)}, bf16[256,2048]{1,0:T(8,128)(2,1)S(1)}, u32[]{:S(2)}, u32[]{:S(2)}) collective-permute-start(bf16[256,2048]{1,0:T(8,128)(2,1)S(1)} %get-tuple-element.29), channel_id=1, source_target_pairs={{0,8},{1,9},{2,10},{3,11},{4,12},{5,13},{6,14},{7,15},{8,0},{9,1},... | collective-permute-start | bytes 3145736 | tf_op jit(solution)/shard_map/ppermute | solution.py:39
  38.8 9.4 %collective-permute-start.4 = (bf16[256,512]{1,0:T(8,128)(2,1)S(1)}, bf16[256,512]{1,0:T(8,128)(2,1)S(1)}, u32[]{:S(2)}, u32[]{:S(2)}) collective-permute-start(bf16[256,512]{1,0:T(8,128)(2,1)S(1)} %add_convert_fusion.1.key_own), channel_id=1, source_target_pairs={{0,8},{1,9},{2,10},{3,11},{4,12},{5,13},{6,14},{7,15},{8,16},{9,17... | collective-permute-start | bytes 786440 | tf_op jit(solution)/shard_map/ppermute | solution.py:39
  44.9 13.0 %collective-permute-start.7 = (bf16[128,2048]{1,0:T(8,128)(2,1)S(1)}, bf16[128,2048]{1,0:T(8,128)(2,1)S(1)}, u32[]{:S(2)}, u32[]{:S(2)}) collective-permute-start(bf16[128,2048]{1,0:T(8,128)(2,1)S(1)} %constant_dynamic-slice_fusion), channel_id=1, source_target_pairs={{0,8},{1,9},{2,10},{3,11},{4,12},{5,13},{6,14},{7,15},{8,0},{9,1},... | collective-permute-start | bytes 1572872 | tf_op jit(solution)/shard_map/ppermute | solution.py:39
  45.0 12.9 %collective-permute-start.6 = (bf16[128,2048]{1,0:T(8,128)(2,1)S(1)}, bf16[128,2048]{1,0:T(8,128)(2,1)S(1)}, u32[]{:S(2)}, u32[]{:S(2)}) collective-permute-start(bf16[128,2048]{1,0:T(8,128)(2,1)S(1)} %constant_dynamic-slice_fusion.1), channel_id=1, source_target_pairs={{0,8},{1,9},{2,10},{3,11},{4,12},{5,13},{6,14},{7,15},{8,0},{9,1},... | collective-permute-start | bytes 1572872 | tf_op jit(solution)/shard_map/ppermute | solution.py:39
  57.9 8.4 %collective-permute-start.8 = (bf16[256,512]{1,0:T(8,128)(2,1)S(1)}, bf16[256,512]{1,0:T(8,128)(2,1)S(1)}, u32[]{:S(2)}, u32[]{:S(2)}) collective-permute-start(bf16[256,512]{1,0:T(8,128)(2,1)S(1)} %get-tuple-element.33), channel_id=1, source_target_pairs={{8,0},{9,1},{10,2},{11,3},{12,4},{13,5},{14,6},{15,7},{16,8},{17,9... | collective-permute-start | bytes 786440 | tf_op jit(solution)/shard_map/ppermute | solution.py:39
  66.4 2.2 %collective-permute-start.11 = (bf16[256,512]{1,0:T(8,128)(2,1)S(1)}, bf16[256,512]{1,0:T(8,128)(2,1)S(1)}, u32[]{:S(2)}, u32[]{:S(2)}) collective-permute-start(bf16[256,512]{1,0:T(8,128)(2,1)S(1)} %add_convert_fusion.refs_2_), channel_id=1, source_target_pairs={{0,8},{1,9},{2,10},{3,11},{4,12},{5,13},{6,14},{7,15},{8,0},{9,1},... | collective-permute-start | bytes 786440 | tf_op jit(solution)/shard_map/ppermute | solution.py:39
  66.5 5.0 %collective-permute-start.10 = (bf16[128,512]{1,0:T(8,128)(2,1)S(1)}, bf16[128,512]{1,0:T(8,128)(2,1)S(1)}, u32[]{:S(2)}, u32[]{:S(2)}) collective-permute-start(bf16[128,512]{1,0:T(8,128)(2,1)S(1)} %get-tuple-element.45), channel_id=1, source_target_pairs={{0,68},{1,69},{2,70},{3,71},{4,0},{5,1},{6,2},{7,3},{8,76},{9,77},... | collective-permute-start | bytes 393224 | tf_op jit(solution)/shard_map/ppermute | solution.py:39
  68.6 6.0 %collective-permute-start.9 = (bf16[128,512]{1,0:T(8,128)(2,1)S(1)}, bf16[128,512]{1,0:T(8,128)(2,1)S(1)}, u32[]{:S(2)}, u32[]{:S(2)}) collective-permute-start(bf16[128,512]{1,0:T(8,128)(2,1)S(1)} %get-tuple-element.46), channel_id=1, source_target_pairs={{0,4},{1,5},{2,6},{3,7},{4,64},{5,65},{6,66},{7,67},{8,12},{9,13},... | collective-permute-start | bytes 393224 | tf_op jit(solution)/shard_map/ppermute | solution.py:39
  74.6 2.1 %collective-permute-start.12 = (bf16[128,512]{1,0:T(8,128)(2,1)S(1)}, bf16[128,512]{1,0:T(8,128)(2,1)S(1)}, u32[]{:S(2)}, u32[]{:S(2)}) collective-permute-start(bf16[128,512]{1,0:T(8,128)(2,1)S(1)} %collective-permute-done.9.refs_4_), channel_id=1, source_target_pairs={{0,8},{1,9},{2,10},{3,11},{4,12},{5,13},{6,14},{7,15},{8,0},{9,1},... | collective-permute-start | bytes 393224 | tf_op jit(solution)/shard_map/ppermute | solution.py:39
  75.7 1.3 collective-permute-start.13
  149.0 5.4 %collective-permute-start.15 = (bf16[1024,512]{1,0:T(8,128)(2,1)S(1)}, bf16[1024,512]{1,0:T(8,128)(2,1)S(1)}, u32[]{:S(2)}, u32[]{:S(2)}) collective-permute-start(bf16[1024,512]{1,0:T(8,128)(2,1)S(1)} %bitcast.30), channel_id=1, source_target_pairs={{0,8},{1,9},{2,10},{3,11},{4,12},{5,13},{6,14},{7,15},{8,0},{9,1},... | collective-permute-start | bytes 3145736 | tf_op jit(solution)/shard_map/ppermute | solution.py:39
  152.1 3.8 %collective-permute-start.14 = (bf16[1024,512]{1,0:T(8,128)(2,1)S(1)}, bf16[1024,512]{1,0:T(8,128)(2,1)S(1)}, u32[]{:S(2)}, u32[]{:S(2)}) collective-permute-start(bf16[1024,512]{1,0:T(8,128)(2,1)S(1)} %bitcast.29), channel_id=1, source_target_pairs={{0,8},{1,9},{2,10},{3,11},{4,12},{5,13},{6,14},{7,15},{8,0},{9,1},... | collective-permute-start | bytes 3145736 | tf_op jit(solution)/shard_map/ppermute | solution.py:39

commit v9 on v8

--- a/solution.py
+++ b/solution.py
@@ -289,10 +289,10 @@
 
 def sum_spread(parts, scale):
     count, rows, width = parts.shape
-    block = pl.BlockSpec((count, rows // 4, width), lambda i: (0, i, 0))
+    block = pl.BlockSpec((count, rows // 2, width), lambda i: (0, i, 0))
     return pl.pallas_call(
         functools.partial(sum_spread_kernel, scale),
-        grid=(4,),
+        grid=(2,),
         in_specs=[block],
         out_specs=block,
         out_shape=jax.ShapeDtypeStruct(parts.shape, BF),

time: 157 us -> 157 us (level)
  no operation moved by 1% of the time
where the time goes in v9:
time: 157 us
  blocking collectives  68.9 us (44%)
  waiting for transfers between devices  35 us (22%)
  starting transfers between devices  22.3 us (14%)
  Pallas kernels  21.9 us (14%)
  local copies, waits for them, and re-layouts  7.65 us (5%)
    all_to_all x1, blocking collectives, shards(): lax.all_to_all(parts.reshape(32, 64, width), chips, split_axis=0, concat_...  36.3 us
    ppermute x16, waiting for transfers between devices, move(): return lax.ppermute(value, AXES, pairs)  35 us
    all_to_all x1, blocking collectives, shards(): lax.all_to_all(spread, chips, split_axis=0, concat_axis=0, tiled=True)  32.6 us
    ppermute x16, starting transfers between devices, move(): return lax.ppermute(value, AXES, pairs)  22.3 us
    pallas_call x1, Pallas kernels, attend(): pl.pallas_call(attend_kernel, grid_spec=pltpu.PrefetchScalarGridSpec(num_...  9.74 us
    unnamed x14, local copies, waits for them, and re-layouts  4.4 us
    pallas_call x2, Pallas kernels, weight_grad(): pl.pallas_call(functools.partial(weight_grad_kernel, len(hidden), far, le...  4.14 us
    pallas_call x3, Pallas kernels, write_rows(): pl.pallas_call(functools.partial(copy_kernel, side, first), in_specs=[any...  3.28 us
  transfers between devices with their start and end apart: 16, of which 11 were waited for; matrix products, arithmetic and copies ran while one was open for 0% of the time, Pallas kernels for 11%

profile of v9, /device:TPU:1, one launch (start us, length us, event | category | flops | bytes accessed | tf_op | source)
XLA Modules:
  0.0 156.8 jit_solution(11612629979623028486)
XLA Ops:
  0.6 2.7 %dynamic-slice_bitcast_fusion.2 = (bf16[128,4096]{1,0:T(8,128)(2,1)}, bf16[128,4096]{1,0:T(8,128)(2,1)S(1)}) fusion(bf16[1,256,8192]{2,1,0:T(8,128)(2,1)} %param.6, s32[]{:T(128)S(6)} %select_n.14), kind=kLoop, calls=%fused_computation.2 | loop fusion | bytes 4194308 | tf_op jit(solution)/shard_map/dynamic_slice | solution.py:359
  3.3 3.3 %collective-permute-start.1 = (bf16[128,4096]{1,0:T(8,128)(2,1)}, bf16[128,4096]{1,0:T(8,128)(2,1)S(1)}, u32[]{:S(2)}, u32[]{:S(2)}) collective-permute-start(bf16[128,4096]{1,0:T(8,128)(2,1)} %get-tuple-element.41), channel_id=1, source_target_pairs={{0,68},{1,69},{2,70},{3,71},{4,0},{5,1},{6,2},{7,3},{8,76},{9,77},... | collective-permute-start | bytes 3145736 | tf_op jit(solution)/shard_map/ppermute | solution.py:39
  6.6 0.0 collective-permute-start
  6.6 0.1 pad_add_fusion.place
  6.7 0.0 copy-start
  6.7 2.2 %copy-done = bf16[1,256,8192]{2,1,0:T(8,128)(2,1)S(1)} copy-done((bf16[1,256,8192]{2,1,0:T(8,128)(2,1)S(1)}, bf16[1,256,8192]{2,1,0:T(8,128)(2,1)}, u32[]{:S(2)}) %copy-start) | copy-done | bytes 4194328
  8.9 0.0 copy-start.2
  8.9 2.2 %copy-done.2 = bf16[4096,512]{1,0:T(8,128)(2,1)S(1)} copy-done((bf16[4096,512]{1,0:T(8,128)(2,1)S(1)}, bf16[4096,512]{1,0:T(8,128)(2,1)}, u32[]{:S(2)}) %copy-start.2) | copy-done | bytes 4194328
  11.1 0.0 copy-start.1
  11.1 2.6 %project_own.1 = f32[256,512]{1,0:T(8,128)S(1)} custom-call(s32[3]{0:T(128)S(1)} %pad_add_fusion.place, bf16[256,8192]{1,0:T(8,128)(2,1)S(1)} %bitcast.25, bf16[4096,512]{1,0:T(8,128)(2,1)S(1)} %copy-done.2), custom_call_target="tpu_custom_call" | custom-call | flops 1073741824 | bytes 6291456 | tf_op jit(solution)/shard_map/project_own/pallas_call | solution.py:67
  13.7 0.0 copy-done.1
  13.7 0.0 copy-start.3
  13.7 0.2 dynamic-slice_bitcast_fusion
  13.9 14.8 %collective-permute-done.1.high.refs_1_ = bf16[128,4096]{1,0:T(8,128)(2,1)S(1)} collective-permute-done((bf16[128,4096]{1,0:T(8,128)(2,1)}, bf16[128,4096]{1,0:T(8,128)(2,1)S(1)}, u32[]{:S(2)}, u32[]{:S(2)}) %collective-permute-start.1) | collective-permute-done | bytes 1048608 | tf_op jit(solution)/shard_map/ppermute | solution.py:39
  28.8 2.8 %collective-permute-done.low.refs_0_ = bf16[128,4096]{1,0:T(8,128)(2,1)S(1)} collective-permute-done((bf16[128,4096]{1,0:T(8,128)(2,1)S(1)}, bf16[128,4096]{1,0:T(8,128)(2,1)S(1)}, u32[]{:S(2)}, u32[]{:S(2)}) %collective-permute-start) | collective-permute-done | bytes 1048608 | tf_op jit(solution)/shard_map/ppermute | solution.py:39
  31.6 0.0 copy-done.3
  31.6 0.0 copy-start.4
  31.6 0.0 copy-start.5
  31.6 0.0 copy-start.6
  31.6 1.5 project_near.1
  33.1 0.6 collective-permute-start.2
  33.7 0.9 collective-permute-start.3
  34.6 2.4 %collective-permute-start.5 = (bf16[256,2048]{1,0:T(8,128)(2,1)S(1)}, bf16[256,2048]{1,0:T(8,128)(2,1)S(1)}, u32[]{:S(2)}, u32[]{:S(2)}) collective-permute-start(bf16[256,2048]{1,0:T(8,128)(2,1)S(1)} %get-tuple-element.29), channel_id=1, source_target_pairs={{0,8},{1,9},{2,10},{3,11},{4,12},{5,13},{6,14},{7,15},{8,0},{9,1},... | collective-permute-start | bytes 3145736 | tf_op jit(solution)/shard_map/ppermute | solution.py:39
  37.1 0.0 collective-permute-done.2
  37.1 1.6 %collective-permute-done.3 = bf16[128,512]{1,0:T(8,128)(2,1)S(1)} collective-permute-done((bf16[128,512]{1,0:T(8,128)(2,1)S(1)}, bf16[128,512]{1,0:T(8,128)(2,1)S(1)}, u32[]{:S(2)}, u32[]{:S(2)}) %collective-permute-start.3) | collective-permute-done | bytes 131104 | tf_op jit(solution)/shard_map/ppermute | solution.py:39
  38.7 0.1 add_convert_fusion.1.key_own
  38.8 6.1 %collective-permute-start.4 = (bf16[256,512]{1,0:T(8,128)(2,1)S(1)}, bf16[256,512]{1,0:T(8,128)(2,1)S(1)}, u32[]{:S(2)}, u32[]{:S(2)}) collective-permute-start(bf16[256,512]{1,0:T(8,128)(2,1)S(1)} %add_convert_fusion.1.key_own), channel_id=1, source_target_pairs={{0,8},{1,9},{2,10},{3,11},{4,12},{5,13},{6,14},{7,15},{8,16},{9,17... | collective-permute-start | bytes 786440 | tf_op jit(solution)/shard_map/ppermute | solution.py:39
  44.9 0.1 collective-permute-start.7
  45.0 0.5 collective-permute-start.6
  45.5 2.7 %collective-permute-done.4.key_halo = bf16[256,512]{1,0:T(8,128)(2,1)S(1)} collective-permute-done((bf16[256,512]{1,0:T(8,128)(2,1)S(1)}, bf16[256,512]{1,0:T(8,128)(2,1)S(1)}, u32[]{:S(2)}, u32[]{:S(2)}) %collective-permute-start.4) | collective-permute-done | bytes 262176 | tf_op jit(solution)/shard_map/ppermute | solution.py:39
  48.1 0.0 copy-done.4
  48.1 0.0 copy-done.5
  48.1 0.0 copy-done.6
  48.2 9.7 %attend.1 = (f32[32,256]{1,0:T(8,128)}, bf16[256,4096]{1,0:T(8,128)(2,1)}, f32[256,512]{1,0:T(8,128)S(1)}, bf16[256,512]{1,0:T(8,128)(2,1)S(1)}) custom-call(s32[3]{0:T(128)S(1)} %pad_add_fusion.place, s32[1,32]{1,0:T(1,128)S(1)} %copy-done.6, bf16[256,4096]{1,0:T(8,128)(2,1)S(1)} %bitcast.27, bf16[256,512]{1,0:T(8,128)(2,1)S(1)} %add_convert_fusion.1.key_own, ...), custom_call_target="tpu_custom_call" | custom-call | flops 4294967296 | bytes 6291456 | tf_op jit(solution)/shard_map/attend/pallas_call | solution.py:211
  57.9 0.0 collective-permute-done.7.refs_3_
  57.9 0.0 collective-permute-done.6.refs_2_
  57.9 0.0 collective-permute-done.5.refs_1_
  57.9 1.9 %collective-permute-start.8 = (bf16[256,512]{1,0:T(8,128)(2,1)S(1)}, bf16[256,512]{1,0:T(8,128)(2,1)S(1)}, u32[]{:S(2)}, u32[]{:S(2)}) collective-permute-start(bf16[256,512]{1,0:T(8,128)(2,1)S(1)} %get-tuple-element.33), channel_id=1, source_target_pairs={{8,0},{9,1},{10,2},{11,3},{12,4},{13,5},{14,6},{15,7},{16,8},{17,9... | collective-permute-start | bytes 786440 | tf_op jit(solution)/shard_map/ppermute | solution.py:39
  59.8 6.5 %collective-permute-done.8 = bf16[256,512]{1,0:T(8,128)(2,1)S(1)} collective-permute-done((bf16[256,512]{1,0:T(8,128)(2,1)S(1)}, bf16[256,512]{1,0:T(8,128)(2,1)S(1)}, u32[]{:S(2)}, u32[]{:S(2)}) %collective-permute-start.8) | collective-permute-done | bytes 262176 | tf_op jit(solution)/shard_map/ppermute | solution.py:39
  66.3 0.1 add_convert_fusion.refs_2_
  66.4 0.1 collective-permute-start.11
  66.5 2.0 %collective-permute-start.10 = (bf16[128,512]{1,0:T(8,128)(2,1)S(1)}, bf16[128,512]{1,0:T(8,128)(2,1)S(1)}, u32[]{:S(2)}, u32[]{:S(2)}) collective-permute-start(bf16[128,512]{1,0:T(8,128)(2,1)S(1)} %get-tuple-element.45), channel_id=1, source_target_pairs={{0,68},{1,69},{2,70},{3,71},{4,0},{5,1},{6,2},{7,3},{8,76},{9,77},... | collective-permute-start | bytes 393224 | tf_op jit(solution)/shard_map/ppermute | solution.py:39
  68.6 0.0 collective-permute-start.9
  68.6 0.0 collective-permute-done.11.refs_3_
  68.6 2.1 %weight_grad.2.refs_8_ = f32[2048,512]{1,0:T(8,128)S(1)} custom-call(s32[3]{0:T(128)S(1)} %pad_add_fusion.place, bf16[256,2048]{1,0:T(8,128)(2,1)S(1)} %get-tuple-element.34.refs_0_, bf16[256,2048]{1,0:T(8,128)(2,1)S(1)} %collective-permute-done.5.refs_1_, bf16[256,512]{1,0:T(8,128)(2,1)S(1)} %add_convert_fusion.refs_2_, ...), custom_call_target="tpu_custom_call" | custom-call | flops 1073741824 | bytes 8388608 | tf_op jit(solution)/shard_map/weight_grad/pallas_call | solution.py:269
  70.7 0.8 collective-permute-done.10.refs_5_
  71.5 3.1 %collective-permute-done.9.refs_4_ = bf16[128,512]{1,0:T(8,128)(2,1)S(1)} collective-permute-done((bf16[128,512]{1,0:T(8,128)(2,1)S(1)}, bf16[128,512]{1,0:T(8,128)(2,1)S(1)}, u32[]{:S(2)}, u32[]{:S(2)}) %collective-permute-start.9) | collective-permute-done | bytes 131104 | tf_op jit(solution)/shard_map/ppermute | solution.py:39
  74.6 1.1 collective-permute-start.12
  75.7 0.0 collective-permute-start.13
  75.7 1.0 collective-permute-done.12.refs_6_
  76.7 0.4 collective-permute-done.13.refs_7_
  77.0 2.1 %weight_grad.3 = bf16[2048,512]{1,0:T(8,128)(2,1)S(1)} custom-call(s32[3]{0:T(128)S(1)} %pad_add_fusion.place, bf16[128,4096]{1,0:T(8,128)(2,1)S(1)} %collective-permute-done.low.refs_0_, bf16[128,4096]{1,0:T(8,128)(2,1)S(1)} %collective-permute-done.1.high.refs_1_, bf16[128,2048]{1,0:T(8,128)(2,1)S(1)} %collective-permute-done.6.refs_2_, ...), custom_call_target="tpu_custom_call" | custom-call | flops 1073741824 | bytes 8388608 | tf_op jit(solution)/shard_map/weight_grad/pallas_call | solution.py:269
  79.1 36.3 %all_to_all.10.parts = bf16[32,64,512]{2,1,0:T(8,128)(2,1)S(1)} all-to-all(bf16[32,64,512]{2,1,0:T(8,128)(2,1)S(1)} %bitcast.26), channel_id=1, replica_groups=mesh['xh'=2,'y'=4,'core'=2,'xl'=2,'z'=4] {'xh','y','z'}, dimensions={0} | all-to-all | bytes 4194304 | tf_op jit(solution)/shard_map/all_to_all | solution.py:394
  115.4 0.7 sum_spread.1
  116.2 32.6 %all_to_all.11 = bf16[32,64,512]{2,1,0:T(8,128)(2,1)S(1)} all-to-all(bf16[32,64,512]{2,1,0:T(8,128)(2,1)S(1)} %sum_spread.1), channel_id=1, replica_groups=mesh['xh'=2,'y'=4,'core'=2,'xl'=2,'z'=4] {'xh','y','z'}, dimensions={0} | all-to-all | bytes 4194304 | tf_op jit(solution)/shard_map/all_to_all | solution.py:396
  148.8 0.2 fusion
  149.0 3.1 %collective-permute-start.15 = (bf16[1024,512]{1,0:T(8,128)(2,1)S(1)}, bf16[1024,512]{1,0:T(8,128)(2,1)S(1)}, u32[]{:S(2)}, u32[]{:S(2)}) collective-permute-start(bf16[1024,512]{1,0:T(8,128)(2,1)S(1)} %bitcast.30), channel_id=1, source_target_pairs={{0,8},{1,9},{2,10},{3,11},{4,12},{5,13},{6,14},{7,15},{8,0},{9,1},... | collective-permute-start | bytes 3145736 | tf_op jit(solution)/shard_map/ppermute | solution.py:39
  152.1 0.1 collective-permute-start.14
  152.1 1.3 write_rows.3.refs_0_
  153.5 0.9 collective-permute-done.15.rows
  154.3 1.0 write_rows.4.refs_0_
  155.3 0.5 collective-permute-done.14.rows
  155.8 1.0 write_rows.5
  (3 shorter events, 0.1 us)
Async XLA Ops:
  3.3 25.5 %collective-permute-start.1 = (bf16[128,4096]{1,0:T(8,128)(2,1)}, bf16[128,4096]{1,0:T(8,128)(2,1)S(1)}, u32[]{:S(2)}, u32[]{:S(2)}) collective-permute-start(bf16[128,4096]{1,0:T(8,128)(2,1)} %get-tuple-element.41), channel_id=1, source_target_pairs={{0,68},{1,69},{2,70},{3,71},{4,0},{5,1},{6,2},{7,3},{8,76},{9,77},... | collective-permute-start | bytes 3145736 | tf_op jit(solution)/shard_map/ppermute | solution.py:39
  6.6 24.9 %collective-permute-start = (bf16[128,4096]{1,0:T(8,128)(2,1)S(1)}, bf16[128,4096]{1,0:T(8,128)(2,1)S(1)}, u32[]{:S(2)}, u32[]{:S(2)}) collective-permute-start(bf16[128,4096]{1,0:T(8,128)(2,1)S(1)} %get-tuple-element.42), channel_id=1, source_target_pairs={{0,4},{1,5},{2,6},{3,7},{4,64},{5,65},{6,66},{7,67},{8,12},{9,13},... | collective-permute-start | bytes 3145736 | tf_op jit(solution)/shard_map/ppermute | solution.py:39
  6.7 2.2 %copy-start = (bf16[1,256,8192]{2,1,0:T(8,128)(2,1)S(1)}, bf16[1,256,8192]{2,1,0:T(8,128)(2,1)}, u32[]{:S(2)}) copy-start(bf16[1,256,8192]{2,1,0:T(8,128)(2,1)} %param.6) | copy-start | bytes 12582916
  8.9 2.2 %copy-start.2 = (bf16[4096,512]{1,0:T(8,128)(2,1)S(1)}, bf16[4096,512]{1,0:T(8,128)(2,1)}, u32[]{:S(2)}) copy-start(bf16[4096,512]{1,0:T(8,128)(2,1)} %weight.3) | copy-start | bytes 12582916
  11.1 2.6 %copy-start.1 = (bf16[1,256,8192]{2,1,0:T(8,128)(2,1)S(1)}, bf16[1,256,8192]{2,1,0:T(8,128)(2,1)}, u32[]{:S(2)}) copy-start(bf16[1,256,8192]{2,1,0:T(8,128)(2,1)} %param.6) | copy-start | bytes 12582916
  13.7 17.9 %copy-start.3 = (bf16[4096,512]{1,0:T(8,128)(2,1)S(1)}, bf16[4096,512]{1,0:T(8,128)(2,1)}, u32[]{:S(2)}) copy-start(bf16[4096,512]{1,0:T(8,128)(2,1)} %weight.3) | copy-start | bytes 12582916
  31.6 16.6 %copy-start.4 = (bf16[1,256,4096]{2,1,0:T(8,128)(2,1)S(1)}, bf16[1,256,4096]{2,1,0:T(8,128)(2,1)}, u32[]{:S(2)}) copy-start(bf16[1,256,4096]{2,1,0:T(8,128)(2,1)} %param.5) | copy-start | bytes 6291460
  31.6 16.6 %copy-start.5 = (bf16[1,256,32]{1,2,0:T(8,128)(2,1)S(1)}, bf16[1,256,32]{1,2,0:T(8,128)(2,1)}, u32[]{:S(2)}) copy-start(bf16[1,256,32]{1,2,0:T(8,128)(2,1)} %param.9) | copy-start | bytes 49156
  31.6 16.6 %copy-start.6 = (s32[1,32]{1,0:T(1,128)S(1)}, s32[1,32]{1,0:T(1,128)}, u32[]{:S(2)}) copy-start(s32[1,32]{1,0:T(1,128)} %lengths.1) | copy-start | bytes 388
  33.1 4.0 %collective-permute-start.2 = (bf16[128,512]{1,0:T(8,128)(2,1)S(1)}, bf16[128,512]{1,0:T(8,128)(2,1)S(1)}, u32[]{:S(2)}, u32[]{:S(2)}) collective-permute-start(bf16[128,512]{1,0:T(8,128)(2,1)S(1)} %get-tuple-element.24), channel_id=1, source_target_pairs={{0,68},{1,69},{2,70},{3,71},{4,0},{5,1},{6,2},{7,3},{8,76},{9,77},... | collective-permute-start | bytes 393224 | tf_op jit(solution)/shard_map/ppermute | solution.py:39
  33.7 5.0 %collective-permute-start.3 = (bf16[128,512]{1,0:T(8,128)(2,1)S(1)}, bf16[128,512]{1,0:T(8,128)(2,1)S(1)}, u32[]{:S(2)}, u32[]{:S(2)}) collective-permute-start(bf16[128,512]{1,0:T(8,128)(2,1)S(1)} %get-tuple-element.25), channel_id=1, source_target_pairs={{0,4},{1,5},{2,6},{3,7},{4,64},{5,65},{6,66},{7,67},{8,12},{9,13},... | collective-permute-start | bytes 393224 | tf_op jit(solution)/shard_map/ppermute | solution.py:39
  34.6 23.3 %collective-permute-start.5 = (bf16[256,2048]{1,0:T(8,128)(2,1)S(1)}, bf16[256,2048]{1,0:T(8,128)(2,1)S(1)}, u32[]{:S(2)}, u32[]{:S(2)}) collective-permute-start(bf16[256,2048]{1,0:T(8,128)(2,1)S(1)} %get-tuple-element.29), channel_id=1, source_target_pairs={{0,8},{1,9},{2,10},{3,11},{4,12},{5,13},{6,14},{7,15},{8,0},{9,1},... | collective-permute-start | bytes 3145736 | tf_op jit(solution)/shard_map/ppermute | solution.py:39
  38.8 9.4 %collective-permute-start.4 = (bf16[256,512]{1,0:T(8,128)(2,1)S(1)}, bf16[256,512]{1,0:T(8,128)(2,1)S(1)}, u32[]{:S(2)}, u32[]{:S(2)}) collective-permute-start(bf16[256,512]{1,0:T(8,128)(2,1)S(1)} %add_convert_fusion.1.key_own), channel_id=1, source_target_pairs={{0,8},{1,9},{2,10},{3,11},{4,12},{5,13},{6,14},{7,15},{8,16},{9,17... | collective-permute-start | bytes 786440 | tf_op jit(solution)/shard_map/ppermute | solution.py:39
  44.9 13.0 %collective-permute-start.7 = (bf16[128,2048]{1,0:T(8,128)(2,1)S(1)}, bf16[128,2048]{1,0:T(8,128)(2,1)S(1)}, u32[]{:S(2)}, u32[]{:S(2)}) collective-permute-start(bf16[128,2048]{1,0:T(8,128)(2,1)S(1)} %constant_dynamic-slice_fusion), channel_id=1, source_target_pairs={{0,8},{1,9},{2,10},{3,11},{4,12},{5,13},{6,14},{7,15},{8,0},{9,1},... | collective-permute-start | bytes 1572872 | tf_op jit(solution)/shard_map/ppermute | solution.py:39
  45.0 12.9 %collective-permute-start.6 = (bf16[128,2048]{1,0:T(8,128)(2,1)S(1)}, bf16[128,2048]{1,0:T(8,128)(2,1)S(1)}, u32[]{:S(2)}, u32[]{:S(2)}) collective-permute-start(bf16[128,2048]{1,0:T(8,128)(2,1)S(1)} %constant_dynamic-slice_fusion.1), channel_id=1, source_target_pairs={{0,8},{1,9},{2,10},{3,11},{4,12},{5,13},{6,14},{7,15},{8,0},{9,1},... | collective-permute-start | bytes 1572872 | tf_op jit(solution)/shard_map/ppermute | solution.py:39
  57.9 8.4 %collective-permute-start.8 = (bf16[256,512]{1,0:T(8,128)(2,1)S(1)}, bf16[256,512]{1,0:T(8,128)(2,1)S(1)}, u32[]{:S(2)}, u32[]{:S(2)}) collective-permute-start(bf16[256,512]{1,0:T(8,128)(2,1)S(1)} %get-tuple-element.33), channel_id=1, source_target_pairs={{8,0},{9,1},{10,2},{11,3},{12,4},{13,5},{14,6},{15,7},{16,8},{17,9... | collective-permute-start | bytes 786440 | tf_op jit(solution)/shard_map/ppermute | solution.py:39
  66.4 2.2 %collective-permute-start.11 = (bf16[256,512]{1,0:T(8,128)(2,1)S(1)}, bf16[256,512]{1,0:T(8,128)(2,1)S(1)}, u32[]{:S(2)}, u32[]{:S(2)}) collective-permute-start(bf16[256,512]{1,0:T(8,128)(2,1)S(1)} %add_convert_fusion.refs_2_), channel_id=1, source_target_pairs={{0,8},{1,9},{2,10},{3,11},{4,12},{5,13},{6,14},{7,15},{8,0},{9,1},... | collective-permute-start | bytes 786440 | tf_op jit(solution)/shard_map/ppermute | solution.py:39
  66.5 5.0 %collective-permute-start.10 = (bf16[128,512]{1,0:T(8,128)(2,1)S(1)}, bf16[128,512]{1,0:T(8,128)(2,1)S(1)}, u32[]{:S(2)}, u32[]{:S(2)}) collective-permute-start(bf16[128,512]{1,0:T(8,128)(2,1)S(1)} %get-tuple-element.45), channel_id=1, source_target_pairs={{0,68},{1,69},{2,70},{3,71},{4,0},{5,1},{6,2},{7,3},{8,76},{9,77},... | collective-permute-start | bytes 393224 | tf_op jit(solution)/shard_map/ppermute | solution.py:39
  68.6 6.0 %collective-permute-start.9 = (bf16[128,512]{1,0:T(8,128)(2,1)S(1)}, bf16[128,512]{1,0:T(8,128)(2,1)S(1)}, u32[]{:S(2)}, u32[]{:S(2)}) collective-permute-start(bf16[128,512]{1,0:T(8,128)(2,1)S(1)} %get-tuple-element.46), channel_id=1, source_target_pairs={{0,4},{1,5},{2,6},{3,7},{4,64},{5,65},{6,66},{7,67},{8,12},{9,13},... | collective-permute-start | bytes 393224 | tf_op jit(solution)/shard_map/ppermute | solution.py:39
  74.6 2.1 %collective-permute-start.12 = (bf16[128,512]{1,0:T(8,128)(2,1)S(1)}, bf16[128,512]{1,0:T(8,128)(2,1)S(1)}, u32[]{:S(2)}, u32[]{:S(2)}) collective-permute-start(bf16[128,512]{1,0:T(8,128)(2,1)S(1)} %collective-permute-done.9.refs_4_), channel_id=1, source_target_pairs={{0,8},{1,9},{2,10},{3,11},{4,12},{5,13},{6,14},{7,15},{8,0},{9,1},... | collective-permute-start | bytes 393224 | tf_op jit(solution)/shard_map/ppermute | solution.py:39
  75.7 1.3 collective-permute-start.13
  149.0 5.4 %collective-permute-start.15 = (bf16[1024,512]{1,0:T(8,128)(2,1)S(1)}, bf16[1024,512]{1,0:T(8,128)(2,1)S(1)}, u32[]{:S(2)}, u32[]{:S(2)}) collective-permute-start(bf16[1024,512]{1,0:T(8,128)(2,1)S(1)} %bitcast.30), channel_id=1, source_target_pairs={{0,8},{1,9},{2,10},{3,11},{4,12},{5,13},{6,14},{7,15},{8,0},{9,1},... | collective-permute-start | bytes 3145736 | tf_op jit(solution)/shard_map/ppermute | solution.py:39
  152.1 3.8 %collective-permute-start.14 = (bf16[1024,512]{1,0:T(8,128)(2,1)S(1)}, bf16[1024,512]{1,0:T(8,128)(2,1)S(1)}, u32[]{:S(2)}, u32[]{:S(2)}) collective-permute-start(bf16[1024,512]{1,0:T(8,128)(2,1)S(1)} %bitcast.29), channel_id=1, source_target_pairs={{0,8},{1,9},{2,10},{3,11},{4,12},{5,13},{6,14},{7,15},{8,0},{9,1},... | collective-permute-start | bytes 3145736 | tf_op jit(solution)/shard_map/ppermute | solution.py:39
